TPU v7x, 32 devices: a whole 2x2x4 slice. The times are simulated.
32 devices in a mesh: rep: 8 (over y, x, core), shard: 4 (over z).
Axes of the slice: x: 2, y: 2, z: 4, core: 2. Of those that a mesh axis runs over, the one named last changes fastest.
Arguments:
- char_ids: int32 [128, 48], P(('rep', 'shard')), may hold values from 0 to 274
- prefix: int32 [128], P(('rep', 'shard')), may hold values from 4 to 24, as said below
- embedding: bfloat16 [2, 275, 100], replicated, may hold values from -6 to 6
- w_in: bfloat16 [2, 4, 100, 2048], P(None, None, None, 'shard'), may hold values from -0.625 to 0.625
- w_rec: bfloat16 [2, 4, 2048, 2048], P(None, None, None, 'shard'), may hold values from -0.125 to 0.125
- gate_bias: bfloat16 [2, 4, 2048], P(None, None, 'shard'), may hold values from -3 to 4
- w_out: bfloat16 [2, 2048, 275], P(None, 'shard'), may hold values from -0.875 to 0.875
- b_out: bfloat16 [2, 275], replicated, may hold values from -3 to 3
Outputs:
- grad_embed: float32 [2, 275, 100], replicated
- grad_in: float32 [2, 4, 100, 2048], P(None, None, None, 'shard')
- grad_rec: float32 [2, 4, 2048, 2048], P(None, None, 'rep', 'shard')
- grad_bias: float32 [2, 4, 2048], P(None, None, 'shard')
- grad_out: float32 [2, 2048, 275], P(None, 'shard')
- grad_bout: float32 [2, 275], replicated
Inputs may be any that keep to these rules, and one draw needn't show every extreme that they name: Some sequence has a prefix of exactly 24 characters.
All inputs are finite; a program needn't handle non-finite values.
Results may differ from a plain program's by a relative error of at most 0.0015.
Values may be sent and summed in bfloat16 or wider, within the bound.
A program may use at most 192 MiB of HBM per device.

v0:
```python
import math

import jax
import jax.numpy as jnp
from jax import lax
from jax.sharding import PartitionSpec as P

PRECISE = lax.Precision.HIGHEST


def one_hot(ids, width, out_type):
    return (ids[..., None] == jnp.arange(width, dtype=jnp.int32)).astype(out_type)


def loss_grad(logits, targets, active, factor):
    probabilities = jax.nn.softmax(logits, axis=-1)
    picked = one_hot(targets, logits.shape[-1], jnp.float32)
    return ((probabilities - picked) * (active * factor)[:, None]).astype(jnp.bfloat16)


def run_forward(projected, w_rec, start_pair, sender):

    def advance(state_pair, slot_proj):
        full_hidden, memory = state_pair
        gate_sum = slot_proj + jnp.einsum(
            "mbk,mgkn->mbgn", full_hidden, w_rec, preferred_element_type=jnp.float32
        )
        in_gate = jax.nn.sigmoid(gate_sum[..., 0, :])
        forget = jax.nn.sigmoid(gate_sum[..., 1, :])
        candidate = jnp.tanh(gate_sum[..., 2, :])
        out_gate = jax.nn.sigmoid(gate_sum[..., 3, :])
        new_memory = forget * memory + in_gate * candidate
        own_hidden = (out_gate * jnp.tanh(new_memory)).astype(jnp.bfloat16)
        new_full = sender(own_hidden)
        record = (
            jnp.stack([in_gate, forget, candidate, out_gate], axis=-2),
            new_memory,
            own_hidden,
            new_full,
        )
        return ((new_full, new_memory), record)

    return lax.scan(advance, start_pair, projected)


def run_backward(records, w_rec, start_pair, sender):

    def retreat(state_pair, record):
        from_later, cell_grad = state_pair
        gate_act, memory, prev_memory, from_decoder = record
        in_gate = gate_act[..., 0, :]
        forget = gate_act[..., 1, :]
        candidate = gate_act[..., 2, :]
        out_gate = gate_act[..., 3, :]
        grad_hidden = from_decoder + from_later
        squashed = jnp.tanh(memory)
        grad_memory = cell_grad + grad_hidden * out_gate * (1.0 - squashed * squashed)
        gate_grad = jnp.stack(
            [
                grad_memory * candidate * in_gate * (1.0 - in_gate),
                grad_memory * prev_memory * forget * (1.0 - forget),
                grad_memory * in_gate * (1.0 - candidate * candidate),
                grad_hidden * squashed * out_gate * (1.0 - out_gate),
            ],
            axis=-2,
        ).astype(jnp.bfloat16)
        partial_sum = jnp.einsum(
            "mbgn,mgkn->mbk", gate_grad, w_rec, preferred_element_type=jnp.float32
        )
        return ((sender(partial_sum), grad_memory * forget), gate_grad)

    return lax.scan(retreat, start_pair, records, reverse=True)


def shifted(values):
    return jnp.concatenate([jnp.zeros_like(values[:1]), values[:-1]], axis=0)


def shards(char_ids, prefix, embedding, w_in, w_rec, gate_bias, w_out, b_out):
    seq_dev, length = char_ids.shape
    half_len = length // 2
    vocab_size = embedding.shape[1]
    unit_count = w_rec.shape[2]
    shard_units = w_rec.shape[3]
    factor = 1.0 / math.sqrt(lax.axis_size("rep") * lax.axis_size("shard") * seq_dev * length)
    group_chars, group_prefix = (
        lax.all_gather(char_ids, "shard", axis=0, tiled=True),
        lax.all_gather(prefix, "shard", axis=0, tiled=True),
    )
    group_size = group_chars.shape[0]
    front_in = group_chars.T
    front_target = jnp.concatenate([group_chars[:, 1:], group_chars[:, :1]], axis=1).T
    timeline = jnp.arange(length, dtype=jnp.int32)[:, None]
    front_active = jnp.broadcast_to(
        (timeline < length - 1).astype(jnp.float32), (length, group_size)
    )
    reverse_steps = jnp.arange(half_len, dtype=jnp.int32)[:, None]
    back_in = jnp.take_along_axis(
        front_in, jnp.maximum(group_prefix[None, :] - 1 - reverse_steps, 0), axis=0
    )
    back_target = jnp.take_along_axis(
        front_in, jnp.maximum(group_prefix[None, :] - 2 - reverse_steps, 0), axis=0
    )
    back_active = (reverse_steps <= group_prefix[None, :] - 2).astype(jnp.float32)
    front_x = jnp.einsum(
        "tbv,ve->tbe",
        one_hot(front_in, vocab_size, jnp.bfloat16),
        embedding[0],
        preferred_element_type=jnp.float32,
    ).astype(jnp.bfloat16)
    back_x = jnp.einsum(
        "tbv,ve->tbe",
        one_hot(back_in, vocab_size, jnp.bfloat16),
        embedding[1],
        preferred_element_type=jnp.float32,
    ).astype(jnp.bfloat16)
    bias_wide = gate_bias.astype(jnp.float32)
    front_proj = (
        jnp.einsum("tbe,gen->tbgn", front_x, w_in[0], preferred_element_type=jnp.float32)
        + bias_wide[0]
    )
    back_proj = (
        jnp.einsum("tbe,gen->tbgn", back_x, w_in[1], preferred_element_type=jnp.float32)
        + bias_wide[1]
    )

    def move_both(own_hidden):
        return lax.all_gather(own_hidden, "shard", axis=2, tiled=True)

    def move_front(own_hidden):
        return lax.all_gather(own_hidden, "shard", axis=2, tiled=True)

    both_proj = jnp.stack([front_proj[:half_len], back_proj], axis=1)
    start_pair = (
        jnp.zeros((2, group_size, unit_count), jnp.bfloat16),
        jnp.zeros((2, group_size, shard_units), jnp.float32),
    )
    (mid_full, mid_memory), early_rec = run_forward(both_proj, w_rec, start_pair, move_both)
    front_weights = w_rec[:1]
    ignored, late_rec = run_forward(
        front_proj[half_len:, None], front_weights, (mid_full[:1], mid_memory[:1]), move_front
    )
    front_rec = tuple(
        (
            jnp.concatenate([head_part[:, :1], tail_part], axis=0)
            for head_part, tail_part in zip(early_rec, late_rec)
        )
    )
    back_rec = tuple((head_part[:, 1:] for head_part in early_rec))
    full_out = lax.all_gather(w_out, "shard", axis=1, tiled=True)
    first_seq = lax.axis_index("shard") * seq_dev
    front_rows = lax.dynamic_slice_in_dim(front_rec[3][:, 0], first_seq, seq_dev, axis=1).reshape(
        length * seq_dev, unit_count
    )
    back_rows = lax.dynamic_slice_in_dim(back_rec[3][:, 0], first_seq, seq_dev, axis=1).reshape(
        half_len * seq_dev, unit_count
    )
    own_front_target = lax.dynamic_slice_in_dim(front_target, first_seq, seq_dev, axis=1).reshape(
        -1
    )
    own_back_target = lax.dynamic_slice_in_dim(back_target, first_seq, seq_dev, axis=1).reshape(-1)
    own_front_active = lax.dynamic_slice_in_dim(front_active, first_seq, seq_dev, axis=1).reshape(
        -1
    )
    own_back_active = lax.dynamic_slice_in_dim(back_active, first_seq, seq_dev, axis=1).reshape(-1)
    front_logits = jnp.dot(front_rows, full_out[0], preferred_element_type=jnp.float32) + b_out[
        0
    ].astype(jnp.float32)
    back_logits = jnp.dot(back_rows, full_out[1], preferred_element_type=jnp.float32) + b_out[
        1
    ].astype(jnp.float32)
    front_grad = loss_grad(front_logits, own_front_target, own_front_active, factor)
    back_grad = loss_grad(back_logits, own_back_target, own_back_active, factor)
    front_part = jnp.einsum(
        "rv,kv->rk", front_grad, full_out[0], preferred_element_type=jnp.float32
    ).reshape(length, seq_dev, unit_count)
    back_part = jnp.einsum(
        "rv,kv->rk", back_grad, full_out[1], preferred_element_type=jnp.float32
    ).reshape(half_len, seq_dev, unit_count)
    front_dec, back_dec = (
        lax.all_to_all(front_part, "shard", split_axis=2, concat_axis=1, tiled=True),
        lax.all_to_all(back_part, "shard", split_axis=2, concat_axis=1, tiled=True),
    )
    front_dec = front_dec[:, None]
    back_dec = back_dec[:, None]
    out_whole = jnp.stack(
        [
            jnp.einsum("rk,rv->kv", front_rows, front_grad, preferred_element_type=jnp.float32),
            jnp.einsum("rk,rv->kv", back_rows, back_grad, preferred_element_type=jnp.float32),
        ]
    )
    out_grad = lax.psum_scatter(out_whole, "shard", scatter_dimension=1, tiled=True)
    bout_part = jnp.stack(
        [
            jnp.sum(front_grad, axis=0, dtype=jnp.float32),
            jnp.sum(back_grad, axis=0, dtype=jnp.float32),
        ]
    )

    def move_front_grad(partial_sum):
        return lax.psum_scatter(partial_sum, "shard", scatter_dimension=2, tiled=True)

    def move_both_grad(partial_sum):
        return lax.psum_scatter(partial_sum, "shard", scatter_dimension=2, tiled=True)

    front_prev_memory = shifted(front_rec[1])
    back_prev_memory = shifted(back_rec[1])
    blank_grad = jnp.zeros((1, group_size, shard_units), jnp.float32)
    late_records = (
        front_rec[0][half_len:],
        front_rec[1][half_len:],
        front_prev_memory[half_len:],
        front_dec[half_len:],
    )
    (carry_hidden, carry_memory), late_grads = run_backward(
        late_records, front_weights, (blank_grad, blank_grad), move_front_grad
    )
    prev_front = shifted(front_rec[3])[:, 0]
    prev_back = shifted(back_rec[3])[:, 0]
    early_records = (
        jnp.concatenate([front_rec[0][:half_len], back_rec[0]], axis=1),
        jnp.concatenate([front_rec[1][:half_len], back_rec[1]], axis=1),
        jnp.concatenate([front_prev_memory[:half_len], back_prev_memory], axis=1),
        jnp.concatenate([front_dec[:half_len], back_dec], axis=1),
    )
    start_back = (
        jnp.concatenate([carry_hidden, blank_grad], axis=0),
        jnp.concatenate([carry_memory, blank_grad], axis=0),
    )
    ignored, early_grads = run_backward(early_records, w_rec, start_back, move_both_grad)
    front_grads = jnp.concatenate([early_grads[:, :1], late_grads], axis=0)[:, 0]
    back_grads = early_grads[:, 1]
    front_rec_grad = jnp.einsum(
        "tbk,tbgn->gkn", prev_front, front_grads, preferred_element_type=jnp.float32
    )
    back_rec_grad = jnp.einsum(
        "tbk,tbgn->gkn", prev_back, back_grads, preferred_element_type=jnp.float32
    )
    rec_grad = lax.psum_scatter(
        jnp.stack([front_rec_grad, back_rec_grad]), "rep", scatter_dimension=2, tiled=True
    )
    in_grad = jnp.stack(
        [
            jnp.einsum("tbe,tbgn->gen", front_x, front_grads, preferred_element_type=jnp.float32),
            jnp.einsum("tbe,tbgn->gen", back_x, back_grads, preferred_element_type=jnp.float32),
        ]
    )
    bias_grad = jnp.stack(
        [
            jnp.sum(front_grads, axis=(0, 1), dtype=jnp.float32),
            jnp.sum(back_grads, axis=(0, 1), dtype=jnp.float32),
        ]
    )
    front_dx = jnp.einsum("tbgn,gen->tbe", front_grads, w_in[0], preferred_element_type=jnp.float32)
    back_dx = jnp.einsum("tbgn,gen->tbe", back_grads, w_in[1], preferred_element_type=jnp.float32)
    embed_grad = jnp.stack(
        [
            jnp.einsum(
                "tbv,tbe->ve",
                one_hot(front_in, vocab_size, jnp.float32),
                front_dx,
                precision=PRECISE,
            ),
            jnp.einsum(
                "tbv,tbe->ve", one_hot(back_in, vocab_size, jnp.float32), back_dx, precision=PRECISE
            ),
        ]
    )
    in_size = in_grad.size
    bias_size = bias_grad.size
    flat_grads = jnp.concatenate([in_grad.reshape(-1), bias_grad.reshape(-1), out_grad.reshape(-1)])
    summed_part = lax.psum_scatter(flat_grads, "rep", scatter_dimension=0, tiled=True)
    summed_flat = lax.all_gather(summed_part, "rep", axis=0, tiled=True)
    in_sum = summed_flat[:in_size].reshape(in_grad.shape)
    bias_sum = summed_flat[in_size : in_size + bias_size].reshape(bias_grad.shape)
    out_sum = summed_flat[in_size + bias_size :].reshape(out_grad.shape)
    embed_sum, bout_sum = lax.psum((embed_grad, bout_part), ("rep", "shard"))
    return (embed_sum, in_sum, rec_grad, bias_sum, out_sum, bout_sum)


def solution(mesh):
    in_specs = (
        P(("rep", "shard"), None),
        P(("rep", "shard")),
        P(),
        P(None, None, None, "shard"),
        P(None, None, None, "shard"),
        P(None, None, "shard"),
        P(None, "shard", None),
        P(),
    )
    out_specs = (
        P(),
        P(None, None, None, "shard"),
        P(None, None, "rep", "shard"),
        P(None, None, "shard"),
        P(None, "shard", None),
        P(),
    )
    return jax.shard_map(shards, mesh=mesh, in_specs=in_specs, out_specs=out_specs, check_vma=False)
```

profile of v0, /device:TPU:0, one launch (start us, length us, event | category | flops | bytes accessed | tf_op | source)
XLA Modules:
  0.0 3158.2 jit_solution(11104834085633158624)
XLA Ops:
  62.0 553.4 %while.76 = (s32[]{:T(128)}, bf16[2,16,2048]{2,1,0:T(8,128)(2,1)S(1)}, f32[2,16,512]{2,1,0:T(8,128)S(1)}, f32[24,2,16,4,512]{4,2,3,1,0:T(8,128)}, f32[24,2,16,51...) while((s32[]{:T(128)}, ...), condition=%wide.region_1.3_spmd.clone, body=%wide.region_0.2_spmd.clone.sunk | while | flops 269090816 | bytes 19464324 | solution.py:43
  616.6 474.4 %while.74 = (s32[]{:T(128)}, bf16[1,16,2048]{2,1,0:T(8,128)(2,1)S(1)}, f32[1,16,512]{2,1,0:T(8,128)S(1)}, f32[24,1,16,4,512]{4,2,3,1,0:T(8,128)}, f32[24,1,16,51...) while((s32[]{:T(128)}, ...), condition=%wide.region_3.5_spmd, body=%wide.region_2.4_spmd.sunk | while | flops 134537216 | bytes 9732213 | solution.py:43
  1205.7 637.4 %while.77 = (s32[]{:T(128)}, f32[1,16,512]{2,1,0:T(8,128)}, f32[1,16,512]{2,1,0:T(8,128)S(1)}, bf16[24,1,16,4,512]{4,2,3,1,0:T(8,128)(2,1)S(1)}, f32[24,1,16,512...) while((s32[]{:T(128)}, f32[1,16,512]{2,1,0:T(8,128)}, ...), condition=%wide.region_8.10_spmd.clone, body=%wide.region_6.9_spmd.clone.sunk | while | flops 134807552 | bytes 9961667 | solution.py:72
  1214.7 21.1 reduce-scatter.11.cloned.1.call-done
  1244.7 17.5 reduce-scatter.11.cloned.1.call-done
  1271.1 17.5 reduce-scatter.11.cloned.1.call-done
  1350.3 17.5 reduce-scatter.11.cloned.1.call-done
  1376.7 17.5 reduce-scatter.11.cloned.1.call-done
  1403.1 17.5 reduce-scatter.11.cloned.1.call-done
  1429.5 17.5 reduce-scatter.11.cloned.1.call-done
  1455.9 17.5 reduce-scatter.11.cloned.1.call-done
  1482.3 17.5 reduce-scatter.11.cloned.1.call-done
  1508.7 17.5 reduce-scatter.11.cloned.1.call-done
  1587.9 17.5 reduce-scatter.11.cloned.1.call-done
  1614.3 17.5 reduce-scatter.11.cloned.1.call-done
  1640.7 17.5 reduce-scatter.11.cloned.1.call-done
  1846.1 763.3 %while.75 = (s32[]{:T(128)}, f32[2,16,512]{2,1,0:T(8,128)}, f32[2,16,512]{2,1,0:T(8,128)S(1)}, bf16[24,2,16,4,512]{4,2,1,3,0:T(8,128)(2,1)S(1)}, f32[24,2,16,512...) while((s32[]{:T(128)}, f32[2,16,512]{2,1,0:T(8,128)}, ...), condition=%wide.region_13.15_spmd, body=%wide.region_11.14_spmd.sunk | while | flops 269598720 | bytes 19923120 | solution.py:72
  1860.0 18.0 reduce-scatter.9.cloned.1.call-done
  1891.7 18.0 reduce-scatter.9.cloned.1.call-done
  1923.5 18.0 reduce-scatter.9.cloned.1.call-done
  1955.3 18.0 reduce-scatter.9.cloned.1.call-done
  1987.1 18.0 reduce-scatter.9.cloned.1.call-done
  2018.9 18.0 reduce-scatter.9.cloned.1.call-done
  2050.7 18.0 reduce-scatter.9.cloned.1.call-done
  2082.5 18.0 reduce-scatter.9.cloned.1.call-done
  2114.3 18.0 reduce-scatter.9.cloned.1.call-done
  2146.1 18.0 reduce-scatter.9.cloned.1.call-done
  2177.9 18.0 reduce-scatter.9.cloned.1.call-done
  2209.7 18.0 reduce-scatter.9.cloned.1.call-done
  2241.5 18.0 reduce-scatter.9.cloned.1.call-done
  2273.3 18.0 reduce-scatter.9.cloned.1.call-done
  2305.1 18.0 reduce-scatter.9.cloned.1.call-done
  2337.0 18.1 reduce-scatter.9.cloned.1.call-done
  2368.8 18.0 reduce-scatter.9.cloned.1.call-done
  2400.6 18.0 reduce-scatter.9.cloned.1.call-done
  2432.4 18.0 reduce-scatter.9.cloned.1.call-done
  2464.2 18.0 reduce-scatter.9.cloned.1.call-done
  2496.0 18.0 reduce-scatter.9.cloned.1.call-done
  2527.8 18.0 reduce-scatter.9.cloned.1.call-done
  2559.6 18.0 reduce-scatter.9.cloned.1.call-done
  2591.4 18.0 reduce-scatter.9.cloned.1.call-done
  2623.7 70.3 %reduce-scatter.5.cloned.1.call-done = f32[2,512,275]{1,2,0:T(8,128)} async-done(((f32[2,2048,275]{1,2,0:T(8,128)}), f32[2,512,275]{1,2,0:T(8,128)}) %reduce-scatter.5.cloned.1.call-update) | async-done | bytes 1126416 | tf_op jit(solution)/shard_map/reduce_scatter | solution.py:192
  2714.3 57.1 %all-reduce.13.cloned.1.call-done = f32[695296]{0:T(1024)} async-done(((f32[695296]{0:T(1024)}), f32[695296]{0:T(1024)}) %all-reduce.13.cloned.1.call-update) | async-done | bytes 2781200
  2791.5 19.1 pad_maximum_fusion
  2811.3 39.5 %psum.15 = f32[2,275]{1,0:T(2,128)} all-reduce(f32[2,275]{1,0:T(2,128)S(1)} %pad_maximum_fusion.7), channel_id=1, replica_groups=mesh['rep'=8,'shard'=4] {'rep','shard'}, use_global_device_ids=true, to_apply=%region_22.24 | all-reduce | flops 550 | bytes 4400 | tf_op jit(solution)/shard_map/psum | solution.py:277
  2850.8 52.2 %all-reduce.11.cloned.1.call-done = f32[2,275,100]{2,1,0:T(8,128)} async-done(((f32[2,275,100]{2,1,0:T(8,128)}), f32[2,275,100]{2,1,0:T(8,128)}) %all-reduce.11.cloned.1.call-update) | async-done | bytes 220016 | tf_op jit(solution)/shard_map/psum | solution.py:277
  2904.8 32.3 %all-gather.7.cloned.1.call-done = f32[8,1,86912]{2,1,0:T(1,128)} async-done(((f32[1,1,86912]{2,1,0:T(1,128)}), f32[8,1,86912]{2,1,0:T(1,128)}) %all-gather.7.cloned.1.call-update) | async-done | bytes 2781200 | tf_op jit(solution)/shard_map/all_gather | solution.py:273
  2947.7 198.2 %reduce-scatter.7.cloned.1.call-done = f32[2,4,256,512]{2,3,1,0:T(8,128)} async-done(((f32[2,4,2048,512]{2,3,1,0:T(8,128)}), f32[2,4,256,512]{2,3,1,0:T(8,128)}) %reduce-scatter.7.cloned.1.call-update) | async-done | bytes 4194320 | tf_op jit(solution)/shard_map/reduce_scatter | solution.py:239
  (940 shorter events, 2007.4 us)
Async XLA Ops:
  7.2 1101.7 %all-gather.5.cloned.1.call-start = ((), (), s32[]{:S(2)}) async-start(), calls=%async_computation.6 | async-start | bytes 2867200 | tf_op jit(solution)/shard_map/all_gather | solution.py:150
  1144.9 30.4 all-to-all-start
  1205.7 30.1 reduce-scatter.11.cloned.1.call-start
  1235.8 26.4 reduce-scatter.11.cloned.1.call-start
  1262.2 26.4 reduce-scatter.11.cloned.1.call-start
  1288.6 26.4 reduce-scatter.11.cloned.1.call-start
  1315.0 26.4 reduce-scatter.11.cloned.1.call-start
  1341.4 26.4 reduce-scatter.11.cloned.1.call-start
  1394.2 26.4 reduce-scatter.11.cloned.1.call-start
  1420.6 26.4 reduce-scatter.11.cloned.1.call-start
  1447.0 26.4 reduce-scatter.11.cloned.1.call-start
  1473.4 26.4 reduce-scatter.11.cloned.1.call-start
  1499.8 26.4 reduce-scatter.11.cloned.1.call-start
  1631.8 26.4 reduce-scatter.11.cloned.1.call-start
  1658.2 26.4 reduce-scatter.11.cloned.1.call-start
  1684.6 26.4 reduce-scatter.11.cloned.1.call-start
  1711.0 26.4 reduce-scatter.11.cloned.1.call-start
  1737.4 26.4 reduce-scatter.11.cloned.1.call-start
  1763.8 26.4 reduce-scatter.11.cloned.1.call-start
  1846.1 31.8 %reduce-scatter.9.cloned.1.call-start = ((), (), s32[]{:S(2)}) async-start(), calls=%async_computation.12 | async-start | bytes 327680 | tf_op jit(solution)/shard_map/while/body/eval_jaxpr/reduce_scatter | solution.py:204
  1877.9 31.8 %reduce-scatter.9.cloned.1.call-start = ((), (), s32[]{:S(2)}) async-start(), calls=%async_computation.12 | async-start | bytes 327680 | tf_op jit(solution)/shard_map/while/body/eval_jaxpr/reduce_scatter | solution.py:204
  1909.7 31.8 %reduce-scatter.9.cloned.1.call-start = ((), (), s32[]{:S(2)}) async-start(), calls=%async_computation.12 | async-start | bytes 327680 | tf_op jit(solution)/shard_map/while/body/eval_jaxpr/reduce_scatter | solution.py:204
  1941.5 31.8 %reduce-scatter.9.cloned.1.call-start = ((), (), s32[]{:S(2)}) async-start(), calls=%async_computation.12 | async-start | bytes 327680 | tf_op jit(solution)/shard_map/while/body/eval_jaxpr/reduce_scatter | solution.py:204
  1973.3 31.8 %reduce-scatter.9.cloned.1.call-start = ((), (), s32[]{:S(2)}) async-start(), calls=%async_computation.12 | async-start | bytes 327680 | tf_op jit(solution)/shard_map/while/body/eval_jaxpr/reduce_scatter | solution.py:204
  2005.1 31.8 %reduce-scatter.9.cloned.1.call-start = ((), (), s32[]{:S(2)}) async-start(), calls=%async_computation.12 | async-start | bytes 327680 | tf_op jit(solution)/shard_map/while/body/eval_jaxpr/reduce_scatter | solution.py:204
  2036.9 31.8 %reduce-scatter.9.cloned.1.call-start = ((), (), s32[]{:S(2)}) async-start(), calls=%async_computation.12 | async-start | bytes 327680 | tf_op jit(solution)/shard_map/while/body/eval_jaxpr/reduce_scatter | solution.py:204
  2068.7 31.8 %reduce-scatter.9.cloned.1.call-start = ((), (), s32[]{:S(2)}) async-start(), calls=%async_computation.12 | async-start | bytes 327680 | tf_op jit(solution)/shard_map/while/body/eval_jaxpr/reduce_scatter | solution.py:204
  2100.5 31.8 %reduce-scatter.9.cloned.1.call-start = ((), (), s32[]{:S(2)}) async-start(), calls=%async_computation.12 | async-start | bytes 327680 | tf_op jit(solution)/shard_map/while/body/eval_jaxpr/reduce_scatter | solution.py:204
  2132.3 31.8 %reduce-scatter.9.cloned.1.call-start = ((), (), s32[]{:S(2)}) async-start(), calls=%async_computation.12 | async-start | bytes 327680 | tf_op jit(solution)/shard_map/while/body/eval_jaxpr/reduce_scatter | solution.py:204
  2164.1 31.8 %reduce-scatter.9.cloned.1.call-start = ((), (), s32[]{:S(2)}) async-start(), calls=%async_computation.12 | async-start | bytes 327680 | tf_op jit(solution)/shard_map/while/body/eval_jaxpr/reduce_scatter | solution.py:204
  2195.9 31.8 %reduce-scatter.9.cloned.1.call-start = ((), (), s32[]{:S(2)}) async-start(), calls=%async_computation.12 | async-start | bytes 327680 | tf_op jit(solution)/shard_map/while/body/eval_jaxpr/reduce_scatter | solution.py:204
  2227.7 31.8 %reduce-scatter.9.cloned.1.call-start = ((), (), s32[]{:S(2)}) async-start(), calls=%async_computation.12 | async-start | bytes 327680 | tf_op jit(solution)/shard_map/while/body/eval_jaxpr/reduce_scatter | solution.py:204
  2259.6 31.8 %reduce-scatter.9.cloned.1.call-start = ((), (), s32[]{:S(2)}) async-start(), calls=%async_computation.12 | async-start | bytes 327680 | tf_op jit(solution)/shard_map/while/body/eval_jaxpr/reduce_scatter | solution.py:204
  2291.4 31.8 %reduce-scatter.9.cloned.1.call-start = ((), (), s32[]{:S(2)}) async-start(), calls=%async_computation.12 | async-start | bytes 327680 | tf_op jit(solution)/shard_map/while/body/eval_jaxpr/reduce_scatter | solution.py:204
  2323.2 31.8 %reduce-scatter.9.cloned.1.call-start = ((), (), s32[]{:S(2)}) async-start(), calls=%async_computation.12 | async-start | bytes 327680 | tf_op jit(solution)/shard_map/while/body/eval_jaxpr/reduce_scatter | solution.py:204
  2355.0 31.8 %reduce-scatter.9.cloned.1.call-start = ((), (), s32[]{:S(2)}) async-start(), calls=%async_computation.12 | async-start | bytes 327680 | tf_op jit(solution)/shard_map/while/body/eval_jaxpr/reduce_scatter | solution.py:204
  2386.8 31.8 %reduce-scatter.9.cloned.1.call-start = ((), (), s32[]{:S(2)}) async-start(), calls=%async_computation.12 | async-start | bytes 327680 | tf_op jit(solution)/shard_map/while/body/eval_jaxpr/reduce_scatter | solution.py:204
  2418.6 31.8 %reduce-scatter.9.cloned.1.call-start = ((), (), s32[]{:S(2)}) async-start(), calls=%async_computation.12 | async-start | bytes 327680 | tf_op jit(solution)/shard_map/while/body/eval_jaxpr/reduce_scatter | solution.py:204
  2450.4 31.8 %reduce-scatter.9.cloned.1.call-start = ((), (), s32[]{:S(2)}) async-start(), calls=%async_computation.12 | async-start | bytes 327680 | tf_op jit(solution)/shard_map/while/body/eval_jaxpr/reduce_scatter | solution.py:204
  2482.2 31.8 %reduce-scatter.9.cloned.1.call-start = ((), (), s32[]{:S(2)}) async-start(), calls=%async_computation.12 | async-start | bytes 327680 | tf_op jit(solution)/shard_map/while/body/eval_jaxpr/reduce_scatter | solution.py:204
  2514.0 31.8 %reduce-scatter.9.cloned.1.call-start = ((), (), s32[]{:S(2)}) async-start(), calls=%async_computation.12 | async-start | bytes 327680 | tf_op jit(solution)/shard_map/while/body/eval_jaxpr/reduce_scatter | solution.py:204
  2545.8 31.8 %reduce-scatter.9.cloned.1.call-start = ((), (), s32[]{:S(2)}) async-start(), calls=%async_computation.12 | async-start | bytes 327680 | tf_op jit(solution)/shard_map/while/body/eval_jaxpr/reduce_scatter | solution.py:204
  2577.6 31.8 %reduce-scatter.9.cloned.1.call-start = ((), (), s32[]{:S(2)}) async-start(), calls=%async_computation.12 | async-start | bytes 327680 | tf_op jit(solution)/shard_map/while/body/eval_jaxpr/reduce_scatter | solution.py:204
  2609.4 84.6 %reduce-scatter.5.cloned.1.call-start = ((), (), s32[]{:S(2)}) async-start(), calls=%async_computation.8 | async-start | bytes 5734400 | tf_op jit(solution)/shard_map/reduce_scatter | solution.py:192
  2610.2 161.2 %all-reduce.13.cloned.1.call-start = ((), (), s32[]{:S(2)}) async-start(), calls=%async_computation.11 | async-start | bytes 5562368
  2704.2 198.8 %all-reduce.11.cloned.1.call-start = ((), (), s32[]{:S(2)}) async-start(), calls=%async_computation.7 | async-start | bytes 573440 | tf_op jit(solution)/shard_map/psum | solution.py:277
  2710.2 226.8 %all-gather.7.cloned.1.call-start = ((), (), s32[]{:S(2)}) async-start(), calls=%async_computation.10 | async-start | bytes 3128832 | tf_op jit(solution)/shard_map/all_gather | solution.py:273
  2773.5 372.4 %reduce-scatter.7.cloned.1.call-start = ((), (), s32[]{:S(2)}) async-start(), calls=%async_computation.9 | async-start | bytes 37748736 | tf_op jit(solution)/shard_map/reduce_scatter | solution.py:239
  (45 other events, 1454.6 us)
Sparse Core Ops, SparseCore 0:
  9.6 52.1 all-gather.4
  1214.8 20.9 reduce-scatter.10
  1244.8 17.3 reduce-scatter.10
  1271.2 17.3 reduce-scatter.10
  1297.6 17.3 reduce-scatter.10
  1324.0 17.3 reduce-scatter.10
  1350.4 17.3 reduce-scatter.10
  1376.8 17.3 reduce-scatter.10
  1403.2 17.3 reduce-scatter.10
  1429.6 17.3 reduce-scatter.10
  1456.0 17.3 reduce-scatter.10
  1482.4 17.3 reduce-scatter.10
  1508.8 17.3 reduce-scatter.10
  1535.2 17.3 reduce-scatter.10
  1561.6 17.3 reduce-scatter.10
  1588.0 17.3 reduce-scatter.10
  1614.4 17.3 reduce-scatter.10
  1640.8 17.3 reduce-scatter.10
  1667.2 17.3 reduce-scatter.10
  1860.1 17.8 reduce-scatter.8
  1891.8 17.8 reduce-scatter.8
  1923.6 17.8 reduce-scatter.8
  1955.4 17.8 reduce-scatter.8
  1987.2 17.8 reduce-scatter.8
  2019.0 17.8 reduce-scatter.8
  2050.8 17.8 reduce-scatter.8
  2082.6 17.8 reduce-scatter.8
  2114.4 17.8 reduce-scatter.8
  2146.2 17.8 reduce-scatter.8
  2178.0 17.8 reduce-scatter.8
  2209.8 17.8 reduce-scatter.8
  2241.6 17.8 reduce-scatter.8
  2273.4 17.8 reduce-scatter.8
  2305.2 17.8 reduce-scatter.8
  2337.0 17.9 reduce-scatter.8
  2368.9 17.8 reduce-scatter.8
  2400.7 17.8 reduce-scatter.8
  2432.5 17.8 reduce-scatter.8
  2464.3 17.8 reduce-scatter.8
  2496.1 17.8 reduce-scatter.8
  2527.9 17.8 reduce-scatter.8
  2559.7 17.8 reduce-scatter.8
  2591.5 17.8 reduce-scatter.8
  2612.6 81.3 reduce-scatter.4
  2704.3 67.0 all-reduce.12
  2777.6 125.3 all-reduce.10
  2905.3 31.7 all-gather.6
  2940.6 205.2 reduce-scatter.6
  (6 shorter events, 103.9 us)
where the time goes:
time: 3180 us; the launch traced here: 3160 us
  waiting for transfers between devices  1270 us (40%)
  matrix products  753 us (24%)
  blocking collectives  700 us (22%)
  local copies, waits for them, and re-layouts  205 us (6%)
  other arithmetic  204 us (6%)
    reduce_scatter x24, waiting for transfers between devices, move_both_grad(): lax.psum_scatter(partial_sum, 'shard', scatter_dimension=2, tiled=True)  432 us
    reduce_scatter x24, waiting for transfers between devices, move_front_grad(): lax.psum_scatter(partial_sum, 'shard', scatter_dimension=2, tiled=True)  424 us
    dot_general x48, matrix products, retreat(): jnp.einsum('mbgn,mgkn->mbk', gate_grad, w_rec, preferred_element_type=jnp...  413 us
    all_gather x24, blocking collectives, move_both(): return lax.all_gather(own_hidden, 'shard', axis=2, tiled=True)  322 us
    all_gather x24, blocking collectives, move_front(): return lax.all_gather(own_hidden, 'shard', axis=2, tiled=True)  316 us
    dot_general x48, matrix products, advance(): jnp.einsum('mbk,mgkn->mbgn', full_hidden, w_rec, preferred_element_type=j...  303 us
    reduce_scatter x1, waiting for transfers between devices, shards(): lax.psum_scatter(jnp.stack([front_rec_grad, back_rec_grad]), 'rep', scatt...  198 us
    reduce_scatter x1, waiting for transfers between devices, shards(): lax.psum_scatter(out_whole, 'shard', scatter_dimension=1, tiled=True)  70.3 us
  transfers between devices with their start and end apart: 56, of which 53 were waited for; matrix products, arithmetic and copies ran while one was open for 17% of the time, Pallas kernels for 0%

commit v1 on v0

v1 whole, which is shorter than its diff:
```python
import functools
import math

import jax
import jax.numpy as jnp
from jax import lax
from jax.experimental import pallas as pl
from jax.experimental.pallas import tpu as pltpu
from jax.sharding import PartitionSpec as P

PRECISE = lax.Precision.HIGHEST
MESH = pl.DeviceIdType.MESH
LANES = 128
MIB = 1 << 20


def one_hot(ids, width, out_type):
    return (ids[..., None] == jnp.arange(width, dtype=jnp.int32)).astype(out_type)


def loss_grad(logits, targets, active, factor):
    probabilities = jax.nn.softmax(logits, axis=-1)
    picked = one_hot(targets, logits.shape[-1], jnp.float32)
    return ((probabilities - picked) * (active * factor)[:, None]).astype(jnp.bfloat16)


def peers_of(place, count):
    if count == 4:
        return [place + 1 - 2 * lax.rem(place, 2), lax.rem(place + 2, 4), 3 - place]
    if count == 2:
        return [1 - place]
    assert count == 1
    return []


def greet(peers):
    barrier = pltpu.get_barrier_semaphore()
    for peer in peers:
        pl.semaphore_signal(barrier, inc=1, device_id={"shard": peer}, device_id_type=MESH)
    pl.semaphore_wait(barrier, len(peers))


def dot_plain(left, right):
    return jnp.dot(left, right, preferred_element_type=jnp.float32)


def dot_turned(left, right):
    return lax.dot_general(left, right, (((1,), (1,)), ((), ())), preferred_element_type=jnp.float32)


def forward_kernel(
    count,
    x_front,
    x_back,
    w_in,
    bias,
    w_hbm,
    full_front,
    full_back,
    acts_front,
    acts_back,
    cell_front,
    cell_back,
    weights,
    load_sem,
    send_sem,
    recv_sem,
):
    place = lax.axis_index("shard")
    peers = peers_of(place, count)
    units = weights.shape[3]
    length, half_len = full_front.shape[0], full_back.shape[0]
    loads = [pltpu.make_async_copy(w_hbm.at[m], weights.at[m], load_sem.at[m]) for m in range(2)]
    for load in loads:
        load.start()
    greet(peers)
    models = ((x_front, full_front, acts_front, cell_front), (x_back, full_back, acts_back, cell_back))

    def columns(owner):
        return pl.ds(pl.multiple_of(owner * units, units), units)

    def exchange(m, t, k):
        full = models[m][1]
        slot = lax.rem(t, 2)
        return pltpu.make_async_remote_copy(
            src_ref=full.at[t, :, columns(place)],
            dst_ref=full.at[t, :, columns(place)],
            send_sem=send_sem.at[m, slot, k],
            recv_sem=recv_sem.at[m, slot, k],
            device_id={"shard": peers[k]},
            device_id_type=MESH,
        )

    def finish(m, t, sums, memory, last):
        full, acts, cell = models[m][1:]
        in_gate = jax.nn.sigmoid(sums[0])
        forget = jax.nn.sigmoid(sums[1])
        candidate = jnp.tanh(sums[2])
        out_gate = jax.nn.sigmoid(sums[3])
        new_memory = in_gate * candidate if memory is None else forget * memory + in_gate * candidate
        full[t, :, columns(place)] = (out_gate * jnp.tanh(new_memory)).astype(jnp.bfloat16)
        for k in range(len(peers)):
            exchange(m, t, k).start()
        for g, value in enumerate((in_gate, forget, candidate, out_gate)):
            acts[t, g] = value
        cell[t] = new_memory

    def start_sums(m, t):
        x_t = models[m][0][t]
        return [bias[m, g] + dot_plain(x_t, w_in[m, g]) for g in range(4)]

    def add_chunk(m, t, owner, sums):
        part = models[m][1][t, :, columns(owner)]
        rows = columns(owner)
        return [sums[g] + dot_plain(part, weights[m, g, rows, :]) for g in range(4)]

    def advance(m, t):
        sums = add_chunk(m, t - 1, place, start_sums(m, t))
        for k in range(len(peers)):
            copy = exchange(m, t - 1, k)
            copy.wait_recv()
            sums = add_chunk(m, t - 1, peers[k], sums)
        for k in range(len(peers)):
            exchange(m, t - 1, k).wait_send()
        finish(m, t, sums, models[m][3][t - 1], False)

    finish(0, 0, start_sums(0, 0), None, False)
    finish(1, 0, start_sums(1, 0), None, False)
    for load in loads:
        load.wait()

    def both(t, carry):
        advance(0, t)
        advance(1, t)
        return carry

    def front_only(t, carry):
        advance(0, t)
        return carry

    lax.fori_loop(1, half_len, both, 0)
    lax.fori_loop(half_len, length, front_only, 0)
    for m, end in ((0, length), (1, half_len)):
        for k in range(len(peers)):
            copy = exchange(m, end - 1, k)
            copy.wait_send()
            copy.wait_recv()


def run_forward(count, x_front, x_back, w_in, bias, w_rec):
    length, rows = x_front.shape[:2]
    half_len = x_back.shape[0]
    units, shard_units = w_rec.shape[2:]
    vmem = pl.BlockSpec(memory_space=pltpu.VMEM)
    shape = jax.ShapeDtypeStruct
    return pl.pallas_call(
        functools.partial(forward_kernel, count),
        out_shape=(
            shape((length, rows, units), jnp.bfloat16),
            shape((half_len, rows, units), jnp.bfloat16),
            shape((length, 4, rows, shard_units), jnp.float32),
            shape((half_len, 4, rows, shard_units), jnp.float32),
            shape((length, rows, shard_units), jnp.float32),
            shape((half_len, rows, shard_units), jnp.float32),
        ),
        in_specs=[vmem] * 4 + [pl.BlockSpec(memory_space=pl.ANY)],
        out_specs=(vmem,) * 6,
        scratch_shapes=[
            pltpu.VMEM(w_rec.shape, jnp.bfloat16),
            pltpu.SemaphoreType.DMA((2,)),
            pltpu.SemaphoreType.DMA((2, 2, max(count - 1, 1))),
            pltpu.SemaphoreType.DMA((2, 2, max(count - 1, 1))),
        ],
        compiler_params=pltpu.CompilerParams(
            collective_id=0, has_side_effects=True, vmem_limit_bytes=56 * MIB
        ),
        name="recurrence_forward",
    )(x_front, x_back, w_in, bias, w_rec)


def backward_kernel(
    count,
    acts_front,
    acts_back,
    cell_front,
    cell_back,
    dec_front,
    dec_back,
    w_hbm,
    gates_front,
    gates_back,
    weights,
    outbox,
    inbox,
    own_part,
    cell_grad,
    load_sem,
    send_sem,
    recv_sem,
):
    place = lax.axis_index("shard")
    peers = peers_of(place, count)
    units = weights.shape[3]
    length, half_len = cell_front.shape[0], cell_back.shape[0]
    loads = [pltpu.make_async_copy(w_hbm.at[m], weights.at[m], load_sem.at[m]) for m in range(2)]
    for load in loads:
        load.start()
    greet(peers)
    models = (
        (acts_front, cell_front, dec_front, gates_front),
        (acts_back, cell_back, dec_back, gates_back),
    )

    def rows_of(owner):
        return pl.ds(pl.multiple_of(owner * units, units), units)

    def exchange(m, t, k):
        slot = lax.rem(t, 2)
        return pltpu.make_async_remote_copy(
            src_ref=outbox.at[m, slot, k],
            dst_ref=inbox.at[m, slot, k],
            send_sem=send_sem.at[m, slot, k],
            recv_sem=recv_sem.at[m, slot, k],
            device_id={"shard": peers[k]},
            device_id_type=MESH,
        )

    def gate_grads(m, t, grad_hidden, carried, prev_memory):
        acts, cell, dec, gates = models[m]
        in_gate, forget, candidate, out_gate = (acts[t, g] for g in range(4))
        squashed = jnp.tanh(cell[t])
        grad_memory = grad_hidden * out_gate * (1.0 - squashed * squashed)
        if carried is not None:
            grad_memory = carried + grad_memory
        cell_grad[m] = grad_memory * forget
        forget_part = jnp.zeros_like(grad_memory)
        if prev_memory is not None:
            forget_part = grad_memory * prev_memory * forget * (1.0 - forget)
        values = (
            grad_memory * candidate * in_gate * (1.0 - in_gate),
            forget_part,
            grad_memory * in_gate * (1.0 - candidate * candidate),
            grad_hidden * squashed * out_gate * (1.0 - out_gate),
        )
        narrow = [value.astype(jnp.bfloat16) for value in values]
        for g in range(4):
            gates[t, :, g * units : (g + 1) * units] = narrow[g]
        return narrow

    def product(m, narrow, owner):
        total = None
        for g in range(4):
            part = dot_turned(narrow[g], weights[m, g, rows_of(owner), :])
            total = part if total is None else total + part
        return total

    def send_products(m, t, narrow):
        for k in reversed(range(len(peers))):
            outbox[m, lax.rem(t, 2), k] = product(m, narrow, peers[k])
            exchange(m, t, k).start()
        own_part[m] = product(m, narrow, place)

    def incoming(m, t):
        total = models[m][2][t - 1] + own_part[m]
        for k in range(len(peers)):
            exchange(m, t, k).wait_recv()
            total = total + inbox[m, lax.rem(t, 2), k]
        for k in range(len(peers)):
            exchange(m, t, k).wait_send()
        return total

    def retreat(m, t):
        total = incoming(m, t + 1)
        narrow = gate_grads(m, t, total, cell_grad[m], models[m][1][t - 1])
        send_products(m, t, narrow)

    for m, end in ((0, length), (1, half_len)):
        t = end - 1
        narrow = gate_grads(m, t, models[m][2][t], None, models[m][1][t - 1])
        loads[m].wait()
        send_products(m, t, narrow)

    def both(step, carry):
        retreat(0, length - 1 - step)
        retreat(1, half_len - 1 - step)
        return carry

    def front_only(step, carry):
        retreat(0, length - 1 - step)
        return carry

    lax.fori_loop(1, half_len - 1, both, 0)
    retreat(0, length - half_len)
    gate_grads(1, 0, incoming(1, 1), cell_grad[1], None)
    lax.fori_loop(half_len, length - 1, front_only, 0)
    gate_grads(0, 0, incoming(0, 1), cell_grad[0], None)


def run_backward(count, acts, cells, decs, w_rec):
    length, rows, shard_units = cells[0].shape
    half_len = cells[1].shape[0]
    vmem = pl.BlockSpec(memory_space=pltpu.VMEM)
    shape = jax.ShapeDtypeStruct
    box = (2, 2, max(count - 1, 1), rows, shard_units)
    return pl.pallas_call(
        functools.partial(backward_kernel, count),
        out_shape=(
            shape((length, rows, 4 * shard_units), jnp.bfloat16),
            shape((half_len, rows, 4 * shard_units), jnp.bfloat16),
        ),
        in_specs=[vmem] * 6 + [pl.BlockSpec(memory_space=pl.ANY)],
        out_specs=(vmem,) * 2,
        scratch_shapes=[
            pltpu.VMEM(w_rec.shape, jnp.bfloat16),
            pltpu.VMEM(box, jnp.float32),
            pltpu.VMEM(box, jnp.float32),
            pltpu.VMEM((2, rows, shard_units), jnp.float32),
            pltpu.VMEM((2, rows, shard_units), jnp.float32),
            pltpu.SemaphoreType.DMA((2,)),
            pltpu.SemaphoreType.DMA(box[:3]),
            pltpu.SemaphoreType.DMA(box[:3]),
        ],
        compiler_params=pltpu.CompilerParams(
            collective_id=1, has_side_effects=True, vmem_limit_bytes=56 * MIB
        ),
        name="recurrence_backward",
    )(*acts, *cells, *decs, w_rec)


def shifted(values):
    return jnp.concatenate([jnp.zeros_like(values[:1]), values[:-1]], axis=0)


def shards(char_ids, prefix, embedding, w_in, w_rec, gate_bias, w_out, b_out):
    seq_dev, length = char_ids.shape
    half_len = length // 2
    vocab_size, embed = embedding.shape[1:]
    shard_units = w_rec.shape[3]
    count = lax.axis_size("shard")
    factor = 1.0 / math.sqrt(lax.axis_size("rep") * count * seq_dev * length)
    ids_and_prefix = jnp.concatenate([char_ids, prefix[:, None]], axis=1)
    gathered = lax.all_gather(ids_and_prefix, "shard", axis=0, tiled=True)
    group_chars, group_prefix = gathered[:, :length], gathered[:, length]
    full_out = lax.all_gather(w_out, "shard", axis=1, tiled=True)
    group_size = group_chars.shape[0]
    front_in = group_chars.T
    front_target = jnp.concatenate([group_chars[:, 1:], group_chars[:, :1]], axis=1).T
    timeline = jnp.arange(length, dtype=jnp.int32)[:, None]
    front_active = jnp.broadcast_to(
        (timeline < length - 1).astype(jnp.float32), (length, group_size)
    )
    reverse_steps = jnp.arange(half_len, dtype=jnp.int32)[:, None]

    def back_pick(offset):
        spot = jnp.maximum(group_prefix[None, :] - offset - reverse_steps, 0)
        chosen = one_hot(spot, length, jnp.int32) * group_chars[None]
        return jnp.sum(chosen, axis=-1)

    back_in = back_pick(1)
    back_target = back_pick(2)
    back_active = (reverse_steps <= group_prefix[None, :] - 2).astype(jnp.float32)
    depth = -(-embed // LANES) * LANES
    table = jnp.pad(embedding, ((0, 0), (0, 0), (0, depth - embed)))
    inputs = jnp.pad(w_in, ((0, 0), (0, 0), (0, depth - embed), (0, 0)))

    def look_up(ids, m):
        return jnp.einsum(
            "tbv,ve->tbe",
            one_hot(ids, vocab_size, jnp.bfloat16),
            table[m],
            preferred_element_type=jnp.float32,
        ).astype(jnp.bfloat16)

    front_x, back_x = look_up(front_in, 0), look_up(back_in, 1)
    bias_wide = gate_bias.astype(jnp.float32)[:, :, None, :]
    full_front, full_back, acts_front, acts_back, cell_front, cell_back = run_forward(
        count, front_x, back_x, inputs, bias_wide, w_rec
    )
    first_unit = lax.axis_index("shard") * shard_units

    def decode(full, m, target, active):
        rows = full.reshape(-1, full.shape[-1])
        logits = jnp.dot(rows, full_out[m], preferred_element_type=jnp.float32) + b_out[m].astype(
            jnp.float32
        )
        grad = loss_grad(logits, target.reshape(-1), active.reshape(-1), factor)
        dec = jnp.einsum("rv,kv->rk", grad, w_out[m], preferred_element_type=jnp.float32)
        own = lax.dynamic_slice_in_dim(rows, first_unit, shard_units, axis=1)
        out_grad = jnp.einsum("rk,rv->kv", own, grad, preferred_element_type=jnp.float32)
        bout = jnp.sum(grad, axis=0, dtype=jnp.float32)
        return dec.reshape(full.shape[0], group_size, shard_units), out_grad, bout

    front_dec, front_out_grad, front_bout = decode(full_front, 0, front_target, front_active)
    back_dec, back_out_grad, back_bout = decode(full_back, 1, back_target, back_active)
    out_sum, bout_sum = lax.psum(
        (jnp.stack([front_out_grad, back_out_grad]), jnp.stack([front_bout, back_bout])), "rep"
    )
    front_grads, back_grads = run_backward(
        count, (acts_front, acts_back), (cell_front, cell_back), (front_dec, back_dec), w_rec
    )
    front_grads = front_grads.reshape(length, group_size, 4, shard_units)
    back_grads = back_grads.reshape(half_len, group_size, 4, shard_units)
    prev_front, prev_back = shifted(full_front), shifted(full_back)
    front_rec_grad = jnp.einsum(
        "tbk,tbgn->gkn", prev_front, front_grads, preferred_element_type=jnp.float32
    )
    back_rec_grad = jnp.einsum(
        "tbk,tbgn->gkn", prev_back, back_grads, preferred_element_type=jnp.float32
    )
    rec_grad = lax.psum_scatter(
        jnp.stack([front_rec_grad, back_rec_grad]), "rep", scatter_dimension=2, tiled=True
    )
    front_x, back_x = front_x[..., :embed], back_x[..., :embed]
    in_grad = jnp.stack(
        [
            jnp.einsum("tbe,tbgn->gen", front_x, front_grads, preferred_element_type=jnp.float32),
            jnp.einsum("tbe,tbgn->gen", back_x, back_grads, preferred_element_type=jnp.float32),
        ]
    )
    bias_grad = jnp.stack(
        [
            jnp.sum(front_grads, axis=(0, 1), dtype=jnp.float32),
            jnp.sum(back_grads, axis=(0, 1), dtype=jnp.float32),
        ]
    )
    front_dx = jnp.einsum("tbgn,gen->tbe", front_grads, w_in[0], preferred_element_type=jnp.float32)
    back_dx = jnp.einsum("tbgn,gen->tbe", back_grads, w_in[1], preferred_element_type=jnp.float32)
    embed_grad = jnp.stack(
        [
            jnp.einsum(
                "tbv,tbe->ve",
                one_hot(front_in, vocab_size, jnp.float32),
                front_dx,
                precision=PRECISE,
            ),
            jnp.einsum(
                "tbv,tbe->ve", one_hot(back_in, vocab_size, jnp.float32), back_dx, precision=PRECISE
            ),
        ]
    )
    in_sum, bias_sum = lax.psum((in_grad, bias_grad), "rep")
    embed_sum = lax.psum(embed_grad, ("rep", "shard"))
    return (embed_sum, in_sum, rec_grad, bias_sum, out_sum, bout_sum)


def solution(mesh):
    in_specs = (
        P(("rep", "shard"), None),
        P(("rep", "shard")),
        P(),
        P(None, None, None, "shard"),
        P(None, None, None, "shard"),
        P(None, None, "shard"),
        P(None, "shard", None),
        P(),
    )
    out_specs = (
        P(),
        P(None, None, None, "shard"),
        P(None, None, "rep", "shard"),
        P(None, None, "shard"),
        P(None, "shard", None),
        P(),
    )
    return jax.shard_map(shards, mesh=mesh, in_specs=in_specs, out_specs=out_specs, check_vma=False)
```

time: 3180 us -> 1010 us (0.32)
  waiting for transfers between devices: 1270 us -> 333 us
  matrix products: 753 us -> 43.5 us
  blocking collectives: 700 us -> 36.5 us
  Pallas kernels: 0 us -> 508 us
  other arithmetic: 204 us -> 28.1 us
  local copies, waits for them, and re-layouts: 205 us -> 40.5 us
    reduce_scatter x49 -> x0, waiting for transfers between devices: 926 us -> none  [the longest x24 432 us: move_both_grad(): lax.psum_scatter(partial_sum, 'shard', scatter_dimension=2, tiled=True)]
    dot_general x106 -> x8, matrix products: 730 us -> 14.5 us  [the longest x2 5.06 us: decode(): jnp.dot(rows, full_out[m], preferred_element_type=jnp.float32)]
    all_gather x49 -> x1, blocking collectives: 650 us -> 13.5 us  [shards(): gathered = lax.all_gather(ids_and_prefix, 'shard', axis=0, tiled=True)]
    pallas_call x0 -> x2, Pallas kernels: none -> 508 us  [the longest x1 270 us: run_backward(): pl.pallas_call(functools.partial(backward_kernel, count), out_shape=(shap...]
    psum x1 -> x2, waiting for transfers between devices: 52.2 us -> 130 us  [the longest x1 70.6 us: shards(): in_sum, bias_sum = lax.psum((in_grad, bias_grad), 'rep')]
    dynamic_update_slice x144 -> x0, other arithmetic: 66.4 us -> none  [the longest x96 65.7 us: run_forward(): return lax.scan(advance, start_pair, projected)]
    unnamed x7 -> x4, waiting for transfers between devices: 57.9 us -> 0.07 us
    squeeze x48 -> x0, local copies, waits for them, and re-layouts: 45.2 us -> none  [run_forward(): return lax.scan(advance, start_pair, projected)]
  transfers between devices with their start and end apart: 56 -> 4, of which waited for: 53 -> 3; matrix products, arithmetic and copies ran while one was open for 17% -> 6% of each run, Pallas kernels for 0% -> 24%
where the time goes in v1:
time: 1010 us; the launch traced here: 1000 us
  Pallas kernels  508 us (50%)
  waiting for transfers between devices  333 us (33%)
  matrix products  43.5 us (4%)
  local copies, waits for them, and re-layouts  40.5 us (4%)
  blocking collectives  36.5 us (4%)
  other arithmetic  28.1 us (3%)
  between operations  14.5 us (1%)
    pallas_call x1, Pallas kernels, run_backward(): pl.pallas_call(functools.partial(backward_kernel, count), out_shape=(shap...  270 us
    pallas_call x1, Pallas kernels, run_forward(): pl.pallas_call(functools.partial(forward_kernel, count), out_shape=(shape...  238 us
    reduce_scatter x1, waiting for transfers between devices, shards(): lax.psum_scatter(jnp.stack([front_rec_grad, back_rec_grad]), 'rep', scatt...  203 us
    psum x1, waiting for transfers between devices, shards(): in_sum, bias_sum = lax.psum((in_grad, bias_grad), 'rep')  70.6 us
    psum x1, waiting for transfers between devices, shards(): embed_sum = lax.psum(embed_grad, ('rep', 'shard'))  59.2 us
    psum x1, blocking collectives, shards(): in_sum, bias_sum = lax.psum((in_grad, bias_grad), 'rep')  22.9 us
  transfers between devices with their start and end apart: 4, of which 3 were waited for; matrix products, arithmetic and copies ran while one was open for 6% of the time, Pallas kernels for 24%

profile of v1, /device:TPU:0, one launch (start us, length us, event | category | flops | bytes accessed | tf_op | source)
XLA Modules:
  0.0 1004.0 jit_solution(16067636676289777082)
XLA Ops:
  7.3 2.0 copy.115
  9.5 13.5 %all-gather = s32[4,4,49]{2,1,0:T(4,128)S(1)} all-gather(s32[1,4,49]{2,1,0:T(4,128)S(1)} %add_bitcast_fusion.1), channel_id=1, replica_groups=mesh['rep'=8,'shard'=4] {'shard'}, dimensions={0}, use_global_device_ids=true | all-gather | bytes 3920 | tf_op jit(solution)/shard_map/all_gather | solution.py:342
  23.7 0.6 reshape.135.bias
  24.3 1.0 select_reduce_fusion
  25.8 0.9 copy-done.4
  26.7 1.1 pad.11.w_in
  27.9 0.9 convolution_convert_fusion.x_back
  29.1 1.0 fusion.28.x_front
  30.1 238.4 %recurrence_forward.1 = (bf16[48,16,2048]{2,1,0:T(8,128)(2,1)}, bf16[24,16,2048]{2,1,0:T(8,128)(2,1)}, f32[48,4,16,512]{3,2,1,0:T(8,128)}, f32[24,4,16,512]{3,2,...) custom-call(bf16[48,16,128]{2,1,0:T(8,128)(2,1)} %fusion.28.x_front, ...), custom_call_target="tpu_custom_call" | custom-call | tf_op jit(solution)/shard_map/recurrence_forward/pallas_call | solution.py:156
  268.4 2.7 slice.73
  271.2 3.9 slice.72
  275.2 2.7 fusion.56
  278.0 0.8 convert_reduce_fusion.3
  278.8 0.9 copy.119
  279.7 2.1 convolution_bitcast_fusion.2
  281.8 2.4 fusion.55
  284.3 0.9 convert_reduce_fusion.2
  285.3 2.4 convolution_bitcast_fusion.3
  288.0 1.2 fusion.39.dec_back
  289.3 1.7 fusion.40.dec_front
  291.0 269.6 %recurrence_backward.1 = (bf16[48,16,2048]{2,1,0:T(8,128)(2,1)}, bf16[24,16,2048]{2,1,0:T(8,128)(2,1)}) custom-call(f32[48,4,16,512]{3,2,1,0:T(8,128)} %get-tuple-element.14.acts_front, f32[24,4,16,512]{3,2,1,0:T(8,128)} %get-tuple-element.15.acts_back, f32[48,16,512]{2,1,0:T(8,128)} %get-tuple-element.16.cell_front, ...), custom_call_target="tpu_custom_call" | custom-call | tf_op jit(solution)/shard_map/recurrence_backward/pallas_call | solution.py:305
  560.6 4.0 reshape.134
  565.1 0.7 copy-done.5
  565.7 0.5 copy-done.9
  566.3 2.1 fusion.31
  568.3 0.7 convolution_bitcast_fusion.5
  569.1 6.1 reshape.133
  575.2 5.4 fusion.23
  580.7 2.0 fusion.17
  582.7 1.2 convolution_bitcast_fusion.4
  583.9 0.7 pad_maximum_fusion.3
  584.7 1.4 pad_maximum_fusion.1
  586.1 1.1 copy-done.1
  587.2 12.4 %convolution_bitcast_fusion.1 = f32[1,4,2048,512]{2,3,1,0:T(8,128)} fusion(bf16[48,2,4,8,512]{4,3,2,1,0:T(8,128)(2,1)S(1)} %bitcast.125, bf16[47,16,2048]{2,1,0:T(8,128)(2,1)} %slice.72), kind=kOutput, calls=%fused_computation.2 | convolution fusion | flops 6442450944 | bytes 23003136 | tf_op jit(solution)/shard_map/tbk,tbgn->gkn/dot_general | solution.py:404
  599.7 1.1 pad_maximum_fusion.2
  600.8 1.3 copy-done.10
  602.2 4.6 convolution_bitcast_fusion
  606.7 18.5 %pad_maximum_fusion = f32[2,4,2048,512]{2,3,1,0:T(8,128)} fusion(f32[1,4,2048,512]{2,3,1,0:T(8,128)S(1)} %convolution_bitcast_fusion, f32[1,4,2048,512]{2,3,1,0:T(8,128)} %convolution_bitcast_fusion.1), kind=kLoop, calls=%fused_computation | loop fusion | flops 8388608 | bytes 67108864 | tf_op jit(solution)/shard_map/stack | solution.py:411
  625.3 0.7 copy-done.17
  626.0 2.4 convert_reduce_fusion
  628.7 22.9 %all-reduce.4 = (f32[2,4,512]{2,1,0:T(4,128)}, f32[2,275]{1,0:T(2,128)}) all-reduce(f32[2,4,512]{2,1,0:T(4,128)S(1)} %pad_maximum_fusion.4, f32[2,275]{1,0:T(2,128)S(1)} %pad_maximum_fusion.5), channel_id=1, replica_groups=mesh['rep'=8,'shard'=4] {'rep'}, use_global_device_ids=true, to_apply=%region_11.12 | all-reduce | flops 4646 | bytes 37168 | tf_op jit(solution)/shard_map/psum | solution.py:441
  651.6 59.2 %all-reduce.9.cloned.1.call-done = f32[2,275,100]{2,1,0:T(8,128)} async-done(((f32[2,275,100]{2,1,0:T(8,128)}), f32[2,275,100]{2,1,0:T(8,128)}) %all-reduce.9.cloned.1.call-update) | async-done | bytes 220016 | tf_op jit(solution)/shard_map/psum | solution.py:442
  710.8 1.8 copy.130
  712.6 70.6 %all-reduce.11.cloned.1.call-done = (f32[2,4,100,512]{3,2,1,0:T(8,128)}, f32[2,512,275]{1,2,0:T(8,128)}) async-done(((f32[2,4,100,512]{3,2,1,0:T(8,128)}, f32[2,512,275]{1,2,0:T(8,128)}), (f32[2,4,100,512]{3,2,1,0:T(8,128)}, f32[2,512,275]{1,2,0:T(8,128)})) %all-reduce.11.cloned.1.call-update) | async-done | bytes 2764816 | tf_op jit(solution)/shard_map/psum | solution.py:441
  783.2 3.8 copy.131
  787.0 1.9 copy.133
  788.8 203.0 %reduce-scatter.2.cloned.1.call-done = f32[2,4,256,512]{2,3,1,0:T(8,128)} async-done(((f32[2,4,2048,512]{2,3,1,0:T(8,128)}), f32[2,4,256,512]{2,3,1,0:T(8,128)}) %reduce-scatter.2.cloned.1.call-update) | async-done | bytes 4194320 | tf_op jit(solution)/shard_map/reduce_scatter | solution.py:410
  991.8 5.2 copy.132
  (81 shorter events, 3.3 us)
Async XLA Ops:
  7.2 2.2 copy-start.22
  7.2 2.3 copy-start.21
  7.2 16.5 %copy-start.19 = (bf16[2,4,512]{2,1,0:T(4,128)(2,1)S(1)}, bf16[2,4,512]{2,1,0:T(4,128)(2,1)}, u32[]{:S(2)}) copy-start(bf16[2,4,512]{2,1,0:T(4,128)(2,1)} %param.13) | copy-start | bytes 24580
  7.2 18.4 %copy-start.16 = (bf16[2,275,100]{2,0,1:T(2,128)(2,1)S(1)}, bf16[2,275,100]{2,0,1:T(2,128)(2,1)}, u32[]{:S(2)}) copy-start(bf16[2,275,100]{2,0,1:T(2,128)(2,1)} %param.10) | copy-start | bytes 330004
  7.2 18.4 %copy-start.13 = (bf16[2,4,100,512]{3,1,2,0:T(4,128)(2,1)S(1)}, bf16[2,4,100,512]{3,1,2,0:T(4,128)(2,1)}, u32[]{:S(2)}) copy-start(bf16[2,4,100,512]{3,1,2,0:T(4,128)(2,1)} %param.11) | copy-start | bytes 2457604
  7.2 267.9 %all-gather.3.cloned.1.call-start = ((), (), s32[]{:S(2)}) async-start(), calls=%async_computation.1 | async-start | bytes 2867200 | tf_op jit(solution)/shard_map/all_gather | solution.py:344
  9.3 701.5 %all-reduce.9.cloned.1.call-start = ((), (), s32[]{:S(2)}) async-start(), calls=%async_computation.2 | async-start | bytes 573440 | tf_op jit(solution)/shard_map/psum | solution.py:442
  25.8 0.9 copy-start.4
  271.2 3.9 copy-start.20
  275.2 6.6 copy-start.3
  285.3 2.8 copy-start.2
  285.3 2.8 copy-start.11
  560.6 4.0 copy-start
  560.6 4.0 copy-start.14
  564.6 1.2 copy-start.5
  564.6 1.7 copy-start.9
  575.2 5.4 copy-start.6
  575.2 5.5 copy-start.15
  584.7 198.5 %all-reduce.11.cloned.1.call-start = ((), (), s32[]{:S(2)}) async-start(), calls=%async_computation.4 | async-start | bytes 5701632 | tf_op jit(solution)/shard_map/psum | solution.py:441
  584.7 2.5 copy-start.1
  587.2 12.5 %copy-start.7 = (f32[1,512,275]{1,2,0:T(8,128)S(1)}, f32[1,512,275]{1,2,0:T(8,128)}, u32[]{:S(2)}) copy-start(f32[1,512,275]{1,2,0:T(8,128)} %convolution_bitcast_fusion.2) | copy-start | bytes 1689604
  587.2 12.5 %copy-start.8 = (f32[1,512,275]{1,2,0:T(8,128)S(1)}, f32[1,512,275]{1,2,0:T(8,128)}, u32[]{:S(2)}) copy-start(f32[1,512,275]{1,2,0:T(8,128)} %convolution_bitcast_fusion.3) | copy-start | bytes 1689604
  600.8 1.4 copy-start.10
  600.8 391.0 %reduce-scatter.2.cloned.1.call-start = ((), (), s32[]{:S(2)}) async-start(), calls=%async_computation.3 | async-start | bytes 37748736 | tf_op jit(solution)/shard_map/reduce_scatter | solution.py:410
  625.3 0.7 copy-start.17
  625.3 0.7 copy-start.18
  783.2 3.8 copy-start.12
Sparse Core Ops, SparseCore 0:
  10.2 76.5 all-gather.2
  584.8 125.9 all-reduce.8
  715.2 67.9 all-reduce.10
  786.6 205.1 reduce-scatter.1

commit v2 on v1

v2 whole, which is shorter than its diff:
```python
import functools
import math
import types

import jax
import jax.numpy as jnp
from jax import lax
from jax.experimental import pallas as pl
from jax.experimental.pallas import tpu as pltpu
from jax.sharding import PartitionSpec as P

PRECISE = lax.Precision.HIGHEST
MESH = pl.DeviceIdType.MESH
LANES = 128
MIB = 1 << 20
B16 = jnp.bfloat16
F32 = jnp.float32
VMEM = pl.BlockSpec(memory_space=pltpu.VMEM)
ANYWHERE = pl.BlockSpec(memory_space=pl.ANY)


def one_hot(ids, width, out_type):
    return (ids[..., None] == jnp.arange(width, dtype=jnp.int32)).astype(out_type)


def loss_grad(logits, targets, active, factor):
    probabilities = jax.nn.softmax(logits, axis=-1)
    picked = one_hot(targets, logits.shape[-1], F32)
    return ((probabilities - picked) * (active * factor)[:, None]).astype(B16)


def peers_of(place, count):
    if count == 4:
        return [place + 1 - 2 * lax.rem(place, 2), lax.rem(place + 2, 4), 3 - place]
    if count == 2:
        return [1 - place]
    assert count == 1
    return []


def others_of(group, groups):
    return [lax.rem(group + j, groups) for j in range(1, groups)]


def greet(peers, others):
    barrier = pltpu.get_barrier_semaphore()
    for peer in peers:
        pl.semaphore_signal(barrier, inc=1, device_id={"shard": peer}, device_id_type=MESH)
    for other in others:
        pl.semaphore_signal(barrier, inc=1, device_id={"rep": other}, device_id_type=MESH)
    pl.semaphore_wait(barrier, len(peers) + len(others))


def span(index, size):
    return pl.ds(pl.multiple_of(index * size, size), size)


def dot(left, right):
    return jnp.dot(left, right, preferred_element_type=F32)


def dot_last(left, right):
    return lax.dot_general(left, right, (((1,), (1,)), ((), ())), preferred_element_type=F32)


def dot_first(left, right):
    return lax.dot_general(left, right, (((0,), (0,)), ((), ())), preferred_element_type=F32)


def column_of(ids, spot):
    lane = lax.broadcasted_iota(jnp.int32, ids.shape, 1)
    return jnp.sum(jnp.where(lane == spot, ids, 0), axis=1, keepdims=True)


def marks(column, width):
    lane = lax.broadcasted_iota(jnp.int32, (column.shape[0], width), 1)
    return (lane == column).astype(F32).astype(B16)


def id_column(ids, ends, m, t):
    return column_of(ids, t) if m == 0 else column_of(ids, jnp.maximum(ends - 1 - t, 0))


def split_three(value):
    first = value.astype(B16)
    rest = value - first.astype(F32)
    second = rest.astype(B16)
    return first, second, (rest - second.astype(F32)).astype(B16)


def call(body, name, ins, outs, scratch, collective_id, cost):
    names = [key for key, _, _ in ins] + [key for key, _, _, _ in outs] + [key for key, _ in scratch]

    def kernel(*refs):
        body(types.SimpleNamespace(**dict(zip(names, refs))))

    results = pl.pallas_call(
        kernel,
        out_shape=tuple(jax.ShapeDtypeStruct(shape, kind) for _, shape, kind, _ in outs),
        in_specs=[spec for _, _, spec in ins],
        out_specs=tuple(spec for _, _, _, spec in outs),
        scratch_shapes=[kind for _, kind in scratch],
        compiler_params=pltpu.CompilerParams(
            collective_id=collective_id, has_side_effects=True, vmem_limit_bytes=60 * MIB
        ),
        cost_estimate=pl.CostEstimate(flops=cost, bytes_accessed=50 * MIB, transcendentals=0),
        name=name,
    )(*[value for _, value, _ in ins])
    return types.SimpleNamespace(**dict(zip([key for key, _, _, _ in outs], results)))


def forward_body(count, groups, stream, length, r):
    place = lax.axis_index("shard")
    group = lax.axis_index("rep")
    peers = peers_of(place, count)
    others = others_of(group, groups) if stream else []
    units = r.weights.shape[3]
    half_len = length // 2
    seq_dev = r.own_ids.shape[0]
    loads = [pltpu.make_async_copy(r.w_rec.at[m], r.weights.at[m], r.load_sem.at[m]) for m in range(2)]
    for load in loads:
        load.start()
    r.id_blocks[group, place, :seq_dev] = r.own_ids[...]
    greet(peers, others)

    def id_copy(k):
        block = r.id_blocks.at[group, place]
        return pltpu.make_async_remote_copy(
            src_ref=block,
            dst_ref=block,
            send_sem=r.id_send.at[k],
            recv_sem=r.id_recv.at[k],
            device_id={"shard": peers[k]},
            device_id_type=MESH,
        )

    def id_spread(j, source):
        return pltpu.make_async_remote_copy(
            src_ref=r.id_blocks.at[group],
            dst_ref=r.id_blocks.at[source],
            send_sem=r.ids_send.at[j],
            recv_sem=r.ids_recv.at[j],
            device_id={"rep": others[j]},
            device_id_type=MESH,
        )

    for k in range(len(peers)):
        id_copy(k).start()
    fulls = (r.full_front, r.full_back)
    acts = (r.acts_front, r.acts_back)
    cells = (r.cell_front, r.cell_back)
    if stream:
        pasts = (r.past_front, r.past_back)
        wide = r.past_front.shape[3]
        r.blank[...] = jnp.zeros_like(r.blank)
        blanks = [pltpu.make_async_copy(r.blank, pasts[m].at[0], r.past_local.at[m]) for m in range(2)]
        for copy in blanks:
            copy.start()

    def spread(m, t):
        if not stream:
            return
        for j, other in enumerate(others):
            pltpu.make_async_remote_copy(
                src_ref=fulls[m].at[t, :, span(other // 2, wide)],
                dst_ref=pasts[m].at[t + 1, group],
                send_sem=r.past_send.at[m, j],
                recv_sem=r.past_recv.at[m, j],
                device_id={"rep": other},
                device_id_type=MESH,
            ).start()
        pltpu.make_async_copy(
            fulls[m].at[t, :, span(group // 2, wide)], pasts[m].at[t + 1, group], r.past_local.at[m]
        ).start()

    def finish_spread(m, steps):
        if not stream:
            return
        for j, other in enumerate(others):
            whole = pltpu.make_async_remote_copy(
                src_ref=pasts[m].at[pl.ds(1, steps), 0],
                dst_ref=pasts[m].at[pl.ds(1, steps), 0],
                send_sem=r.past_send.at[m, j],
                recv_sem=r.past_recv.at[m, j],
                device_id={"rep": other},
                device_id_type=MESH,
            )
            whole.wait_send()
            whole.wait_recv()
        mine = pasts[m].at[pl.ds(1, steps), 0]
        pltpu.make_async_copy(mine, mine, r.past_local.at[m]).wait()

    def exchange(m, t, k):
        slot = lax.rem(t, 2)
        own = fulls[m].at[t, :, span(place, units)]
        return pltpu.make_async_remote_copy(
            src_ref=own,
            dst_ref=own,
            send_sem=r.send_sem.at[m, slot, k],
            recv_sem=r.recv_sem.at[m, slot, k],
            device_id={"shard": peers[k]},
            device_id_type=MESH,
        )

    def finish(m, t, sums, memory):
        in_gate = jax.nn.sigmoid(sums[0])
        forget = jax.nn.sigmoid(sums[1])
        candidate = jnp.tanh(sums[2])
        out_gate = jax.nn.sigmoid(sums[3])
        new_memory = in_gate * candidate if memory is None else forget * memory + in_gate * candidate
        fulls[m][t, :, span(place, units)] = (out_gate * jnp.tanh(new_memory)).astype(B16)
        for k in reversed(range(len(peers))):
            exchange(m, t, k).start()
        for g, value in enumerate((in_gate, forget, candidate, out_gate)):
            acts[m][t, g] = value
        cells[m][t] = new_memory

    def start_sums(m, t):
        ids, ends = r.group_ids[...], r.group_ids[:, length : length + 1]
        spots = marks(id_column(ids, ends, m, t), r.table.shape[1])
        x_t = dot(spots, r.table[m]).astype(B16)
        return [r.bias[m, g : g + 1] + dot(x_t, r.w_in[m, g]) for g in range(4)]

    def add_chunk(m, t, owner, sums):
        part = fulls[m][t, :, span(owner, units)]
        return [sums[g] + dot(part, r.weights[m, g, span(owner, units), :]) for g in range(4)]

    def advance(m, t):
        sums = add_chunk(m, t - 1, place, start_sums(m, t))
        for k in range(len(peers)):
            exchange(m, t - 1, k).wait_recv()
            sums = add_chunk(m, t - 1, peers[k], sums)
        for k in range(len(peers)):
            exchange(m, t - 1, k).wait_send()
        finish(m, t, sums, cells[m][t - 1])
        spread(m, t - 1)

    def turn_copy(slot, m, g, p):
        return pltpu.make_async_copy(
            r.turned.at[slot],
            r.w_turned.at[m, span(g, units), span(p, units)],
            r.turn_sem.at[slot],
        )

    blocks = 8 * count

    def turn(block, slot):
        m, g, p = block // (4 * count), lax.rem(block // count, 4), lax.rem(block, count)

        @pl.when(block < blocks)
        def _():
            @pl.when(block >= 2)
            def _():
                turn_copy(slot, 0, 0, 0).wait()

            r.turned[slot] = r.weights[m, g, span(p, units), :].T
            turn_copy(slot, m, g, p).start()

    for k in range(len(peers)):
        id_copy(k).wait_send()
        id_copy(k).wait_recv()
    for s in range(count):
        r.group_ids[s * seq_dev : (s + 1) * seq_dev] = r.id_blocks[group, s, :seq_dev]
    for j in range(len(others)):
        id_spread(j, group).start()
    if stream:
        for copy in blanks:
            copy.wait()
    finish(0, 0, start_sums(0, 0), None)
    finish(1, 0, start_sums(1, 0), None)
    for load in loads:
        load.wait()

    def both(t, carry):
        advance(0, t)
        advance(1, t)
        return carry

    def front_only(t, carry):
        advance(0, t)
        turn(2 * (t - half_len), 0)
        turn(2 * (t - half_len) + 1, 1)
        return carry

    assert blocks <= 2 * (length - half_len)
    lax.fori_loop(1, half_len, both, 0)
    lax.fori_loop(half_len, length, front_only, 0)
    for m, end in ((0, length), (1, half_len)):
        for k in range(len(peers)):
            copy = exchange(m, end - 1, k)
            copy.wait_send()
            copy.wait_recv()
    for slot in range(2):
        turn_copy(slot, 0, 0, 0).wait()
    finish_spread(0, length - 1)
    finish_spread(1, half_len - 1)
    for j in range(len(others)):
        copy = id_spread(j, group)
        copy.wait_send()
        copy.wait_recv()
    if stream:
        r.every_ids[...] = r.id_blocks[:, :, :seq_dev].reshape(r.every_ids.shape)


def run_forward(count, groups, stream, length, own_ids, table, w_in, bias, w_rec):
    half_len = length // 2
    units, shard_units = w_rec.shape[2:]
    seq_dev = own_ids.shape[0]
    rows = seq_dev * count
    dma = pltpu.SemaphoreType.DMA
    links = max(count - 1, 1)
    ins = [
        ("own_ids", own_ids, VMEM),
        ("table", table, VMEM),
        ("w_in", w_in, VMEM),
        ("bias", bias, VMEM),
        ("w_rec", w_rec, ANYWHERE),
    ]
    outs = [
        ("full_front", (length, rows, units), B16, VMEM),
        ("full_back", (half_len, rows, units), B16, VMEM),
        ("acts_front", (length, 4, rows, shard_units), F32, VMEM),
        ("acts_back", (half_len, 4, rows, shard_units), F32, VMEM),
        ("cell_front", (length, rows, shard_units), F32, VMEM),
        ("cell_back", (half_len, rows, shard_units), F32, VMEM),
        ("group_ids", (rows, LANES), jnp.int32, VMEM),
        ("w_turned", (2, 4 * shard_units, units), B16, ANYWHERE),
    ]
    scratch = [
        ("weights", pltpu.VMEM(w_rec.shape, B16)),
        ("turned", pltpu.VMEM((2, shard_units, shard_units), B16)),
        ("id_blocks", pltpu.VMEM((groups, count, max(8, seq_dev), LANES), jnp.int32)),
        ("load_sem", dma((2,))),
        ("turn_sem", dma((2,))),
        ("send_sem", dma((2, 2, links))),
        ("recv_sem", dma((2, 2, links))),
        ("id_send", dma((links,))),
        ("id_recv", dma((links,))),
    ]
    if stream:
        wide = units // (groups // 2)
        outs += [
            ("past_front", (length, groups, rows, wide), B16, ANYWHERE),
            ("past_back", (half_len, groups, rows, wide), B16, ANYWHERE),
            ("every_ids", (groups * rows, LANES), jnp.int32, VMEM),
        ]
        scratch += [
            ("blank", pltpu.VMEM((groups, rows, wide), B16)),
            ("past_send", dma((2, groups - 1))),
            ("past_recv", dma((2, groups - 1))),
            ("past_local", dma((2,))),
            ("ids_send", dma((groups - 1,))),
            ("ids_recv", dma((groups - 1,))),
        ]
    body = functools.partial(forward_body, count, groups, stream, length)
    return call(body, "recurrence_forward", ins, outs, scratch, 0, 10**11)


def backward_body(count, groups, stream, r):
    place = lax.axis_index("shard")
    group = lax.axis_index("rep")
    core = lax.rem(group, 2)
    peers = peers_of(place, count)
    others = others_of(group, groups) if stream else []
    units = r.cell_front.shape[2]
    length, half_len = r.cell_front.shape[0], r.cell_back.shape[0]
    loads = [pltpu.make_async_copy(r.w_turned.at[m], r.weights.at[m], r.load_sem.at[m]) for m in range(2)]
    for load in loads:
        load.start()
    acts = (r.acts_front, r.acts_back)
    cells = (r.cell_front, r.cell_back)
    decs = (r.dec_front, r.dec_back)
    gates = (r.gates_front, r.gates_back)
    ends = (length, half_len)
    if stream:
        r.sums[...] = jnp.zeros_like(r.sums)
        r.rec_sums[...] = jnp.zeros_like(r.rec_sums)
        wides = (r.wide_front, r.wide_back)
        pasts = (r.past_front, r.past_back)
    greet(peers, others)

    def wide_copy(m, t, j):
        other = others[j]
        return pltpu.make_async_remote_copy(
            src_ref=gates[m].at[t, :, span(lax.rem(other, 2), 2 * units)],
            dst_ref=wides[m].at[t, group],
            send_sem=r.wide_send.at[m, j],
            recv_sem=r.wide_recv.at[m, t // 2],
            device_id={"rep": other},
            device_id_type=MESH,
        )

    def spread(m, t):
        if not stream:
            return
        for j in range(len(others)):
            wide_copy(m, t, j).start()
        pltpu.make_async_copy(
            gates[m].at[t, :, span(core, 2 * units)], wides[m].at[t, group], r.wide_local.at[m, t // 2]
        ).start()

    def arrive(m, pair):
        far = wides[m].at[pl.ds(2 * pair, 2), pl.ds(0, groups - 1)]
        pltpu.make_async_remote_copy(
            src_ref=far,
            dst_ref=far,
            send_sem=r.wide_send.at[m, 0],
            recv_sem=r.wide_recv.at[m, pair],
            device_id={"rep": others[0]},
            device_id_type=MESH,
        ).wait_recv()
        near = wides[m].at[pl.ds(2 * pair, 2), 0]
        pltpu.make_async_copy(near, near, r.wide_local.at[m, pair]).wait()

    def fetches(m, pair):
        slot = lax.rem(pair, 2)
        return (
            pltpu.make_async_copy(
                wides[m].at[pl.ds(2 * pair, 2)], r.wide_slot.at[m, slot], r.fetch_sem.at[m, slot, 0]
            ),
            pltpu.make_async_copy(
                pasts[m].at[pl.ds(2 * pair, 2)], r.past_slot.at[m, slot], r.fetch_sem.at[m, slot, 1]
            ),
        )

    def fetch(m, pair):
        arrive(m, pair)
        for copy in fetches(m, pair):
            copy.start()

    def accumulate(m, pair):
        slot = lax.rem(pair, 2)
        for copy in fetches(m, pair):
            copy.wait()
        dz = r.wide_slot[m, slot].reshape(-1, 2 * units)
        past = r.past_slot[m, slot].reshape(dz.shape[0], -1)
        r.rec_sums[m] += dot_first(past, dz)
        ids, stops = r.every_ids[...], r.every_ids[:, length : length + 1]
        spots = [marks(id_column(ids, stops, m, 2 * pair + i), r.sums.shape[1]) for i in range(2)]
        r.sums[m] += dot_first(jnp.concatenate(spots, axis=0), dz)

    def exchange(m, t, k):
        slot = lax.rem(t, 2)
        return pltpu.make_async_remote_copy(
            src_ref=r.outbox.at[m, slot, k],
            dst_ref=r.inbox.at[m, slot, k],
            send_sem=r.send_sem.at[m, slot, k],
            recv_sem=r.recv_sem.at[m, slot, k],
            device_id={"shard": peers[k]},
            device_id_type=MESH,
        )

    def gate_grads(m, t, grad_hidden, carried, prev_memory):
        in_gate, forget, candidate, out_gate = (acts[m][t, g] for g in range(4))
        squashed = jnp.tanh(cells[m][t])
        grad_memory = grad_hidden * out_gate * (1.0 - squashed * squashed)
        if carried is not None:
            grad_memory = carried + grad_memory
        r.cell_grad[m] = grad_memory * forget
        forget_part = jnp.zeros_like(grad_memory)
        if prev_memory is not None:
            forget_part = grad_memory * prev_memory * forget * (1.0 - forget)
        values = (
            grad_memory * candidate * in_gate * (1.0 - in_gate),
            forget_part,
            grad_memory * in_gate * (1.0 - candidate * candidate),
            grad_hidden * squashed * out_gate * (1.0 - out_gate),
        )
        for g, value in enumerate(values):
            gates[m][t, :, g * units : (g + 1) * units] = value.astype(B16)

    def product(m, t, owner):
        return dot(gates[m][t], r.weights[m, :, span(owner, units)])

    def send_products(m, t):
        for k in reversed(range(len(peers))):
            r.outbox[m, lax.rem(t, 2), k] = product(m, t, peers[k])
            exchange(m, t, k).start()
        r.own_part[m] = product(m, t, place)
        spread(m, t)

    def incoming(m, t):
        total = decs[m][t - 1] + r.own_part[m]
        for k in range(len(peers)):
            exchange(m, t, k).wait_recv()
            total = total + r.inbox[m, lax.rem(t, 2), k]
        for k in range(len(peers)):
            exchange(m, t, k).wait_send()
        return total

    def retreat(m, t):
        gate_grads(m, t, incoming(m, t + 1), r.cell_grad[m], cells[m][t - 1])
        send_products(m, t)

    def first(m):
        t = ends[m] - 1
        gate_grads(m, t, decs[m][t], None, cells[m][t - 1])
        loads[m].wait()
        send_products(m, t)

    def last(m):
        gate_grads(m, 0, incoming(m, 1), r.cell_grad[m], None)
        spread(m, 0)

    def lagged(work, m, step):
        if not stream:
            return
        pairs = ends[m] // 2

        @pl.when(jnp.logical_and(step >= 2, step < pairs + 2))
        def _():
            work(m, pairs + 1 - step)

    first(0)
    first(1)
    retreat(0, length - 2)
    retreat(1, half_len - 2)

    def both(step, carry):
        retreat(0, length - 1 - 2 * step)
        lagged(fetch, 0, step)
        retreat(1, half_len - 1 - 2 * step)
        lagged(fetch, 1, step)
        retreat(0, length - 2 - 2 * step)
        lagged(accumulate, 0, step)
        retreat(1, half_len - 2 - 2 * step)
        lagged(accumulate, 1, step)
        return carry

    def front_only(step, carry):
        retreat(0, length - 1 - 2 * step)
        lagged(fetch, 0, step)
        lagged(fetch, 1, step)
        retreat(0, length - 2 - 2 * step)
        lagged(accumulate, 0, step)
        lagged(accumulate, 1, step)
        return carry

    assert half_len % 2 == 0 and length == 2 * half_len
    turns = half_len // 2
    lax.fori_loop(1, turns - 1, both, 0)
    retreat(0, length - 1 - 2 * (turns - 1))
    lagged(fetch, 0, turns - 1)
    retreat(1, 1)
    lagged(fetch, 1, turns - 1)
    retreat(0, length - 2 * turns)
    lagged(accumulate, 0, turns - 1)
    last(1)
    lagged(accumulate, 1, turns - 1)
    lax.fori_loop(turns, 2 * turns - 1, front_only, 0)
    retreat(0, 1)
    lagged(fetch, 0, 2 * turns - 1)
    last(0)
    lagged(accumulate, 0, 2 * turns - 1)
    if not stream:
        return
    lagged(fetch, 0, 2 * turns)
    lagged(accumulate, 0, 2 * turns)
    lagged(fetch, 0, 2 * turns + 1)
    lagged(accumulate, 0, 2 * turns + 1)
    for m in range(2):
        for j, other in enumerate(others):
            part = wides[m].at[:, 0]
            pltpu.make_async_remote_copy(
                src_ref=part,
                dst_ref=part,
                send_sem=r.wide_send.at[m, j],
                recv_sem=r.wide_recv.at[m, 0],
                device_id={"rep": other},
                device_id_type=MESH,
            ).wait_send()
    sibling = group + 1 - 2 * core
    depth = r.rec_grad.shape[2]

    def swap(m, g, which, src, dst, sem):
        return (
            pltpu.make_async_remote_copy(
                src_ref=src(m, g, 1 - core),
                dst_ref=dst.at[m, 2 * core + g],
                send_sem=r.swap_send.at[which, m, g],
                recv_sem=r.swap_recv.at[which, m, g],
                device_id={"rep": sibling},
                device_id_type=MESH,
            ),
            pltpu.make_async_copy(
                src(m, g, core), dst.at[m, 2 * core + g], r.swap_local.at[which, m, g]
            ),
        )

    def rec_part(m, g, owner):
        return r.rec_sums.at[m, span(owner, depth), pl.ds(g * units, units)]

    def in_part(m, g, owner):
        return r.in_sums.at[m, g]

    swaps = []
    for m in range(2):
        for g in range(2):
            swaps += swap(m, g, 0, rec_part, r.rec_grad, None)
    for copy in swaps:
        copy.start()
    for m in range(2):
        embed_part = None
        in_sum = None
        for part in split_three(r.sums[m]):
            in_term = dot_first(r.table[m], part)
            embed_term = sum(
                dot_last(part[:, g * units : (g + 1) * units], r.w_pair[m, g]) for g in range(2)
            )
            in_sum = in_term if in_sum is None else in_sum + in_term
            embed_part = embed_term if embed_part is None else embed_part + embed_term
        for g in range(2):
            r.in_sums[m, g] = in_sum[:, g * units : (g + 1) * units]
        r.embed_part[m] = embed_part
    more = []
    for m in range(2):
        for g in range(2):
            more += swap(m, g, 1, in_part, r.in_grad, None)
    for copy in more:
        copy.start()
    rows = r.embed_half.shape[1]
    piece = rows // count

    def embed_swap(source, target, which, owner):
        return pltpu.make_async_remote_copy(
            src_ref=source.at[:, span(owner, rows)],
            dst_ref=target,
            send_sem=r.embed_send.at[which],
            recv_sem=r.embed_recv.at[which],
            device_id={"rep": sibling},
            device_id_type=MESH,
        )

    copy = embed_swap(r.embed_part, r.embed_half, 0, 1 - core)
    copy.start()
    copy.wait()
    r.embed_half[...] += r.embed_part[:, span(core, rows)]

    def embed_reduce(k):
        return pltpu.make_async_remote_copy(
            src_ref=r.embed_half.at[:, span(peers[k], piece)],
            dst_ref=r.embed_inbox.at[k],
            send_sem=r.reduce_send.at[k],
            recv_sem=r.reduce_recv.at[k],
            device_id={"shard": peers[k]},
            device_id_type=MESH,
        )

    def embed_gather(k):
        own = r.embed_full.at[:, pl.ds(pl.multiple_of(core * rows + place * piece, 8), piece)]
        return pltpu.make_async_remote_copy(
            src_ref=own,
            dst_ref=own,
            send_sem=r.gather_send.at[k],
            recv_sem=r.gather_recv.at[k],
            device_id={"shard": peers[k]},
            device_id_type=MESH,
        )

    for k in reversed(range(len(peers))):
        embed_reduce(k).start()
    total = r.embed_half[:, span(place, piece)]
    for k in range(len(peers)):
        embed_reduce(k).wait()
        total = total + r.embed_inbox[k]
    r.embed_full[:, pl.ds(pl.multiple_of(core * rows + place * piece, 8), piece)] = total
    for k in reversed(range(len(peers))):
        embed_gather(k).start()
    for k in range(len(peers)):
        embed_gather(k).wait()
    copy = pltpu.make_async_remote_copy(
        src_ref=r.embed_full.at[:, span(core, rows)],
        dst_ref=r.embed_full.at[:, span(core, rows)],
        send_sem=r.embed_send.at[1],
        recv_sem=r.embed_recv.at[1],
        device_id={"rep": sibling},
        device_id_type=MESH,
    )
    copy.start()
    copy.wait()
    for copy in swaps + more:
        copy.wait()


def run_backward(count, groups, stream, ran, decs, table, w_pair):
    length, rows, shard_units = ran.cell_front.shape
    half_len = ran.cell_back.shape[0]
    units = ran.w_turned.shape[2]
    links = max(count - 1, 1)
    dma = pltpu.SemaphoreType.DMA
    box = (2, 2, links, rows, shard_units)
    ins = [
        ("acts_front", ran.acts_front, VMEM),
        ("acts_back", ran.acts_back, VMEM),
        ("cell_front", ran.cell_front, VMEM),
        ("cell_back", ran.cell_back, VMEM),
        ("dec_front", decs[0], VMEM),
        ("dec_back", decs[1], VMEM),
        ("w_turned", ran.w_turned, ANYWHERE),
    ]
    gates = [
        ("gates_front", (length, rows, 4 * shard_units)),
        ("gates_back", (half_len, rows, 4 * shard_units)),
    ]
    scratch = [
        ("weights", pltpu.VMEM(ran.w_turned.shape, B16)),
        ("outbox", pltpu.VMEM(box, F32)),
        ("inbox", pltpu.VMEM(box, F32)),
        ("own_part", pltpu.VMEM((2, rows, shard_units), F32)),
        ("cell_grad", pltpu.VMEM((2, rows, shard_units), F32)),
        ("load_sem", dma((2,))),
        ("send_sem", dma(box[:3])),
        ("recv_sem", dma(box[:3])),
    ]
    if stream:
        wide = ran.past_front.shape[3]
        vocab, depth = table.shape[1:]
        reduced = -(-vocab // (16 * count)) * 8 * count
        padded = 2 * reduced
        table = jnp.pad(table, ((0, 0), (0, padded - vocab), (0, 0)))
        ins += [
            ("past_front", ran.past_front, ANYWHERE),
            ("past_back", ran.past_back, ANYWHERE),
            ("every_ids", ran.every_ids, VMEM),
            ("table", table, VMEM),
            ("w_pair", w_pair, VMEM),
        ]
        outs = [
            ("wide_front", (length, groups, rows, 2 * shard_units), B16, ANYWHERE),
            ("wide_back", (half_len, groups, rows, 2 * shard_units), B16, ANYWHERE),
            ("rec_grad", (2, 4, wide // 2, shard_units), F32, ANYWHERE),
            ("in_grad", (2, 4, depth, shard_units), F32, ANYWHERE),
            ("embed_full", (2, padded, depth), F32, VMEM),
        ]
        scratch += [(key, pltpu.VMEM(shape, B16)) for key, shape in gates]
        scratch += [
            ("sums", pltpu.VMEM((2, padded, 2 * shard_units), F32)),
            ("rec_sums", pltpu.VMEM((2, wide, 2 * shard_units), F32)),
            ("in_sums", pltpu.VMEM((2, 2, depth, shard_units), F32)),
            ("embed_part", pltpu.VMEM((2, padded, depth), F32)),
            ("embed_half", pltpu.VMEM((2, reduced, depth), F32)),
            ("embed_inbox", pltpu.VMEM((links, 2, reduced // count, depth), F32)),
            ("wide_slot", pltpu.VMEM((2, 2, 2, groups, rows, 2 * shard_units), B16)),
            ("past_slot", pltpu.VMEM((2, 2, 2, groups, rows, wide), B16)),
            ("wide_send", dma((2, groups - 1))),
            ("wide_recv", dma((2, length // 2))),
            ("wide_local", dma((2, length // 2))),
            ("fetch_sem", dma((2, 2, 2))),
            ("swap_send", dma((2, 2, 2))),
            ("swap_recv", dma((2, 2, 2))),
            ("swap_local", dma((2, 2, 2))),
            ("embed_send", dma((2,))),
            ("embed_recv", dma((2,))),
            ("reduce_send", dma((links,))),
            ("reduce_recv", dma((links,))),
            ("gather_send", dma((links,))),
            ("gather_recv", dma((links,))),
        ]
    else:
        outs = [(key, shape, B16, VMEM) for key, shape in gates]
    body = functools.partial(backward_body, count, groups, stream)
    return call(body, "recurrence_backward", ins, outs, scratch, 1, 10**11)


def shifted(values):
    return jnp.concatenate([jnp.zeros_like(values[:1]), values[:-1]], axis=0)


def reduced_grads(ran, gates, embedding, w_in, ids, group_size):
    embed = embedding.shape[2]

    def per_model(full, grads, ids, m):
        grads = grads.reshape(grads.shape[0], group_size, 4, -1)
        rec = jnp.einsum("tbk,tbgn->gkn", shifted(full), grads, preferred_element_type=F32)
        spots = one_hot(ids, embedding.shape[1], B16)
        x = jnp.einsum("tbv,ve->tbe", spots, embedding[m], preferred_element_type=F32).astype(B16)
        in_grad = jnp.einsum("tbe,tbgn->gen", x, grads, preferred_element_type=F32)
        bias = jnp.sum(grads, axis=(0, 1), dtype=F32)
        dx = jnp.einsum("tbgn,gen->tbe", grads, w_in[m], preferred_element_type=F32)
        embed_grad = jnp.einsum("tbv,tbe->ve", spots.astype(F32), dx, precision=PRECISE)
        return rec, in_grad, bias, embed_grad

    parts = (
        per_model(ran.full_front, gates.gates_front, ids[0], 0),
        per_model(ran.full_back, gates.gates_back, ids[1], 1),
    )
    rec, in_grad, bias, embed_grad = (jnp.stack(values) for values in zip(*parts))
    rec_grad = lax.psum_scatter(rec, "rep", scatter_dimension=2, tiled=True)
    in_sum, bias_sum = lax.psum((in_grad, bias), "rep")
    embed_sum = lax.psum(embed_grad, ("rep", "shard"))
    return embed_sum, in_sum, rec_grad, bias_sum


def shards(char_ids, prefix, embedding, w_in, w_rec, gate_bias, w_out, b_out):
    seq_dev, length = char_ids.shape
    half_len = length // 2
    vocab_size, embed = embedding.shape[1:]
    shard_units = w_rec.shape[3]
    count, groups = lax.axis_size("shard"), lax.axis_size("rep")
    stream = groups == 8
    group_size = seq_dev * count
    factor = 1.0 / math.sqrt(groups * count * seq_dev * length)
    own_ids = jnp.concatenate([char_ids, prefix[:, None]], axis=1)
    own_ids = jnp.pad(own_ids, ((0, 0), (0, LANES - length - 1)))
    full_out = lax.all_gather(w_out, "shard", axis=1, tiled=True)
    depth = -(-(embed + 1) // LANES) * LANES
    padded = -(-vocab_size // LANES) * LANES
    table = jnp.pad(embedding, ((0, 0), (0, 0), (0, 1)), constant_values=1)
    table = jnp.pad(table, ((0, 0), (0, padded - vocab_size), (0, depth - embed - 1)))
    inputs = jnp.pad(w_in, ((0, 0), (0, 0), (0, depth - embed), (0, 0)))
    ran = run_forward(
        count, groups, stream, length, own_ids, table, inputs, gate_bias.astype(F32), w_rec
    )
    group_chars, group_prefix = ran.group_ids[:, :length], ran.group_ids[:, length]
    front_in = group_chars.T
    front_target = jnp.concatenate([group_chars[:, 1:], group_chars[:, :1]], axis=1).T
    timeline = jnp.arange(length, dtype=jnp.int32)[:, None]
    front_active = jnp.broadcast_to((timeline < length - 1).astype(F32), (length, group_size))
    reverse_steps = jnp.arange(half_len, dtype=jnp.int32)[:, None]

    def back_pick(offset):
        spot = jnp.maximum(group_prefix[None, :] - offset - reverse_steps, 0)
        chosen = one_hot(spot, length, jnp.int32) * group_chars[None]
        return jnp.sum(chosen, axis=-1)

    back_target = back_pick(2)
    back_active = (reverse_steps <= group_prefix[None, :] - 2).astype(F32)
    first_unit = lax.axis_index("shard") * shard_units

    def decode(full, m, target, active):
        rows = full.reshape(-1, full.shape[-1])
        logits = dot(rows, full_out[m]) + b_out[m].astype(F32)
        grad = loss_grad(logits, target.reshape(-1), active.reshape(-1), factor)
        dec = dot_last(grad, w_out[m])
        own = lax.dynamic_slice_in_dim(rows, first_unit, shard_units, axis=1)
        out_grad = dot_first(own, grad)
        bout = jnp.sum(grad, axis=0, dtype=F32)
        return dec.reshape(full.shape[0], group_size, shard_units), out_grad, bout

    front_dec, front_out_grad, front_bout = decode(ran.full_front, 0, front_target, front_active)
    back_dec, back_out_grad, back_bout = decode(ran.full_back, 1, back_target, back_active)
    out_and_bout = jnp.stack(
        [
            jnp.concatenate([front_out_grad, front_bout[None]], axis=0),
            jnp.concatenate([back_out_grad, back_bout[None]], axis=0),
        ]
    )
    out_and_bout = lax.psum(out_and_bout, "rep")
    out_sum, bout_sum = out_and_bout[:, :shard_units], out_and_bout[:, shard_units]
    core = lax.rem(lax.axis_index("rep"), 2)
    w_pair = lax.dynamic_slice_in_dim(inputs, 2 * core, 2, axis=1)
    done = run_backward(
        count, groups, stream, ran, (front_dec, back_dec), table[:, :vocab_size], w_pair
    )
    if stream:
        in_sum, bias_sum = done.in_grad[:, :, :embed], done.in_grad[:, :, embed]
        embed_sum = done.embed_full[:, :vocab_size, :embed]
        rec_grad = done.rec_grad
    else:
        embed_sum, in_sum, rec_grad, bias_sum = reduced_grads(
            ran, done, embedding, w_in, (front_in, back_pick(1)), group_size
        )
    return (embed_sum, in_sum, rec_grad, bias_sum, out_sum, bout_sum)


def solution(mesh):
    in_specs = (
        P(("rep", "shard"), None),
        P(("rep", "shard")),
        P(),
        P(None, None, None, "shard"),
        P(None, None, None, "shard"),
        P(None, None, "shard"),
        P(None, "shard", None),
        P(),
    )
    out_specs = (
        P(),
        P(None, None, None, "shard"),
        P(None, None, "rep", "shard"),
        P(None, None, "shard"),
        P(None, "shard", None),
        P(),
    )
    return jax.shard_map(shards, mesh=mesh, in_specs=in_specs, out_specs=out_specs, check_vma=False)
```

time: 1010 us -> 582 us (0.58)
  waiting for transfers between devices: 333 us -> 0.04 us
  blocking collectives: 36.5 us -> 0 us
  matrix products: 43.5 us -> 11.2 us
  other arithmetic: 28.1 us -> 6.67 us
  local copies, waits for them, and re-layouts: 40.5 us -> 21.7 us
  Pallas kernels: 508 us -> 524 us
    reduce_scatter x1 -> x0, waiting for transfers between devices: 203 us -> none  [shards(): lax.psum_scatter(jnp.stack([front_rec_grad, back_rec_grad]), 'rep', scatt...]
    psum x2 -> x1, waiting for transfers between devices: 130 us -> 0.01 us  [shards(): out_and_bout = lax.psum(out_and_bout, 'rep')]
    dot_general x16 -> x6, matrix products: 43.5 us -> 11.2 us  [the longest x2 5.41 us: dot(): return jnp.dot(left, right, preferred_element_type=F32)]
    psum x1 -> x0, blocking collectives: 22.9 us -> none  [shards(): in_sum, bias_sum = lax.psum((in_grad, bias_grad), 'rep')]
    another operation x6 -> x2, other arithmetic: 21.7 us -> 1.31 us  [shards(): jnp.stack([jnp.concatenate([front_out_grad, front_bout[None]], axis=0), j...]
    pallas_call x2, Pallas kernels: 508 us -> 524 us  [call(): pl.pallas_call(kernel, out_shape=tuple((jax.ShapeDtypeStruct(shape, kind)...]
    all_gather x1 -> x0, blocking collectives: 13.5 us -> none  [shards(): gathered = lax.all_gather(ids_and_prefix, 'shard', axis=0, tiled=True)]
    reshape x2 -> x0, local copies, waits for them, and re-layouts: 10.1 us -> none  [the longest x1 6.15 us: shards(): front_grads = front_grads.reshape(length, group_size, 4, shard_units)]
  transfers between devices with their start and end apart: 4 -> 2, of which waited for: 3 -> 0; matrix products, arithmetic and copies ran while one was open for 6% -> 3% of each run, Pallas kernels for 24% -> 91%
where the time goes in v2:
time: 582 us; the launch traced here: 578 us
  Pallas kernels  524 us (90%)
  local copies, waits for them, and re-layouts  21.7 us (4%)
  between operations  14.5 us (2%)
  matrix products  11.2 us (2%)
  other arithmetic  6.67 us (1%)
    pallas_call x2, Pallas kernels, call(): pl.pallas_call(kernel, out_shape=tuple((jax.ShapeDtypeStruct(shape, kind)...  524 us
    unnamed x32, local copies, waits for them, and re-layouts  12.4 us
  transfers between devices with their start and end apart: 2, of which 0 were waited for; matrix products, arithmetic and copies ran while one was open for 3% of the time, Pallas kernels for 91%

profile of v2, /device:TPU:0, one launch (start us, length us, event | category | flops | bytes accessed | tf_op | source)
XLA Modules:
  0.0 578.0 jit_solution(5817200438600792524)
XLA Ops:
  7.3 2.0 copy.41
  9.3 0.0 all-reduce.6.cloned.1.call-start
  9.3 0.1 copy.38
  9.4 0.6 convert_element_type.43.refs_3_
  10.1 0.7 fusion.7.refs_1_
  10.8 0.2 copy.40
  11.0 0.1 pad_add_fusion
  11.0 0.6 pad.20.refs_0_
  11.6 1.1 pad.23.refs_2_
  12.7 242.7 %recurrence_forward.1 = (bf16[48,16,2048]{2,1,0:T(8,128)(2,1)}, bf16[24,16,2048]{2,1,0:T(8,128)(2,1)}, f32[48,4,16,512]{3,2,1,0:T(8,128)}, f32[24,4,16,512]{3,2,...) custom-call(s32[4,128]{1,0:T(4,128)} %pad.20.refs_0_, ...), custom_call_target="tpu_custom_call" | custom-call | flops 99999997952 | bytes 52428800 | tf_op jit(solution)/shard_map/recurrence_forward/pallas_call | solution.py:97
  255.5 0.1 broadcast_in_dim.9
  255.6 0.1 mul.55
  255.6 0.9 slice.53
  256.5 1.0 add_reduce_fusion
  257.5 0.1 mul.62
  257.6 1.3 select_reduce_fusion
  258.9 0.1 eq.50
  259.0 0.1 add_bitcast_fusion
  259.0 0.1 copy.42
  259.1 0.1 eq.43
  259.2 0.9 constant_dynamic-slice_fusion.refs_11_
  260.1 0.8 slice_select_fusion.refs_10_
  260.9 2.1 fusion.15
  263.0 0.1 fusion.8
  263.1 0.2 convert_reduce_fusion.1
  263.3 0.2 copy.45
  263.5 1.3 fusion.5
  264.8 3.3 fusion.14
  268.2 0.1 fusion.2
  268.3 0.4 convert_reduce_fusion
  268.7 1.5 fusion
  270.2 0.3 copy.43
  270.5 0.1 broadcast_in_dim.12
  270.6 0.1 broadcast_in_dim.13
  270.7 0.1 maximum_bitcast_fusion
  270.8 1.2 pad_maximum_fusion
  272.1 1.3 fusion.9.refs_5_
  273.3 1.7 fusion.10.refs_4_
  275.0 281.1 %recurrence_backward.1 = (bf16[48,8,16,1024]{3,2,1,0:T(8,128)(2,1)}, bf16[24,8,16,1024]{3,2,1,0:T(8,128)(2,1)}, f32[2,4,256,512]{3,2,1,0:T(8,128)}, f32[2,4,128,512]{3,2,1,0:T(8,128)}, f32[2,320,128]{2,1,0:T(8,128)}) custom-call(f32[48,4,16,512]{3,2,1,0:T(8,128)} %get-tuple-element.20.refs_0_, f32[24,4,16,512]{3,2,1,0:T(8,128)} %get-tuple-element.21.refs_1_, ...), custom_call_target="tpu_custom_call" | custom-call | flops 99999997952 | bytes 52428800 | tf_op jit(solution)/shard_map/recurrence_backward/pallas_call | solution.py:97
  556.1 0.9 slice.64
  557.1 1.6 slice.63
  558.7 0.9 copy.49
  559.6 2.2 copy.50
  561.8 0.6 copy.54
  562.4 1.3 slice-done
  563.7 1.9 copy.51
  565.6 0.8 slice_reduce_fusion
  566.3 4.6 copy.57
  (36 shorter events, 0.2 us)
Async XLA Ops:
  7.2 2.2 copy-start.11
  7.2 2.3 copy-start.7
  7.2 2.9 copy-start.5
  7.2 3.6 copy-start.2
  7.2 253.7 %all-gather.2.cloned.1.call-start = ((), (), s32[]{:S(2)}) async-start(), calls=%async_computation | async-start | bytes 2867200 | tf_op jit(solution)/shard_map/all_gather | solution.py:805
  9.3 1.7 copy-start.9
  9.3 553.2 %all-reduce.6.cloned.1.call-start = ((), (), s32[]{:S(2)}) async-start(), calls=%async_computation.1 | async-start | bytes 2867200 | tf_op jit(solution)/shard_map/psum | solution.py:848
  12.7 246.5 %copy-start.8 = (bf16[2,275]{1,0:T(2,128)(2,1)S(1)}, bf16[2,275]{1,0:T(2,128)(2,1)}, u32[]{:S(2)}) copy-start(bf16[2,275]{1,0:T(2,128)(2,1)} %param.15) | copy-start | bytes 3304
  12.7 247.4 %copy-start.10 = (pred[320]{0:T(512)(128)(4,1)S(1)}, pred[320]{0:T(512)(128)(4,1)}, u32[]{:S(2)}) copy-start(pred[320]{0:T(512)(128)(4,1)} %constant.38.clone.1) | copy-start | bytes 964
  255.4 4.6 copy-start.3
  255.5 5.4 copy-start.6
  270.8 1.2 copy-start
  557.1 1.7 copy-start.4
  562.4 1.3 slice-start
  563.7 1.9 copy-start.1
Sparse Core Ops, SparseCore 0:
  10.2 83.5 all-gather.1
  272.2 77.0 all-reduce.5

commit v3 on v2

--- a/solution.py
+++ b/solution.py
@@ -439,11 +439,17 @@
         spots = [marks(id_column(ids, stops, m, 2 * pair + i), r.sums.shape[1]) for i in range(2)]
         r.sums[m] += dot_first(jnp.concatenate(spots, axis=0), dz)
 
+    def box(side, m, t, k):
+        slot = lax.rem(t, 2)
+        if k == 0:
+            return (r.outbox if side == 0 else r.inbox).at[m, slot]
+        return (r.outbox_far if side == 0 else r.inbox_far).at[m, slot, k - 1]
+
     def exchange(m, t, k):
         slot = lax.rem(t, 2)
         return pltpu.make_async_remote_copy(
-            src_ref=r.outbox.at[m, slot, k],
-            dst_ref=r.inbox.at[m, slot, k],
+            src_ref=box(0, m, t, k),
+            dst_ref=box(1, m, t, k),
             send_sem=r.send_sem.at[m, slot, k],
             recv_sem=r.recv_sem.at[m, slot, k],
             device_id={"shard": peers[k]},
@@ -474,7 +480,8 @@
 
     def send_products(m, t):
         for k in reversed(range(len(peers))):
-            r.outbox[m, lax.rem(t, 2), k] = product(m, t, peers[k])
+            target = box(0, m, t, k)
+            target[...] = product(m, t, peers[k]).astype(target.dtype)
             exchange(m, t, k).start()
         r.own_part[m] = product(m, t, place)
         spread(m, t)
@@ -483,14 +490,17 @@
         total = decs[m][t - 1] + r.own_part[m]
         for k in range(len(peers)):
             exchange(m, t, k).wait_recv()
-            total = total + r.inbox[m, lax.rem(t, 2), k]
+            total = total + box(1, m, t, k)[...].astype(F32)
+        return total
+
+    def sent(m, t):
         for k in range(len(peers)):
             exchange(m, t, k).wait_send()
-        return total
 
     def retreat(m, t):
         gate_grads(m, t, incoming(m, t + 1), r.cell_grad[m], cells[m][t - 1])
         send_products(m, t)
+        sent(m, t + 1)
 
     def first(m):
         t = ends[m] - 1
@@ -501,63 +511,49 @@
     def last(m):
         gate_grads(m, 0, incoming(m, 1), r.cell_grad[m], None)
         spread(m, 0)
+        sent(m, 1)
 
     def lagged(work, m, step):
         if not stream:
             return
-        pairs = ends[m] // 2
-
-        @pl.when(jnp.logical_and(step >= 2, step < pairs + 2))
-        def _():
-            work(m, pairs + 1 - step)
-
+        if m == 0:
+            pl.when(step >= 2)(lambda: work(0, length // 2 + 1 - step))
+        else:
+            ready = jnp.logical_and(step >= 3, lax.rem(step, 2) == 1)
+            pl.when(ready)(lambda: work(1, half_len // 2 - 1 - (step - 3) // 2))
+
+    assert half_len % 2 == 0 and length == 2 * half_len
+    final = half_len - 1
     first(0)
     first(1)
     retreat(0, length - 2)
-    retreat(1, half_len - 2)
-
-    def both(step, carry):
-        retreat(0, length - 1 - 2 * step)
-        lagged(fetch, 0, step)
-        retreat(1, half_len - 1 - 2 * step)
-        lagged(fetch, 1, step)
-        retreat(0, length - 2 - 2 * step)
-        lagged(accumulate, 0, step)
-        retreat(1, half_len - 2 - 2 * step)
-        lagged(accumulate, 1, step)
-        return carry
-
-    def front_only(step, carry):
+
+    def turn(step, carry):
         retreat(0, length - 1 - 2 * step)
         lagged(fetch, 0, step)
         lagged(fetch, 1, step)
+        retreat(1, half_len - 1 - step)
         retreat(0, length - 2 - 2 * step)
         lagged(accumulate, 0, step)
         lagged(accumulate, 1, step)
         return carry
 
-    assert half_len % 2 == 0 and length == 2 * half_len
-    turns = half_len // 2
-    lax.fori_loop(1, turns - 1, both, 0)
-    retreat(0, length - 1 - 2 * (turns - 1))
-    lagged(fetch, 0, turns - 1)
-    retreat(1, 1)
-    lagged(fetch, 1, turns - 1)
-    retreat(0, length - 2 * turns)
-    lagged(accumulate, 0, turns - 1)
+    lax.fori_loop(1, final, turn, 0)
+    retreat(0, 1)
+    lagged(fetch, 0, final)
+    lagged(fetch, 1, final)
     last(1)
-    lagged(accumulate, 1, turns - 1)
-    lax.fori_loop(turns, 2 * turns - 1, front_only, 0)
-    retreat(0, 1)
-    lagged(fetch, 0, 2 * turns - 1)
     last(0)
-    lagged(accumulate, 0, 2 * turns - 1)
     if not stream:
         return
-    lagged(fetch, 0, 2 * turns)
-    lagged(accumulate, 0, 2 * turns)
-    lagged(fetch, 0, 2 * turns + 1)
-    lagged(accumulate, 0, 2 * turns + 1)
+    fetch(0, 1)
+    accumulate(0, 2)
+    accumulate(1, 1)
+    accumulate(0, 1)
+    fetch(1, 0)
+    fetch(0, 0)
+    accumulate(1, 0)
+    accumulate(0, 0)
     for m in range(2):
         for j, other in enumerate(others):
             part = wides[m].at[:, 0]
@@ -688,7 +684,8 @@
     units = ran.w_turned.shape[2]
     links = max(count - 1, 1)
     dma = pltpu.SemaphoreType.DMA
-    box = (2, 2, links, rows, shard_units)
+    box = (2, 2, rows, shard_units)
+    far_box = (2, 2, max(links - 1, 1), rows, shard_units)
     ins = [
         ("acts_front", ran.acts_front, VMEM),
         ("acts_back", ran.acts_back, VMEM),
@@ -706,11 +703,13 @@
         ("weights", pltpu.VMEM(ran.w_turned.shape, B16)),
         ("outbox", pltpu.VMEM(box, F32)),
         ("inbox", pltpu.VMEM(box, F32)),
+        ("outbox_far", pltpu.VMEM(far_box, B16)),
+        ("inbox_far", pltpu.VMEM(far_box, B16)),
         ("own_part", pltpu.VMEM((2, rows, shard_units), F32)),
         ("cell_grad", pltpu.VMEM((2, rows, shard_units), F32)),
         ("load_sem", dma((2,))),
-        ("send_sem", dma(box[:3])),
-        ("recv_sem", dma(box[:3])),
+        ("send_sem", dma((2, 2, links))),
+        ("recv_sem", dma((2, 2, links))),
     ]
     if stream:
         wide = ran.past_front.shape[3]

time: 582 us -> 542 us (0.931)
  Pallas kernels: 524 us -> 487 us
    pallas_call x2, Pallas kernels: 524 us -> 487 us  [call(): pl.pallas_call(kernel, out_shape=tuple((jax.ShapeDtypeStruct(shape, kind)...]
  transfers between devices with their start and end apart: 2 -> 2, of which waited for: 0 -> 0; matrix products, arithmetic and copies ran while one was open for 3% -> 3% of each run, Pallas kernels for 91% -> 90%
where the time goes in v3:
time: 542 us; the launch traced here: 541 us
  Pallas kernels  487 us (90%)
  local copies, waits for them, and re-layouts  21.7 us (4%)
  between operations  14.3 us (3%)
  matrix products  11.2 us (2%)
  other arithmetic  6.67 us (1%)
    pallas_call x2, Pallas kernels, call(): pl.pallas_call(kernel, out_shape=tuple((jax.ShapeDtypeStruct(shape, kind)...  487 us
    unnamed x32, local copies, waits for them, and re-layouts  12.4 us
  transfers between devices with their start and end apart: 2, of which 0 were waited for; matrix products, arithmetic and copies ran while one was open for 3% of the time, Pallas kernels for 90%

profile of v3, /device:TPU:0, one launch (start us, length us, event | category | flops | bytes accessed | tf_op | source)
XLA Modules:
  0.0 541.2 jit_solution(18322605100928895846)
XLA Ops:
  7.3 2.0 copy.41
  9.3 0.0 all-reduce.6.cloned.1.call-start
  9.3 0.1 copy.38
  9.4 0.6 convert_element_type.43.refs_3_
  10.1 0.7 fusion.7.refs_1_
  10.8 0.2 copy.40
  11.0 0.1 pad_add_fusion
  11.0 0.6 pad.20.refs_0_
  11.6 1.1 pad.23.refs_2_
  12.7 242.7 %recurrence_forward.1 = (bf16[48,16,2048]{2,1,0:T(8,128)(2,1)}, bf16[24,16,2048]{2,1,0:T(8,128)(2,1)}, f32[48,4,16,512]{3,2,1,0:T(8,128)}, f32[24,4,16,512]{3,2,...) custom-call(s32[4,128]{1,0:T(4,128)} %pad.20.refs_0_, ...), custom_call_target="tpu_custom_call" | custom-call | flops 99999997952 | bytes 52428800 | tf_op jit(solution)/shard_map/recurrence_forward/pallas_call | solution.py:97
  255.5 0.1 broadcast_in_dim.9
  255.6 0.1 mul.55
  255.6 0.9 slice.53
  256.5 1.0 add_reduce_fusion
  257.5 0.1 mul.62
  257.6 1.3 select_reduce_fusion
  258.9 0.1 eq.50
  259.0 0.1 add_bitcast_fusion
  259.0 0.1 copy.42
  259.1 0.1 eq.43
  259.2 0.9 constant_dynamic-slice_fusion.refs_11_
  260.1 0.8 slice_select_fusion.refs_10_
  260.9 2.1 fusion.15
  263.0 0.1 fusion.8
  263.1 0.2 convert_reduce_fusion.1
  263.3 0.2 copy.45
  263.5 1.3 fusion.5
  264.8 3.3 fusion.14
  268.2 0.1 fusion.2
  268.3 0.4 convert_reduce_fusion
  268.7 1.5 fusion
  270.2 0.3 copy.43
  270.5 0.1 broadcast_in_dim.12
  270.6 0.1 broadcast_in_dim.13
  270.7 0.1 maximum_bitcast_fusion
  270.8 1.2 pad_maximum_fusion
  272.1 1.3 fusion.9.refs_5_
  273.3 1.7 fusion.10.refs_4_
  275.0 244.5 %recurrence_backward.1 = (bf16[48,8,16,1024]{3,2,1,0:T(8,128)(2,1)}, bf16[24,8,16,1024]{3,2,1,0:T(8,128)(2,1)}, f32[2,4,256,512]{3,2,1,0:T(8,128)}, f32[2,4,128,512]{3,2,1,0:T(8,128)}, f32[2,320,128]{2,1,0:T(8,128)}) custom-call(f32[48,4,16,512]{3,2,1,0:T(8,128)} %get-tuple-element.20.refs_0_, f32[24,4,16,512]{3,2,1,0:T(8,128)} %get-tuple-element.21.refs_1_, ...), custom_call_target="tpu_custom_call" | custom-call | flops 99999997952 | bytes 52428800 | tf_op jit(solution)/shard_map/recurrence_backward/pallas_call | solution.py:97
  519.6 0.9 slice.64
  520.5 1.6 slice.63
  522.2 0.9 copy.49
  523.0 2.2 copy.50
  525.3 0.6 copy.54
  525.9 1.3 slice-done
  527.1 1.9 copy.51
  529.0 0.8 slice_reduce_fusion
  529.8 4.6 copy.57
  (36 shorter events, 0.2 us)
Async XLA Ops:
  7.2 2.2 copy-start.11
  7.2 2.3 copy-start.7
  7.2 2.9 copy-start.5
  7.2 3.6 copy-start.2
  7.2 253.7 %all-gather.2.cloned.1.call-start = ((), (), s32[]{:S(2)}) async-start(), calls=%async_computation | async-start | bytes 2867200 | tf_op jit(solution)/shard_map/all_gather | solution.py:804
  9.3 1.7 copy-start.9
  9.3 516.6 %all-reduce.6.cloned.1.call-start = ((), (), s32[]{:S(2)}) async-start(), calls=%async_computation.1 | async-start | bytes 2867200 | tf_op jit(solution)/shard_map/psum | solution.py:847
  12.7 246.5 %copy-start.8 = (bf16[2,275]{1,0:T(2,128)(2,1)S(1)}, bf16[2,275]{1,0:T(2,128)(2,1)}, u32[]{:S(2)}) copy-start(bf16[2,275]{1,0:T(2,128)(2,1)} %param.15) | copy-start | bytes 3304
  12.7 247.4 %copy-start.10 = (pred[320]{0:T(512)(128)(4,1)S(1)}, pred[320]{0:T(512)(128)(4,1)}, u32[]{:S(2)}) copy-start(pred[320]{0:T(512)(128)(4,1)} %constant.38.clone.1) | copy-start | bytes 964
  255.4 4.6 copy-start.3
  255.5 5.4 %copy-start.6 = (bf16[24,16,2048]{2,1,0:T(8,128)(2,1)S(1)}, bf16[24,16,2048]{2,1,0:T(8,128)(2,1)}, u32[]{:S(2)}) copy-start(bf16[24,16,2048]{2,1,0:T(8,128)(2,1)} %get-tuple-element.26) | copy-start | bytes 4718596
  270.8 1.2 copy-start
  520.5 1.7 copy-start.4
  525.9 1.3 slice-start
  527.1 1.9 copy-start.1
Sparse Core Ops, SparseCore 0:
  10.2 83.5 all-gather.1
  272.2 76.9 all-reduce.5

commit v4 on v3

v4 whole, which is shorter than its diff:
```python
import functools
import math
import types

import jax
import jax.numpy as jnp
from jax import lax
from jax.experimental import pallas as pl
from jax.experimental.pallas import tpu as pltpu
from jax.sharding import PartitionSpec as P

PRECISE = lax.Precision.HIGHEST
MESH = pl.DeviceIdType.MESH
LANES = 128
MIB = 1 << 20
B16 = jnp.bfloat16
F32 = jnp.float32
VMEM = pl.BlockSpec(memory_space=pltpu.VMEM)
ANYWHERE = pl.BlockSpec(memory_space=pl.ANY)


def one_hot(ids, width, out_type):
    return (ids[..., None] == jnp.arange(width, dtype=jnp.int32)).astype(out_type)


def loss_grad(logits, targets, active, factor):
    probabilities = jax.nn.softmax(logits, axis=-1)
    picked = one_hot(targets, logits.shape[-1], F32)
    return ((probabilities - picked) * (active * factor)[:, None]).astype(B16)


def peers_of(place, count):
    if count == 4:
        return [place + 1 - 2 * lax.rem(place, 2), lax.rem(place + 2, 4), 3 - place]
    if count == 2:
        return [1 - place]
    assert count == 1
    return []


def others_of(group, groups):
    return [lax.rem(group + j, groups) for j in range(1, groups)]


def greet(peers, others):
    barrier = pltpu.get_barrier_semaphore()
    for peer in peers:
        pl.semaphore_signal(barrier, inc=1, device_id={"shard": peer}, device_id_type=MESH)
    for other in others:
        pl.semaphore_signal(barrier, inc=1, device_id={"rep": other}, device_id_type=MESH)
    pl.semaphore_wait(barrier, len(peers) + len(others))


def span(index, size):
    return pl.ds(pl.multiple_of(index * size, size), size)


def dot(left, right):
    return jnp.dot(left, right, preferred_element_type=F32)


def dot_last(left, right):
    return lax.dot_general(left, right, (((1,), (1,)), ((), ())), preferred_element_type=F32)


def dot_first(left, right):
    return lax.dot_general(left, right, (((0,), (0,)), ((), ())), preferred_element_type=F32)


def column_of(ids, spot):
    lane = lax.broadcasted_iota(jnp.int32, ids.shape, 1)
    return jnp.sum(jnp.where(lane == spot, ids, 0), axis=1, keepdims=True)


def marks(column, width):
    lane = lax.broadcasted_iota(jnp.int32, (column.shape[0], width), 1)
    return (lane == column).astype(F32).astype(B16)


def id_column(ids, ends, m, t):
    return column_of(ids, t) if m == 0 else column_of(ids, jnp.maximum(ends - 1 - t, 0))


def split_three(value):
    first = value.astype(B16)
    rest = value - first.astype(F32)
    second = rest.astype(B16)
    return first, second, (rest - second.astype(F32)).astype(B16)


def call(body, name, ins, outs, scratch, collective_id, cost):
    names = [*ins, *outs, *scratch]

    def kernel(*refs):
        body(types.SimpleNamespace(**dict(zip(names, refs))))

    results = pl.pallas_call(
        kernel,
        out_shape=tuple(jax.ShapeDtypeStruct(shape, kind) for shape, kind, _ in outs.values()),
        in_specs=[spec for _, spec in ins.values()],
        out_specs=tuple(spec for _, _, spec in outs.values()),
        scratch_shapes=list(scratch.values()),
        compiler_params=pltpu.CompilerParams(
            collective_id=collective_id, has_side_effects=True, vmem_limit_bytes=62 * MIB
        ),
        cost_estimate=pl.CostEstimate(flops=cost, bytes_accessed=50 * MIB, transcendentals=0),
        name=name,
    )(*[value for value, _ in ins.values()])
    return types.SimpleNamespace(**dict(zip(outs, results)))


def forward_body(count, length, r):
    place = lax.axis_index("shard")
    peers = peers_of(place, count)
    units = r.weights.shape[3]
    half_len = length // 2
    seq_dev = r.own_ids.shape[0]
    loads = [pltpu.make_async_copy(r.w_rec.at[m], r.weights.at[m], r.load_sem.at[m]) for m in range(2)]
    for load in loads:
        load.start()
    r.id_blocks[place, :seq_dev] = r.own_ids[...]
    greet(peers, [])

    def id_copy(k):
        block = r.id_blocks.at[place]
        return pltpu.make_async_remote_copy(
            src_ref=block,
            dst_ref=block,
            send_sem=r.id_send.at[k],
            recv_sem=r.id_recv.at[k],
            device_id={"shard": peers[k]},
            device_id_type=MESH,
        )

    for k in range(len(peers)):
        id_copy(k).start()
    fulls = (r.full_front, r.full_back)
    acts = (r.acts_front, r.acts_back)
    cells = (r.cell_front, r.cell_back)
    def exchange(m, t, k):
        slot = lax.rem(t, 2)
        own = fulls[m].at[t, :, span(place, units)]
        return pltpu.make_async_remote_copy(
            src_ref=own,
            dst_ref=own,
            send_sem=r.send_sem.at[m, slot, k],
            recv_sem=r.recv_sem.at[m, slot, k],
            device_id={"shard": peers[k]},
            device_id_type=MESH,
        )

    def finish(m, t, sums, memory):
        in_gate = jax.nn.sigmoid(sums[0])
        forget = jax.nn.sigmoid(sums[1])
        candidate = jnp.tanh(sums[2])
        out_gate = jax.nn.sigmoid(sums[3])
        new_memory = in_gate * candidate if memory is None else forget * memory + in_gate * candidate
        fulls[m][t, :, span(place, units)] = (out_gate * jnp.tanh(new_memory)).astype(B16)
        for k in reversed(range(len(peers))):
            exchange(m, t, k).start()
        for g, value in enumerate((in_gate, forget, candidate, out_gate)):
            acts[m][t, g] = value
        cells[m][t] = new_memory

    def start_sums(m, t):
        ids, ends = r.group_ids[...], r.group_ids[:, length : length + 1]
        spots = marks(id_column(ids, ends, m, t), r.table.shape[1])
        x_t = dot(spots, r.table[m]).astype(B16)
        return [r.bias[m, g : g + 1] + dot(x_t, r.w_in[m, g]) for g in range(4)]

    def add_chunk(m, t, owner, sums):
        part = fulls[m][t, :, span(owner, units)]
        return [sums[g] + dot(part, r.weights[m, g, span(owner, units), :]) for g in range(4)]

    def advance(m, t):
        sums = add_chunk(m, t - 1, place, start_sums(m, t))
        for k in range(len(peers)):
            exchange(m, t - 1, k).wait_recv()
            sums = add_chunk(m, t - 1, peers[k], sums)
        for k in range(len(peers)):
            exchange(m, t - 1, k).wait_send()
        finish(m, t, sums, cells[m][t - 1])

    def turn_copy(slot, m, g, p):
        return pltpu.make_async_copy(
            r.turned.at[slot],
            r.w_turned.at[m, span(g, units), span(p, units)],
            r.turn_sem.at[slot],
        )

    blocks = 8 * count

    def turn(block, slot):
        m, g, p = block // (4 * count), lax.rem(block // count, 4), lax.rem(block, count)

        @pl.when(block < blocks)
        def _():
            @pl.when(block >= 2)
            def _():
                turn_copy(slot, 0, 0, 0).wait()

            r.turned[slot] = r.weights[m, g, span(p, units), :].T
            turn_copy(slot, m, g, p).start()

    for k in range(len(peers)):
        id_copy(k).wait_send()
        id_copy(k).wait_recv()
    for s in range(count):
        r.group_ids[s * seq_dev : (s + 1) * seq_dev] = r.id_blocks[s, :seq_dev]
    finish(0, 0, start_sums(0, 0), None)
    finish(1, 0, start_sums(1, 0), None)
    for load in loads:
        load.wait()

    def both(t, carry):
        advance(0, t)
        advance(1, t)
        return carry

    def front_only(t, carry):
        advance(0, t)
        turn(2 * (t - half_len), 0)
        turn(2 * (t - half_len) + 1, 1)
        return carry

    assert blocks <= 2 * (length - half_len)
    lax.fori_loop(1, half_len, both, 0)
    lax.fori_loop(half_len, length, front_only, 0)
    for m, end in ((0, length), (1, half_len)):
        for k in range(len(peers)):
            copy = exchange(m, end - 1, k)
            copy.wait_send()
            copy.wait_recv()
    for slot in range(2):
        turn_copy(slot, 0, 0, 0).wait()


def run_forward(count, length, own_ids, table, w_in, bias, w_rec):
    half_len = length // 2
    units, shard_units = w_rec.shape[2:]
    seq_dev = own_ids.shape[0]
    rows = seq_dev * count
    dma = pltpu.SemaphoreType.DMA
    links = max(count - 1, 1)
    ins = dict(
        own_ids=(own_ids, VMEM),
        table=(table, VMEM),
        w_in=(w_in, VMEM),
        bias=(bias, VMEM),
        w_rec=(w_rec, ANYWHERE),
    )
    outs = dict(
        full_front=((length, rows, units), B16, VMEM),
        full_back=((half_len, rows, units), B16, VMEM),
        acts_front=((length, 4, rows, shard_units), F32, VMEM),
        acts_back=((half_len, 4, rows, shard_units), F32, VMEM),
        cell_front=((length, rows, shard_units), F32, VMEM),
        cell_back=((half_len, rows, shard_units), F32, VMEM),
        group_ids=((rows, LANES), jnp.int32, VMEM),
        w_turned=((2, 4 * shard_units, units), B16, ANYWHERE),
    )
    scratch = dict(
        weights=(pltpu.VMEM(w_rec.shape, B16)),
        turned=(pltpu.VMEM((2, shard_units, shard_units), B16)),
        id_blocks=(pltpu.VMEM((count, max(8, seq_dev), LANES), jnp.int32)),
        load_sem=(dma((2,))),
        turn_sem=(dma((2,))),
        send_sem=(dma((2, 2, links))),
        recv_sem=(dma((2, 2, links))),
        id_send=(dma((links,))),
        id_recv=(dma((links,))),
    )
    body = functools.partial(forward_body, count, length)
    return call(body, "recurrence_forward", ins, outs, scratch, 0, 10**11)


def backward_body(count, r):
    place = lax.axis_index("shard")
    peers = peers_of(place, count)
    units = r.cell_front.shape[2]
    length, half_len = r.cell_front.shape[0], r.cell_back.shape[0]
    loads = [pltpu.make_async_copy(r.w_turned.at[m], r.weights.at[m], r.load_sem.at[m]) for m in range(2)]
    for load in loads:
        load.start()
    acts = (r.acts_front, r.acts_back)
    cells = (r.cell_front, r.cell_back)
    decs = (r.dec_front, r.dec_back)
    gates = (r.gates_front, r.gates_back)
    ends = (length, half_len)
    greet(peers, [])

    def box(side, m, t, k):
        slot = lax.rem(t, 2)
        if k == 0:
            return (r.outbox if side == 0 else r.inbox).at[m, slot]
        return (r.outbox_far if side == 0 else r.inbox_far).at[m, slot, k - 1]

    def exchange(m, t, k):
        slot = lax.rem(t, 2)
        return pltpu.make_async_remote_copy(
            src_ref=box(0, m, t, k),
            dst_ref=box(1, m, t, k),
            send_sem=r.send_sem.at[m, slot, k],
            recv_sem=r.recv_sem.at[m, slot, k],
            device_id={"shard": peers[k]},
            device_id_type=MESH,
        )

    def gate_grads(m, t, grad_hidden, carried, prev_memory):
        in_gate, forget, candidate, out_gate = (acts[m][t, g] for g in range(4))
        squashed = jnp.tanh(cells[m][t])
        grad_memory = grad_hidden * out_gate * (1.0 - squashed * squashed)
        if carried is not None:
            grad_memory = carried + grad_memory
        r.cell_grad[m] = grad_memory * forget
        forget_part = jnp.zeros_like(grad_memory)
        if prev_memory is not None:
            forget_part = grad_memory * prev_memory * forget * (1.0 - forget)
        values = (
            grad_memory * candidate * in_gate * (1.0 - in_gate),
            forget_part,
            grad_memory * in_gate * (1.0 - candidate * candidate),
            grad_hidden * squashed * out_gate * (1.0 - out_gate),
        )
        for g, value in enumerate(values):
            gates[m][t, :, g * units : (g + 1) * units] = value.astype(B16)

    def product(m, t, owner):
        return dot(gates[m][t], r.weights[m, :, span(owner, units)])

    def send_products(m, t):
        for k in reversed(range(len(peers))):
            target = box(0, m, t, k)
            target[...] = product(m, t, peers[k]).astype(target.dtype)
            exchange(m, t, k).start()
        r.own_part[m] = product(m, t, place)

    def incoming(m, t):
        total = decs[m][t - 1] + r.own_part[m]
        for k in range(len(peers)):
            exchange(m, t, k).wait_recv()
            total = total + box(1, m, t, k)[...].astype(F32)
        return total

    def sent(m, t):
        for k in range(len(peers)):
            exchange(m, t, k).wait_send()

    def retreat(m, t):
        gate_grads(m, t, incoming(m, t + 1), r.cell_grad[m], cells[m][t - 1])
        send_products(m, t)
        sent(m, t + 1)

    def first(m):
        t = ends[m] - 1
        gate_grads(m, t, decs[m][t], None, cells[m][t - 1])
        loads[m].wait()
        send_products(m, t)

    def last(m):
        gate_grads(m, 0, incoming(m, 1), r.cell_grad[m], None)
        sent(m, 1)

    assert half_len % 2 == 0 and length == 2 * half_len
    final = half_len - 1
    first(0)
    first(1)
    retreat(0, length - 2)

    def turn(step, carry):
        retreat(0, length - 1 - 2 * step)
        retreat(1, half_len - 1 - step)
        retreat(0, length - 2 - 2 * step)
        return carry

    lax.fori_loop(1, final, turn, 0)
    retreat(0, 1)
    last(1)
    last(0)


def run_backward(count, ran, decs):
    length, rows, shard_units = ran.cell_front.shape
    half_len = ran.cell_back.shape[0]
    units = ran.w_turned.shape[2]
    links = max(count - 1, 1)
    dma = pltpu.SemaphoreType.DMA
    box = (2, 2, rows, shard_units)
    far_box = (2, 2, max(links - 1, 1), rows, shard_units)
    ins = dict(
        acts_front=(ran.acts_front, VMEM),
        acts_back=(ran.acts_back, VMEM),
        cell_front=(ran.cell_front, VMEM),
        cell_back=(ran.cell_back, VMEM),
        dec_front=(decs[0], VMEM),
        dec_back=(decs[1], VMEM),
        w_turned=(ran.w_turned, ANYWHERE),
    )
    gates = dict(
        gates_front=(length, rows, 4 * shard_units),
        gates_back=(half_len, rows, 4 * shard_units),
    )
    scratch = dict(
        weights=(pltpu.VMEM(ran.w_turned.shape, B16)),
        outbox=(pltpu.VMEM(box, F32)),
        inbox=(pltpu.VMEM(box, F32)),
        outbox_far=(pltpu.VMEM(far_box, B16)),
        inbox_far=(pltpu.VMEM(far_box, B16)),
        own_part=(pltpu.VMEM((2, rows, shard_units), F32)),
        cell_grad=(pltpu.VMEM((2, rows, shard_units), F32)),
        load_sem=(dma((2,))),
        send_sem=(dma((2, 2, links))),
        recv_sem=(dma((2, 2, links))),
    )
    outs = {key: (shape, B16, VMEM) for key, shape in gates.items()}
    body = functools.partial(backward_body, count)
    return call(body, "recurrence_backward", ins, outs, scratch, 1, 10**11)


def step_body(count, groups, factor, r):
    place = lax.axis_index("shard")
    group = lax.axis_index("rep")
    core = lax.rem(group, 2)
    sibling = group + 1 - 2 * core
    peers = peers_of(place, count)
    others = others_of(group, groups)
    units = r.weights.shape[3]
    length, half_len = r.full_front.shape[0], r.full_back.shape[0]
    ends = (length, half_len)
    rows = r.group_ids.shape[0]
    seq_dev = r.chars.shape[0]
    vocab, _, embed = r.embedding.shape
    wide = r.past_front.shape[3]
    fulls = (r.full_front, r.full_back)
    acts = (r.acts_front, r.acts_back)
    cells = (r.cell_front, r.cell_back)
    logit_grads = (r.logits_front, r.logits_back)
    pasts = (r.past_front, r.past_back)
    wides = (r.wide_front, r.wide_back)
    own_columns = span(place, units)

    inner = (place * (count - 1 - place)) // 2
    urgent = [
        (a + inner * (c - a), peers[a] + inner * (peers[c] - peers[a])) for a, c in ((2, 1), (1, 0), (0, 2))
    ]

    def to_peer(src, dst, send, recv, peer):
        return pltpu.make_async_remote_copy(
            src_ref=src,
            dst_ref=dst,
            send_sem=send,
            recv_sem=recv,
            device_id={"shard": peer},
            device_id_type=MESH,
        )

    def to_group(src, dst, send, recv, other):
        return pltpu.make_async_remote_copy(
            src_ref=src,
            dst_ref=dst,
            send_sem=send,
            recv_sem=recv,
            device_id={"rep": other},
            device_id_type=MESH,
        )

    loads = [pltpu.make_async_copy(r.w_rec.at[m], r.weights.at[m], r.load_sem.at[m]) for m in range(2)]
    for load in loads:
        load.start()
    barrier = pltpu.get_barrier_semaphore()
    for peer in peers:
        pl.semaphore_signal(barrier, inc=1, device_id={"shard": peer}, device_id_type=MESH)
    for other in others:
        pl.semaphore_signal(barrier, inc=1, device_id={"rep": other}, device_id_type=MESH)
    r.id_blocks[group, place, :seq_dev, :length] = r.chars[...]
    corner = (seq_dev, seq_dev)
    diagonal = lax.broadcasted_iota(jnp.int32, corner, 0) == lax.broadcasted_iota(jnp.int32, corner, 1)
    stops_across = jnp.broadcast_to(r.prefix[...], corner)
    r.id_blocks[group, place, :seq_dev, length : length + 1] = jnp.sum(
        jnp.where(diagonal, stops_across, 0), axis=1, keepdims=True
    )
    lane = lax.broadcasted_iota(jnp.int32, r.table.shape, 2)
    r.table[...] = jnp.where(lane == embed, 1.0, 0.0).astype(B16)
    r.inputs[...] = jnp.zeros_like(r.inputs)
    r.out_own[...] = jnp.zeros_like(r.out_own)
    for m in range(2):
        r.table[m, :vocab, :embed] = r.embedding[:, m, :]
        r.out_own[m, :vocab] = r.w_out[:, m, :]
        for g in range(4):
            r.inputs[m, g, :embed] = r.w_in[m, :, g, :]
    r.out_bias[...] = jnp.full_like(r.out_bias, -1e30)
    r.out_bias[:, :vocab] = r.b_out[...].astype(F32)
    share = units // groups
    for m in range(2):
        r.out_full[m, place] = r.out_own[m].T.reshape(groups, share, -1)
    r.blank[...] = jnp.zeros_like(r.blank)
    pl.semaphore_wait(barrier, len(peers) + len(others))

    def id_copy(k):
        block = r.id_blocks.at[group, place]
        return to_peer(block, block, r.id_send.at[k], r.id_recv.at[k], peers[k])

    def id_spread(j):
        block = r.id_blocks.at[group]
        return to_group(block, block, r.ids_send.at[j], r.ids_recv.at[j], others[j])

    for k in range(len(peers)):
        id_copy(k).start()
    blanks = [pltpu.make_async_copy(r.blank, pasts[m].at[0], r.past_local.at[m]) for m in range(2)]
    for copy in blanks:
        copy.start()
    r.in_sums[...] = jnp.zeros_like(r.in_sums)
    r.embed_part[...] = jnp.zeros_like(r.embed_part)
    r.rec_sums[...] = jnp.zeros_like(r.rec_sums)
    r.out_sums[...] = jnp.zeros_like(r.out_sums)

    def share_copy(n):
        k, m = len(peers) - 1 - n // 2, n % 2
        block = r.out_full.at[m, place, group]
        return to_peer(block, block, r.share_send.at[n], r.share_recv.at[n], peers[k])

    def share_spread(j, k):
        source = r.out_full.at[:, peers[k], group]
        other = lax.rem(group + 1 + j, groups)
        return to_group(source, source, r.all_send.at[j, k], r.all_recv.at[j, k], other)

    first_spread = 2 * len(peers) + 3

    def send_shares(t):
        for n in range(2 * len(peers)):
            pl.when(t == n + 1)(share_copy(n).start)

        @pl.when(t == first_spread - 1)
        def _():
            for n in range(2 * len(peers)):
                share_copy(n).wait()

        @pl.when(jnp.logical_and(t >= first_spread, t < first_spread + groups - 1))
        def _():
            for k in range(len(peers)):
                share_spread(t - first_spread, k).start()

    def spread_past(m, t):
        for j, other in enumerate(others):
            to_group(
                fulls[m].at[t, :, span(other // 2, wide)],
                pasts[m].at[t + 1, group],
                r.past_send.at[m, j],
                r.past_recv.at[m, j],
                other,
            ).start()
        pltpu.make_async_copy(
            fulls[m].at[t, :, span(group // 2, wide)], pasts[m].at[t + 1, group], r.past_local.at[m]
        ).start()

    def finish_past(m, steps):
        for j, other in enumerate(others):
            part = pasts[m].at[pl.ds(1, steps), 0]
            copy = to_group(part, part, r.past_send.at[m, j], r.past_recv.at[m, j], other)
            copy.wait_send()
            copy.wait_recv()
        mine = pasts[m].at[pl.ds(1, steps), 0]
        pltpu.make_async_copy(mine, mine, r.past_local.at[m]).wait()

    def exchange(m, t, k, peer):
        slot = lax.rem(t, 2)
        own = fulls[m].at[t, :, own_columns]
        return to_peer(own, own, r.hidden_send.at[m, slot, k], r.hidden_recv.at[m, slot, k], peer)

    def finish(m, t, sums, memory):
        in_gate = jax.nn.sigmoid(sums[0])
        forget = jax.nn.sigmoid(sums[1])
        candidate = jnp.tanh(sums[2])
        out_gate = jax.nn.sigmoid(sums[3])
        new_memory = in_gate * candidate if memory is None else forget * memory + in_gate * candidate
        fulls[m][t, :, own_columns] = (out_gate * jnp.tanh(new_memory)).astype(B16)
        for k, peer in urgent:
            exchange(m, t, k, peer).start()
        for g, value in enumerate((in_gate, forget, candidate, out_gate)):
            acts[m][t, g] = value
        cells[m][t] = new_memory

    def start_sums(m, t):
        ids, stops = r.group_ids[...], r.group_ids[:, length : length + 1]
        x_t = dot(marks(id_column(ids, stops, m, t), r.table.shape[1]), r.table[m]).astype(B16)
        return [
            r.gate_bias[m, g : g + 1, :].astype(F32) + dot(x_t, r.inputs[m, g]) for g in range(4)
        ]

    def add_chunk(m, t, owner, sums):
        part = fulls[m][t, :, span(owner, units)]
        return [sums[g] + dot(part, r.weights[m, g, span(owner, units), :]) for g in range(4)]

    def advance(m, t):
        sums = add_chunk(m, t - 1, place, start_sums(m, t))
        for k in range(len(peers)):
            exchange(m, t - 1, k, peers[k]).wait_recv()
            sums = add_chunk(m, t - 1, peers[k], sums)
        finish(m, t, sums, cells[m][t - 1])
        for k in range(len(peers)):
            exchange(m, t - 1, k, peers[k]).wait_send()
        spread_past(m, t - 1)

    def turn_block(m, g, p):
        r.weights[m, g, span(p, units), :] = r.weights[m, g, span(p, units), :].T

    stretch = 4

    def decode(m, chunk):
        t0 = stretch * chunk
        hidden = fulls[m][pl.ds(t0, stretch)].reshape(stretch * rows, count * units)
        logits = dot(hidden, r.out_full[m].reshape(count * units, -1)) + r.out_bias[m : m + 1, :]
        grown = jnp.exp(logits - jnp.max(logits, axis=1, keepdims=True))
        chances = grown / jnp.sum(grown, axis=1, keepdims=True)
        ids, stops = r.group_ids[...], r.group_ids[:, length : length + 1]
        targets, active = [], []
        for i in range(stretch):
            t = t0 + i
            if m == 0:
                targets.append(column_of(ids, lax.rem(t + 1, length)))
                live = jnp.full((rows, 1), t, jnp.int32) < length - 1
            else:
                targets.append(column_of(ids, jnp.maximum(stops - 2 - t, 0)))
                live = stops >= t + 2
            active.append(jnp.where(live, factor, 0.0).astype(F32))
        target, weight = jnp.concatenate(targets, axis=0), jnp.concatenate(active, axis=0)
        lane = lax.broadcasted_iota(jnp.int32, logits.shape, 1)
        picked = (lane == target).astype(F32)
        grad = ((chances - picked) * weight).astype(B16)
        logit_grads[m][pl.ds(t0, stretch)] = grad.reshape(stretch, rows, -1)
        own = fulls[m][pl.ds(t0, stretch), :, own_columns].reshape(stretch * rows, units)
        ones = jnp.ones((stretch * rows, LANES), B16)
        r.out_sums[m] += dot_first(grad, jnp.concatenate([own, ones], axis=1))

    piece = r.out_inbox.shape[2]

    def out_send(m, j):
        other = lax.rem(group + 1 + j, groups)
        return to_group(
            r.out_sums.at[m, span(other, piece)],
            r.out_inbox.at[m, j],
            r.out_send.at[m, j],
            r.out_recv.at[m, j],
            other,
        )

    def out_share(m, j):
        own = r.out_total.at[m, span(group, piece)]
        other = lax.rem(group + 1 + j, groups)
        return to_group(own, own, r.total_send.at[m, j], r.total_recv.at[m, j], other)

    def out_reduce(m):
        total = r.out_sums[m, span(group, piece)]
        for j in range(groups - 1):
            copy = out_send(m, j)
            copy.wait_send()
            copy.wait_recv()
        for j in range(groups - 1):
            total = total + r.out_inbox[m, j]
        r.out_total[m, span(group, piece)] = total

    def out_steps(m, n):
        pl.when(jnp.logical_and(n >= 0, n < groups - 1))(lambda: out_send(m, n).start())
        pl.when(n == groups)(lambda: out_reduce(m))
        ready = jnp.logical_and(n > groups, n < 2 * groups)
        pl.when(ready)(lambda: out_share(m, n - groups - 1).start())

    for k in range(len(peers)):
        id_copy(k).wait()
    for s in range(count):
        r.group_ids[s * seq_dev : (s + 1) * seq_dev] = r.id_blocks[group, s, :seq_dev]
    for j in range(len(others)):
        id_spread(j).start()
    for copy in blanks:
        copy.wait()
    for m in range(2):
        finish(m, 0, start_sums(m, 0), None)
    for load in loads:
        load.wait()

    def both(t, carry):
        advance(0, t)
        advance(1, t)
        send_shares(t)
        return carry

    back_chunks = half_len // stretch
    blocks = 4 * count
    assert half_len % stretch == 0 and length == 2 * half_len and half_len % 2 == 0
    assert first_spread + groups - 1 <= half_len and blocks <= half_len
    assert back_chunks + 2 * groups <= half_len

    def front_only(t, carry):
        advance(0, t)
        n = t - half_len
        pl.when(n < blocks)(lambda: turn_block(1, n // count, lax.rem(n, count)))
        pl.when(n < back_chunks)(lambda: decode(1, n))
        begun = n >= back_chunks
        early = jnp.logical_and(begun, stretch * (n - back_chunks + 1) <= t)
        late = jnp.logical_and(stretch * (n - back_chunks + 1) > t, lax.rem(t, stretch) == 0)
        pl.when(early)(lambda: decode(0, n - back_chunks))
        pl.when(jnp.logical_and(begun, late))(lambda: decode(0, t // stretch - 1))
        out_steps(1, n - back_chunks)
        return carry

    def settle(m):
        for k in range(len(peers)):
            exchange(m, ends[m] - 1, k, peers[k]).wait()

    lax.fori_loop(1, half_len, both, 0)
    settle(1)
    for j in range(groups - 1):
        for k in range(len(peers)):
            share_spread(j, k).wait()
    lax.fori_loop(half_len, length, front_only, 0)
    for g in range(4):
        for p in range(count):
            turn_block(0, g, p)
    settle(0)
    decode(0, length // stretch - 1)
    finish_past(0, length - 1)
    finish_past(1, half_len - 1)
    for j in range(len(others)):
        id_spread(j).wait()
    r.every_ids[...] = r.id_blocks[:, :, :seq_dev].reshape(r.every_ids.shape)

    gates = fulls

    def spread_gates(m, t):
        for j, other in enumerate(others):
            to_group(
                gates[m].at[t, :, span(lax.rem(other, 2), 2 * units)],
                wides[m].at[t, group],
                r.wide_send.at[m, j],
                r.wide_recv.at[m, t // 2],
                other,
            ).start()
        pltpu.make_async_copy(
            gates[m].at[t, :, span(core, 2 * units)], wides[m].at[t, group], r.wide_local.at[m, t // 2]
        ).start()

    def arrive(m, pair):
        far = wides[m].at[pl.ds(2 * pair, 2), pl.ds(0, groups - 1)]
        to_group(far, far, r.wide_send.at[m, 0], r.wide_recv.at[m, pair], others[0]).wait_recv()
        near = wides[m].at[pl.ds(2 * pair, 2), 0]
        pltpu.make_async_copy(near, near, r.wide_local.at[m, pair]).wait()

    def fetches(m, pair):
        slot = lax.rem(pair, 2)
        return (
            pltpu.make_async_copy(
                wides[m].at[pl.ds(2 * pair, 2)], r.wide_slot.at[m, slot], r.fetch_sem.at[m, slot, 0]
            ),
            pltpu.make_async_copy(
                pasts[m].at[pl.ds(2 * pair, 2)], r.past_slot.at[m, slot], r.fetch_sem.at[m, slot, 1]
            ),
        )

    def fetch(m, pair):
        arrive(m, pair)
        for copy in fetches(m, pair):
            copy.start()

    def accumulate(m, pair):
        slot = lax.rem(pair, 2)
        for copy in fetches(m, pair):
            copy.wait()
        dz = r.wide_slot[m, slot].reshape(-1, 2 * units)
        past = r.past_slot[m, slot].reshape(dz.shape[0], -1)
        r.rec_sums[m] += dot_first(past, dz)
        ids, stops = r.every_ids[...], r.every_ids[:, length : length + 1]
        spots = [marks(id_column(ids, stops, m, 2 * pair + i), r.table.shape[1]) for i in range(2)]
        spots = jnp.concatenate(spots, axis=0)
        r.in_sums[m] += dot_first(dot(spots, r.table[m]).astype(B16), dz)
        grad_x = None
        for g in range(2):
            term = dot_last(dz[:, g * units : (g + 1) * units], r.inputs[m, 2 * core + g])
            grad_x = term if grad_x is None else grad_x + term
        for part in split_three(grad_x):
            r.embed_part[m] += dot_first(spots, part)

    def give(m, t, k, peer):
        slot = lax.rem(t, 2)
        return to_peer(
            r.outbox.at[m, slot, k],
            r.inbox.at[m, slot, k],
            r.grad_send.at[m, slot, k],
            r.grad_recv.at[m, slot, k],
            peer,
        )

    def slopes(m, t, prev_memory):
        in_gate, forget, candidate, out_gate = (acts[m][t, g] for g in range(4))
        squashed = jnp.tanh(cells[m][t])
        forget_slope = jnp.zeros_like(forget)
        if prev_memory is not None:
            forget_slope = prev_memory * forget * (1.0 - forget)
        return (
            candidate * in_gate * (1.0 - in_gate),
            forget_slope,
            in_gate * (1.0 - candidate * candidate),
            squashed * out_gate * (1.0 - out_gate),
            out_gate * (1.0 - squashed * squashed),
            forget,
        )

    def gate_grads(m, t, slope, grad_hidden, carried):
        grad_memory = grad_hidden * slope[4]
        if carried is not None:
            grad_memory = carried + grad_memory
        values = [grad_memory * slope[g] for g in range(3)] + [grad_hidden * slope[3]]
        for g, value in enumerate(values):
            gates[m][t, :, g * units : (g + 1) * units] = value.astype(B16)
        r.cell_grad[m] = grad_memory * slope[5]

    def product(m, t, owner):
        total = None
        for g in range(4):
            part = dot(
                gates[m][t, :, g * units : (g + 1) * units], r.weights[m, g, span(owner, units), :]
            )
            total = part if total is None else total + part
        return total

    def from_decoder(m, t):
        return dot(logit_grads[m][t], r.out_own[m])

    def send_products(m, t):
        for k, peer in urgent:
            r.outbox[m, lax.rem(t, 2), k] = product(m, t, peer).astype(B16)
            give(m, t, k, peer).start()
        r.own_part[m] = product(m, t, place) + from_decoder(m, t - 1)
        spread_gates(m, t)

    def incoming(m, t):
        total = r.own_part[m]
        for k in range(len(peers)):
            give(m, t, k, peers[k]).wait_recv()
            total = total + r.inbox[m, lax.rem(t, 2), k].astype(F32)
        return total

    def sent(m, t):
        for k in range(len(peers)):
            give(m, t, k, peers[k]).wait_send()

    def retreat(m, t):
        slope = slopes(m, t, cells[m][t - 1])
        gate_grads(m, t, slope, incoming(m, t + 1), r.cell_grad[m])
        send_products(m, t)
        sent(m, t + 1)

    def first(m):
        t = ends[m] - 1
        gate_grads(m, t, slopes(m, t, cells[m][t - 1]), from_decoder(m, t), None)
        send_products(m, t)

    def last(m):
        slope = slopes(m, 0, None)
        gate_grads(m, 0, slope, incoming(m, 1), r.cell_grad[m])
        spread_gates(m, 0)
        sent(m, 1)

    def lagged(work, m, step):
        if m == 0:
            pl.when(step >= 2)(lambda: work(0, length // 2 + 1 - step))
        else:
            ready = jnp.logical_and(step >= 3, lax.rem(step, 2) == 1)
            pl.when(ready)(lambda: work(1, half_len // 2 - 1 - (step - 3) // 2))

    final = half_len - 1
    first(0)
    first(1)
    retreat(0, length - 2)

    def turn(step, carry):
        retreat(0, length - 1 - 2 * step)
        lagged(fetch, 0, step)
        lagged(fetch, 1, step)
        retreat(1, half_len - 1 - step)
        retreat(0, length - 2 - 2 * step)
        lagged(accumulate, 0, step)
        lagged(accumulate, 1, step)
        out_steps(0, step - 1)
        return carry

    lax.fori_loop(1, final, turn, 0)
    retreat(0, 1)
    lagged(fetch, 0, final)
    lagged(fetch, 1, final)
    last(1)
    last(0)
    fetch(0, 1)
    accumulate(0, 2)
    accumulate(1, 1)
    accumulate(0, 1)
    for m in range(2):
        for j in range(groups - 1):
            out_share(m, j).wait()
    for m in range(2):
        r.grad_out[:, m, :] = r.out_total[m, :vocab, :units]
        r.grad_bout[m : m + 1, :] = r.out_total[m, :, units:].T[:1, :vocab]
    fetch(1, 0)
    fetch(0, 0)
    accumulate(1, 0)
    accumulate(0, 0)

    depth = r.rec_grad.shape[2]
    kept = r.in_all.shape[2]

    def swap(m, g, i):
        source, target = (
            (r.rec_sums.at[m, span(1 - core, depth), pl.ds(g * units, units)], r.rec_grad),
            (r.in_sums.at[m, pl.ds(0, kept), pl.ds(g * units, units)], r.in_all),
        )[i]
        target = target.at[m, 2 * core + g]
        return to_group(source, target, r.swap_send.at[i, m, g], r.swap_recv.at[i, m, g], sibling)

    def keep(m, g):
        return pltpu.make_async_copy(
            r.rec_sums.at[m, span(core, depth), pl.ds(g * units, units)],
            r.rec_grad.at[m, 2 * core + g],
            r.keep_sem.at[m, g],
        )

    half = r.embed_half.shape[1]
    slice_rows = half // count
    pair_copy = to_group(
        r.embed_part.at[:, span(1 - core, half)],
        r.embed_half,
        r.embed_send.at[0],
        r.embed_recv.at[0],
        sibling,
    )
    cells_of = [(m, g) for m in range(2) for g in range(2)]
    for m, g in cells_of:
        swap(m, g, 1).start()
    pair_copy.start()
    for m, g in cells_of:
        swap(m, g, 0).start()
        keep(m, g).start()
        r.in_all[m, 2 * core + g] = r.in_sums[m, :kept, g * units : (g + 1) * units]
    pair_copy.wait()
    r.embed_half[...] += r.embed_part[:, span(core, half)]
    own_slice = r.embed_full.at[:, pl.ds(pl.multiple_of(core * half + place * slice_rows, 8), slice_rows)]

    def embed_reduce(k):
        return to_peer(
            r.embed_half.at[:, span(peers[k], slice_rows)],
            r.embed_inbox.at[k],
            r.reduce_send.at[k],
            r.reduce_recv.at[k],
            peers[k],
        )

    def embed_gather(k):
        return to_peer(own_slice, own_slice, r.gather_send.at[k], r.gather_recv.at[k], peers[k])

    for k in reversed(range(len(peers))):
        embed_reduce(k).start()
    total = r.embed_half[:, span(place, slice_rows)]
    for k in range(len(peers)):
        embed_reduce(k).wait()
        total = total + r.embed_inbox[k]
    own_slice[...] = total
    for k in reversed(range(len(peers))):
        embed_gather(k).start()
    for m, g in cells_of:
        swap(m, g, 1).wait()
    for m in range(2):
        for g in range(4):
            r.grad_in[m, :, g, :] = r.in_all[m, g, :embed]
    r.grad_bias[...] = r.in_all[:, :, embed, :]
    for m, g in cells_of:
        swap(m, g, 0).wait()
        keep(m, g).wait()
    for m in range(2):
        for j in range(groups - 1):
            part = wides[m].at[:, 0]
            to_group(part, part, r.wide_send.at[m, j], r.wide_recv.at[m, 0], others[j]).wait_send()
    for k in range(len(peers)):
        embed_gather(k).wait()
    whole_half = r.embed_full.at[:, span(core, half)]
    pair_copy = to_group(whole_half, whole_half, r.embed_send.at[1], r.embed_recv.at[1], sibling)
    pair_copy.start()
    pair_copy.wait()
    for m in range(2):
        r.grad_embed[:, m, :] = r.embed_full[m, :vocab, :embed]


def run_step(count, groups, factor, char_ids, prefix, embedding, w_in, w_rec, gate_bias, w_out, b_out):
    seq_dev, length = char_ids.shape
    half_len = length // 2
    units, shard_units = w_rec.shape[2:]
    vocab, embed = embedding.shape[1:]
    rows = seq_dev * count
    wide = units // (groups // 2)
    depth = -(-(embed + 1) // LANES) * LANES
    lanes = -(-vocab // LANES) * LANES
    reduced = -(-vocab // (16 * count)) * 8 * count
    padded = 2 * reduced
    piece = lanes // groups
    links = count - 1
    far = groups - 1
    dma = pltpu.SemaphoreType.DMA
    ins = dict(
        chars=(char_ids, VMEM),
        prefix=(prefix[None], VMEM),
        embedding=(embedding.transpose(1, 0, 2), VMEM),
        w_in=(w_in.transpose(0, 2, 1, 3), VMEM),
        gate_bias=(gate_bias, VMEM),
        w_out=(w_out.transpose(2, 0, 1), VMEM),
        b_out=(b_out, VMEM),
        w_rec=(w_rec, ANYWHERE),
    )
    outs = dict(
        grad_embed=((vocab, 2, embed), F32, VMEM),
        grad_in=((2, embed, 4, shard_units), F32, VMEM),
        rec_grad=((2, 4, wide // 2, shard_units), F32, ANYWHERE),
        grad_bias=((2, 4, shard_units), F32, VMEM),
        grad_out=((vocab, 2, shard_units), F32, VMEM),
        grad_bout=((2, vocab), F32, VMEM),
        past_front=((length, groups, rows, wide), B16, ANYWHERE),
        past_back=((half_len, groups, rows, wide), B16, ANYWHERE),
        wide_front=((length, groups, rows, 2 * shard_units), B16, ANYWHERE),
        wide_back=((half_len, groups, rows, 2 * shard_units), B16, ANYWHERE),
    )
    arrays = dict(
        weights=(w_rec.shape, B16),
        out_bias=((2, lanes), F32),
        out_full=((2, count, groups, shard_units // groups, lanes), B16),
        id_blocks=((groups, count, max(8, seq_dev), LANES), jnp.int32),
        group_ids=((rows, LANES), jnp.int32),
        every_ids=((groups * rows, LANES), jnp.int32),
        blank=((groups, rows, wide), B16),
        full_front=((length, rows, units), B16),
        full_back=((half_len, rows, units), B16),
        acts_front=((length, 4, rows, shard_units), F32),
        acts_back=((half_len, 4, rows, shard_units), F32),
        cell_front=((length, rows, shard_units), F32),
        cell_back=((half_len, rows, shard_units), F32),
        logits_front=((length, rows, lanes), B16),
        logits_back=((half_len, rows, lanes), B16),
        out_sums=((2, lanes, shard_units + LANES), F32),
        out_inbox=((2, far, piece, shard_units + LANES), F32),
        out_total=((2, lanes, shard_units + LANES), F32),
        outbox=((2, 2, links, rows, shard_units), B16),
        inbox=((2, 2, links, rows, shard_units), B16),
        own_part=((2, rows, shard_units), F32),
        cell_grad=((2, rows, shard_units), F32),
        rec_sums=((2, wide, 2 * shard_units), F32),
        in_sums=((2, depth, 2 * shard_units), F32),
        in_all=((2, 4, -(-(embed + 1) // 8) * 8, shard_units), F32),
        table=((2, padded, depth), B16),
        inputs=((2, 4, depth, shard_units), B16),
        out_own=((2, lanes, shard_units), B16),
        embed_part=((2, padded, depth), F32),
        embed_half=((2, reduced, depth), F32),
        embed_full=((2, padded, depth), F32),
        embed_inbox=((links, 2, reduced // count, depth), F32),
        wide_slot=((2, 2, 2, groups, rows, 2 * shard_units), B16),
        past_slot=((2, 2, 2, groups, rows, wide), B16),
    )
    semaphores = dict(
        load_sem=(2,),
        id_send=(links,),
        id_recv=(links,),
        ids_send=(far,),
        ids_recv=(far,),
        share_send=(2 * links,),
        share_recv=(2 * links,),
        all_send=(far, links),
        all_recv=(far, links),
        past_send=(2, far),
        past_recv=(2, far),
        past_local=(2,),
        hidden_send=(2, 2, links),
        hidden_recv=(2, 2, links),
        out_send=(2, far),
        out_recv=(2, far),
        total_send=(2, far),
        total_recv=(2, far),
        wide_send=(2, far),
        wide_recv=(2, length // 2),
        wide_local=(2, length // 2),
        fetch_sem=(2, 2, 2),
        grad_send=(2, 2, links),
        grad_recv=(2, 2, links),
        swap_send=(2, 2, 2),
        swap_recv=(2, 2, 2),
        keep_sem=(2, 2),
        embed_send=(2,),
        embed_recv=(2,),
        reduce_send=(links,),
        reduce_recv=(links,),
        gather_send=(links,),
        gather_recv=(links,),
    )
    scratch = {key: pltpu.VMEM(shape, kind) for key, (shape, kind) in arrays.items()}
    scratch |= {key: dma(shape) for key, shape in semaphores.items()}
    body = functools.partial(step_body, count, groups, factor)
    return call(body, "lstm_step", ins, outs, scratch, 2, 10**11)


def shifted(values):
    return jnp.concatenate([jnp.zeros_like(values[:1]), values[:-1]], axis=0)


def reduced_grads(ran, gates, embedding, w_in, ids, group_size):
    embed = embedding.shape[2]

    def per_model(full, grads, ids, m):
        grads = grads.reshape(grads.shape[0], group_size, 4, -1)
        rec = jnp.einsum("tbk,tbgn->gkn", shifted(full), grads, preferred_element_type=F32)
        spots = one_hot(ids, embedding.shape[1], B16)
        x = jnp.einsum("tbv,ve->tbe", spots, embedding[m], preferred_element_type=F32).astype(B16)
        in_grad = jnp.einsum("tbe,tbgn->gen", x, grads, preferred_element_type=F32)
        bias = jnp.sum(grads, axis=(0, 1), dtype=F32)
        dx = jnp.einsum("tbgn,gen->tbe", grads, w_in[m], preferred_element_type=F32)
        embed_grad = jnp.einsum("tbv,tbe->ve", spots.astype(F32), dx, precision=PRECISE)
        return rec, in_grad, bias, embed_grad

    parts = (
        per_model(ran.full_front, gates.gates_front, ids[0], 0),
        per_model(ran.full_back, gates.gates_back, ids[1], 1),
    )
    rec, in_grad, bias, embed_grad = (jnp.stack(values) for values in zip(*parts))
    rec_grad = lax.psum_scatter(rec, "rep", scatter_dimension=2, tiled=True)
    in_sum, bias_sum = lax.psum((in_grad, bias), "rep")
    embed_sum = lax.psum(embed_grad, ("rep", "shard"))
    return embed_sum, in_sum, rec_grad, bias_sum


def shards(char_ids, prefix, embedding, w_in, w_rec, gate_bias, w_out, b_out):
    seq_dev, length = char_ids.shape
    half_len = length // 2
    vocab_size, embed = embedding.shape[1:]
    shard_units = w_rec.shape[3]
    count, groups = lax.axis_size("shard"), lax.axis_size("rep")
    group_size = seq_dev * count
    factor = 1.0 / math.sqrt(groups * count * seq_dev * length)
    if groups == 8 and count == 4 and length == 48:
        done = run_step(
            count, groups, factor, char_ids, prefix, embedding, w_in, w_rec, gate_bias, w_out, b_out
        )
        return (
            done.grad_embed.transpose(1, 0, 2),
            done.grad_in.transpose(0, 2, 1, 3),
            done.rec_grad,
            done.grad_bias,
            done.grad_out.transpose(1, 2, 0),
            done.grad_bout,
        )
    own_ids = jnp.concatenate([char_ids, prefix[:, None]], axis=1)
    own_ids = jnp.pad(own_ids, ((0, 0), (0, LANES - length - 1)))
    full_out = lax.all_gather(w_out, "shard", axis=1, tiled=True)
    depth = -(-(embed + 1) // LANES) * LANES
    padded = -(-vocab_size // LANES) * LANES
    table = jnp.pad(embedding, ((0, 0), (0, 0), (0, 1)), constant_values=1)
    table = jnp.pad(table, ((0, 0), (0, padded - vocab_size), (0, depth - embed - 1)))
    inputs = jnp.pad(w_in, ((0, 0), (0, 0), (0, depth - embed), (0, 0)))
    ran = run_forward(count, length, own_ids, table, inputs, gate_bias.astype(F32), w_rec)
    group_chars, group_prefix = ran.group_ids[:, :length], ran.group_ids[:, length]
    front_in = group_chars.T
    front_target = jnp.concatenate([group_chars[:, 1:], group_chars[:, :1]], axis=1).T
    timeline = jnp.arange(length, dtype=jnp.int32)[:, None]
    front_active = jnp.broadcast_to((timeline < length - 1).astype(F32), (length, group_size))
    reverse_steps = jnp.arange(half_len, dtype=jnp.int32)[:, None]

    def back_pick(offset):
        spot = jnp.maximum(group_prefix[None, :] - offset - reverse_steps, 0)
        chosen = one_hot(spot, length, jnp.int32) * group_chars[None]
        return jnp.sum(chosen, axis=-1)

    back_target = back_pick(2)
    back_active = (reverse_steps <= group_prefix[None, :] - 2).astype(F32)
    first_unit = lax.axis_index("shard") * shard_units

    def decode(full, m, target, active):
        rows = full.reshape(-1, full.shape[-1])
        logits = dot(rows, full_out[m]) + b_out[m].astype(F32)
        grad = loss_grad(logits, target.reshape(-1), active.reshape(-1), factor)
        dec = dot_last(grad, w_out[m])
        own = lax.dynamic_slice_in_dim(rows, first_unit, shard_units, axis=1)
        out_grad = dot_first(own, grad)
        bout = jnp.sum(grad, axis=0, dtype=F32)
        return dec.reshape(full.shape[0], group_size, shard_units), out_grad, bout

    front_dec, front_out_grad, front_bout = decode(ran.full_front, 0, front_target, front_active)
    back_dec, back_out_grad, back_bout = decode(ran.full_back, 1, back_target, back_active)
    out_and_bout = jnp.stack(
        [
            jnp.concatenate([front_out_grad, front_bout[None]], axis=0),
            jnp.concatenate([back_out_grad, back_bout[None]], axis=0),
        ]
    )
    out_and_bout = lax.psum(out_and_bout, "rep")
    out_sum, bout_sum = out_and_bout[:, :shard_units], out_and_bout[:, shard_units]
    done = run_backward(count, ran, (front_dec, back_dec))
    embed_sum, in_sum, rec_grad, bias_sum = reduced_grads(
        ran, done, embedding, w_in, (front_in, back_pick(1)), group_size
    )
    return (embed_sum, in_sum, rec_grad, bias_sum, out_sum, bout_sum)


def solution(mesh):
    in_specs = (
        P(("rep", "shard"), None),
        P(("rep", "shard")),
        P(),
        P(None, None, None, "shard"),
        P(None, None, None, "shard"),
        P(None, None, "shard"),
        P(None, "shard", None),
        P(),
    )
    out_specs = (
        P(),
        P(None, None, None, "shard"),
        P(None, None, "rep", "shard"),
        P(None, None, "shard"),
        P(None, "shard", None),
        P(),
    )
    return jax.shard_map(shards, mesh=mesh, in_specs=in_specs, out_specs=out_specs, check_vma=False)
```

time: 542 us -> 485 us (0.89)
  Pallas kernels: 487 us -> 473 us
  between operations: 14.3 us -> 0.65 us
  matrix products: 11.2 us -> 0 us
  local copies, waits for them, and re-layouts: 21.7 us -> 11.5 us
  other arithmetic: 6.67 us -> 0 us
    pallas_call x2 -> x1, Pallas kernels: 487 us -> 473 us  [call(): pl.pallas_call(kernel, out_shape=tuple((jax.ShapeDtypeStruct(shape, kind)...]
    dot_general x6 -> x0, matrix products: 11.2 us -> none  [the longest x2 5.41 us: dot(): return jnp.dot(left, right, preferred_element_type=F32)]
    slice x7 -> x0, local copies, waits for them, and re-layouts: 5.51 us -> none  [the longest x2 2.56 us: shards(): in_sum, bias_sum = (done.in_grad[:, :, :embed], done.in_grad[:, :, embed])]
    unnamed x32 -> x12, local copies, waits for them, and re-layouts: 12.4 us -> 11.5 us
  transfers between devices with their start and end apart: 2 -> 0, of which waited for: 0 -> 0; matrix products, arithmetic and copies ran while one was open for 3% -> 0% of each run, Pallas kernels for 90% -> 0%
where the time goes in v4:
time: 485 us
  Pallas kernels  473 us (98%)
  local copies, waits for them, and re-layouts  11.5 us (2%)
    pallas_call x1, Pallas kernels, call(): pl.pallas_call(kernel, out_shape=tuple((jax.ShapeDtypeStruct(shape, kind)...  473 us
    unnamed x12, local copies, waits for them, and re-layouts  11.5 us

profile of v4, /device:TPU:0, one launch (start us, length us, event | category | flops | bytes accessed | tf_op | source)
XLA Modules:
  0.0 485.1 jit_solution(14418236944271684342)
XLA Ops:
  0.6 473.0 %lstm_step.1 = (f32[275,2,100]{2,1,0:T(2,128)}, f32[2,100,4,512]{3,2,1,0:T(4,128)}, f32[2,4,256,512]{3,2,1,0:T(8,128)}, f32[2,4,512]{2,1,0:T(4,128)}, f32[275,2,...) custom-call(s32[4,48]{1,0:T(4,128)} %refs_0_.1, ...), custom_call_target="tpu_custom_call" | custom-call | flops 99999997952 | bytes 52428800 | tf_op jit(solution)/shard_map/lstm_step/pallas_call | solution.py:97
  473.6 1.7 copy.20
  475.3 2.9 copy.21
  478.2 0.0 copy-start.1
  478.2 0.0 copy-start
  478.2 0.0 copy-start.2
  478.2 4.7 copy.22
  482.9 0.0 copy-done.1
  482.9 0.6 copy.23
  483.5 0.0 copy-done
  483.5 1.0 copy.24
  484.5 0.0 copy-done.2
  484.5 0.6 copy.25
Async XLA Ops:
  478.2 4.7 copy-start.1
  478.2 5.3 %copy-start = (f32[275,2,512]{2,1,0:T(2,128)S(1)}, f32[275,2,512]{2,1,0:T(2,128)}, u32[]{:S(2)}) copy-start(f32[275,2,512]{2,1,0:T(2,128)} %get-tuple-element.16) | copy-start | bytes 3379204
  478.2 6.3 %copy-start.2 = (f32[2,275]{1,0:T(2,128)S(1)}, f32[2,275]{1,0:T(2,128)}, u32[]{:S(2)}) copy-start(f32[2,275]{1,0:T(2,128)} %get-tuple-element.29) | copy-start | bytes 6604

commit v5 on v4

--- a/solution.py
+++ b/solution.py
@@ -479,40 +479,41 @@
     r.id_blocks[group, place, :seq_dev, length : length + 1] = jnp.sum(
         jnp.where(diagonal, stops_across, 0), axis=1, keepdims=True
     )
+    pl.semaphore_wait(barrier, len(peers) + len(others))
+
+    def id_copy(k):
+        block = r.id_blocks.at[group, place]
+        return to_peer(block, block, r.id_send.at[k], r.id_recv.at[k], peers[k])
+
+    def id_spread(j):
+        block = r.id_blocks.at[group]
+        return to_group(block, block, r.ids_send.at[j], r.ids_recv.at[j], others[j])
+
+    for k in range(len(peers)):
+        id_copy(k).start()
     lane = lax.broadcasted_iota(jnp.int32, r.table.shape, 2)
     r.table[...] = jnp.where(lane == embed, 1.0, 0.0).astype(B16)
     r.inputs[...] = jnp.zeros_like(r.inputs)
-    r.out_own[...] = jnp.zeros_like(r.out_own)
     for m in range(2):
         r.table[m, :vocab, :embed] = r.embedding[:, m, :]
-        r.out_own[m, :vocab] = r.w_out[:, m, :]
         for g in range(4):
             r.inputs[m, g, :embed] = r.w_in[m, :, g, :]
-    r.out_bias[...] = jnp.full_like(r.out_bias, -1e30)
-    r.out_bias[:, :vocab] = r.b_out[...].astype(F32)
-    share = units // groups
-    for m in range(2):
-        r.out_full[m, place] = r.out_own[m].T.reshape(groups, share, -1)
-    r.blank[...] = jnp.zeros_like(r.blank)
-    pl.semaphore_wait(barrier, len(peers) + len(others))
-
-    def id_copy(k):
-        block = r.id_blocks.at[group, place]
-        return to_peer(block, block, r.id_send.at[k], r.id_recv.at[k], peers[k])
-
-    def id_spread(j):
-        block = r.id_blocks.at[group]
-        return to_group(block, block, r.ids_send.at[j], r.ids_recv.at[j], others[j])
-
-    for k in range(len(peers)):
-        id_copy(k).start()
+
     blanks = [pltpu.make_async_copy(r.blank, pasts[m].at[0], r.past_local.at[m]) for m in range(2)]
-    for copy in blanks:
-        copy.start()
-    r.in_sums[...] = jnp.zeros_like(r.in_sums)
-    r.embed_part[...] = jnp.zeros_like(r.embed_part)
-    r.rec_sums[...] = jnp.zeros_like(r.rec_sums)
-    r.out_sums[...] = jnp.zeros_like(r.out_sums)
+
+    def prepare_decoder():
+        r.out_own[...] = jnp.zeros_like(r.out_own)
+        r.out_bias[...] = jnp.full_like(r.out_bias, -1e30)
+        r.out_bias[:, :vocab] = r.b_out[...].astype(F32)
+        for m in range(2):
+            r.out_own[m, :vocab] = r.w_out[:, m, :]
+            r.out_full[m, place] = r.out_own[m].T.reshape(groups, units // groups, -1)
+        r.out_sums[...] = jnp.zeros_like(r.out_sums)
+
+    def prepare_sums():
+        r.in_sums[...] = jnp.zeros_like(r.in_sums)
+        r.embed_part[...] = jnp.zeros_like(r.embed_part)
+        r.rec_sums[...] = jnp.zeros_like(r.rec_sums)
 
     def share_copy(n):
         k, m = len(peers) - 1 - n // 2, n % 2
@@ -665,65 +666,6 @@
         ready = jnp.logical_and(n > groups, n < 2 * groups)
         pl.when(ready)(lambda: out_share(m, n - groups - 1).start())
 
-    for k in range(len(peers)):
-        id_copy(k).wait()
-    for s in range(count):
-        r.group_ids[s * seq_dev : (s + 1) * seq_dev] = r.id_blocks[group, s, :seq_dev]
-    for j in range(len(others)):
-        id_spread(j).start()
-    for copy in blanks:
-        copy.wait()
-    for m in range(2):
-        finish(m, 0, start_sums(m, 0), None)
-    for load in loads:
-        load.wait()
-
-    def both(t, carry):
-        advance(0, t)
-        advance(1, t)
-        send_shares(t)
-        return carry
-
-    back_chunks = half_len // stretch
-    blocks = 4 * count
-    assert half_len % stretch == 0 and length == 2 * half_len and half_len % 2 == 0
-    assert first_spread + groups - 1 <= half_len and blocks <= half_len
-    assert back_chunks + 2 * groups <= half_len
-
-    def front_only(t, carry):
-        advance(0, t)
-        n = t - half_len
-        pl.when(n < blocks)(lambda: turn_block(1, n // count, lax.rem(n, count)))
-        pl.when(n < back_chunks)(lambda: decode(1, n))
-        begun = n >= back_chunks
-        early = jnp.logical_and(begun, stretch * (n - back_chunks + 1) <= t)
-        late = jnp.logical_and(stretch * (n - back_chunks + 1) > t, lax.rem(t, stretch) == 0)
-        pl.when(early)(lambda: decode(0, n - back_chunks))
-        pl.when(jnp.logical_and(begun, late))(lambda: decode(0, t // stretch - 1))
-        out_steps(1, n - back_chunks)
-        return carry
-
-    def settle(m):
-        for k in range(len(peers)):
-            exchange(m, ends[m] - 1, k, peers[k]).wait()
-
-    lax.fori_loop(1, half_len, both, 0)
-    settle(1)
-    for j in range(groups - 1):
-        for k in range(len(peers)):
-            share_spread(j, k).wait()
-    lax.fori_loop(half_len, length, front_only, 0)
-    for g in range(4):
-        for p in range(count):
-            turn_block(0, g, p)
-    settle(0)
-    decode(0, length // stretch - 1)
-    finish_past(0, length - 1)
-    finish_past(1, half_len - 1)
-    for j in range(len(others)):
-        id_spread(j).wait()
-    r.every_ids[...] = r.id_blocks[:, :, :seq_dev].reshape(r.every_ids.shape)
-
     gates = fulls
 
     def spread_gates(m, t):
@@ -860,50 +802,6 @@
         spread_gates(m, 0)
         sent(m, 1)
 
-    def lagged(work, m, step):
-        if m == 0:
-            pl.when(step >= 2)(lambda: work(0, length // 2 + 1 - step))
-        else:
-            ready = jnp.logical_and(step >= 3, lax.rem(step, 2) == 1)
-            pl.when(ready)(lambda: work(1, half_len // 2 - 1 - (step - 3) // 2))
-
-    final = half_len - 1
-    first(0)
-    first(1)
-    retreat(0, length - 2)
-
-    def turn(step, carry):
-        retreat(0, length - 1 - 2 * step)
-        lagged(fetch, 0, step)
-        lagged(fetch, 1, step)
-        retreat(1, half_len - 1 - step)
-        retreat(0, length - 2 - 2 * step)
-        lagged(accumulate, 0, step)
-        lagged(accumulate, 1, step)
-        out_steps(0, step - 1)
-        return carry
-
-    lax.fori_loop(1, final, turn, 0)
-    retreat(0, 1)
-    lagged(fetch, 0, final)
-    lagged(fetch, 1, final)
-    last(1)
-    last(0)
-    fetch(0, 1)
-    accumulate(0, 2)
-    accumulate(1, 1)
-    accumulate(0, 1)
-    for m in range(2):
-        for j in range(groups - 1):
-            out_share(m, j).wait()
-    for m in range(2):
-        r.grad_out[:, m, :] = r.out_total[m, :vocab, :units]
-        r.grad_bout[m : m + 1, :] = r.out_total[m, :, units:].T[:1, :vocab]
-    fetch(1, 0)
-    fetch(0, 0)
-    accumulate(1, 0)
-    accumulate(0, 0)
-
     depth = r.rec_grad.shape[2]
     kept = r.in_all.shape[2]
 
@@ -922,69 +820,236 @@
             r.keep_sem.at[m, g],
         )
 
+    def start_swaps(m):
+        for g in range(2):
+            swap(m, g, 1).start()
+        for g in range(2):
+            swap(m, g, 0).start()
+            keep(m, g).start()
+            r.in_all[m, 2 * core + g] = r.in_sums[m, :kept, g * units : (g + 1) * units]
+
+    def finish_inputs(m):
+        for g in range(2):
+            swap(m, g, 1).wait()
+        for g in range(4):
+            r.grad_in[m, :, g, :] = r.in_all[m, g, :embed]
+        r.grad_bias[m] = r.in_all[m, :, embed, :]
+
+    def finish_swaps(m):
+        for g in range(2):
+            swap(m, g, 0).wait()
+            keep(m, g).wait()
+
     half = r.embed_half.shape[1]
     slice_rows = half // count
-    pair_copy = to_group(
-        r.embed_part.at[:, span(1 - core, half)],
-        r.embed_half,
-        r.embed_send.at[0],
-        r.embed_recv.at[0],
-        sibling,
-    )
-    cells_of = [(m, g) for m in range(2) for g in range(2)]
-    for m, g in cells_of:
-        swap(m, g, 1).start()
-    pair_copy.start()
-    for m, g in cells_of:
-        swap(m, g, 0).start()
-        keep(m, g).start()
-        r.in_all[m, 2 * core + g] = r.in_sums[m, :kept, g * units : (g + 1) * units]
-    pair_copy.wait()
-    r.embed_half[...] += r.embed_part[:, span(core, half)]
-    own_slice = r.embed_full.at[:, pl.ds(pl.multiple_of(core * half + place * slice_rows, 8), slice_rows)]
-
-    def embed_reduce(k):
+
+    def embed_pair(m):
+        return to_group(
+            r.embed_part.at[m, span(1 - core, half)],
+            r.embed_half.at[m],
+            r.embed_send.at[m, 0],
+            r.embed_recv.at[m, 0],
+            sibling,
+        )
+
+    def embed_reduce(m, k):
         return to_peer(
-            r.embed_half.at[:, span(peers[k], slice_rows)],
-            r.embed_inbox.at[k],
-            r.reduce_send.at[k],
-            r.reduce_recv.at[k],
+            r.embed_half.at[m, span(peers[k], slice_rows)],
+            r.embed_inbox.at[m, k],
+            r.reduce_send.at[m, k],
+            r.reduce_recv.at[m, k],
             peers[k],
         )
 
-    def embed_gather(k):
-        return to_peer(own_slice, own_slice, r.gather_send.at[k], r.gather_recv.at[k], peers[k])
-
-    for k in reversed(range(len(peers))):
-        embed_reduce(k).start()
-    total = r.embed_half[:, span(place, slice_rows)]
+    def own_slice(m):
+        first_row = pl.multiple_of(core * half + place * slice_rows, 8)
+        return r.embed_full.at[m, pl.ds(first_row, slice_rows)]
+
+    def embed_gather(m, k):
+        return to_peer(
+            own_slice(m), own_slice(m), r.gather_send.at[m, k], r.gather_recv.at[m, k], peers[k]
+        )
+
+    def embed_return(m):
+        whole = r.embed_full.at[m, span(core, half)]
+        return to_group(whole, whole, r.embed_send.at[m, 1], r.embed_recv.at[m, 1], sibling)
+
+    def embed_stage(m, stage):
+        if stage == 0:
+            embed_pair(m).start()
+        elif stage == 1:
+            embed_pair(m).wait()
+            r.embed_half[m] += r.embed_part[m, span(core, half)]
+            for k in reversed(range(len(peers))):
+                embed_reduce(m, k).start()
+        elif stage == 2:
+            total = r.embed_half[m, span(place, slice_rows)]
+            for k in range(len(peers)):
+                embed_reduce(m, k).wait()
+                total = total + r.embed_inbox[m, k]
+            own_slice(m)[...] = total
+            for k in reversed(range(len(peers))):
+                embed_gather(m, k).start()
+        elif stage == 3:
+            for k in range(len(peers)):
+                embed_gather(m, k).wait()
+            embed_return(m).start()
+        else:
+            embed_return(m).wait()
+            r.grad_embed[:, m, :] = r.embed_full[m, :vocab, :embed]
+
     for k in range(len(peers)):
-        embed_reduce(k).wait()
-        total = total + r.embed_inbox[k]
-    own_slice[...] = total
-    for k in reversed(range(len(peers))):
-        embed_gather(k).start()
-    for m, g in cells_of:
-        swap(m, g, 1).wait()
+        id_copy(k).wait()
+    for s in range(count):
+        r.group_ids[s * seq_dev : (s + 1) * seq_dev] = r.id_blocks[group, s, :seq_dev]
+    for j in range(len(others)):
+        id_spread(j).start()
     for m in range(2):
-        for g in range(4):
-            r.grad_in[m, :, g, :] = r.in_all[m, g, :embed]
-    r.grad_bias[...] = r.in_all[:, :, embed, :]
-    for m, g in cells_of:
-        swap(m, g, 0).wait()
-        keep(m, g).wait()
+        finish(m, 0, start_sums(m, 0), None)
+    r.blank[...] = jnp.zeros_like(r.blank)
+    for copy in blanks:
+        copy.start()
+    prepare_decoder()
+    for copy in blanks:
+        copy.wait()
+    for load in loads:
+        load.wait()
+
+    shared = first_spread + groups
+
+    def both(t, carry):
+        advance(0, t)
+        advance(1, t)
+        send_shares(t)
+        pl.when(t == 2)(prepare_sums)
+
+        @pl.when(t == shared)
+        def _():
+            for j in range(groups - 1):
+                for k in range(len(peers)):
+                    share_spread(j, k).wait()
+
+        chunk = t - shared - 1
+        pl.when(jnp.logical_and(chunk >= 0, stretch * (chunk + 1) <= t))(lambda: decode(0, chunk))
+        return carry
+
+    decoded = 0
+    while stretch * (decoded + 1) <= shared + 1 + decoded and shared + 1 + decoded < half_len:
+        decoded += 1
+
+    def settle(m):
+        for k in range(len(peers)):
+            exchange(m, ends[m] - 1, k, peers[k]).wait()
+
+    back_chunks = half_len // stretch
+    blocks = 4 * count
+    begin = 3
+    back_pairs = half_len // 2
+    front_pairs = length // 2
+    assert half_len % stretch == 0 and length == 2 * half_len and half_len % 2 == 0
+    assert first_spread + groups - 1 <= half_len
+    assert back_chunks == 2 * begin and blocks <= 6 * begin and groups < half_len // 2
+
+    def front_only(t, carry):
+        advance(0, t)
+        n = t - half_len
+
+        @pl.when(n < begin)
+        def _():
+            for i in range(2):
+                decode(1, back_chunks - 1 - 2 * n - i)
+            for i in range(6):
+                block = 6 * n + i
+                pl.when(block < blocks)(lambda: turn_block(1, block // count, lax.rem(block, count)))
+
+        @pl.when(n == begin)
+        def _():
+            finish_past(1, half_len - 1)
+            first(1)
+
+        pl.when(n > begin)(lambda: retreat(1, half_len - 1 - (n - begin)))
+        begun = n >= begin
+        chunk = n - begin + decoded
+        early = jnp.logical_and(begun, stretch * (chunk + 1) <= t)
+        late = jnp.logical_and(stretch * (chunk + 1) > t, lax.rem(t, stretch) == 0)
+        pl.when(early)(lambda: decode(0, chunk))
+        pl.when(jnp.logical_and(begun, late))(lambda: decode(0, t // stretch - 1))
+        behind = n - begin - 5
+        even = jnp.logical_and(behind >= 0, lax.rem(n - begin, 2) == 1)
+        odd = jnp.logical_and(behind >= 1, lax.rem(n - begin, 2) == 0)
+        pl.when(even)(lambda: fetch(1, back_pairs - 1 - behind // 2))
+        pl.when(odd)(lambda: accumulate(1, back_pairs - 1 - behind // 2))
+        return carry
+
+    lax.fori_loop(1, half_len, both, 0)
+    settle(1)
+    for j in range(len(others)):
+        id_spread(j).wait()
+    r.every_ids[...] = r.id_blocks[:, :, :seq_dev].reshape(r.every_ids.shape)
+    lax.fori_loop(half_len, length, front_only, 0)
+    for g in range(4):
+        for p in range(count):
+            turn_block(0, g, p)
+    settle(0)
+    decode(0, length // stretch - 1)
+    finish_past(0, length - 1)
+
+    first(0)
+    retreat(1, begin - 1)
+    retreat(0, length - 2)
+    retreat(1, begin - 2)
+    fetched = (half_len - begin - 5) // 2
+    left = back_pairs - fetched
+    after = left + 2
+
+    def turn(step, carry):
+        retreat(0, length - 1 - 2 * step)
+        pl.when(step == 1)(lambda: last(1))
+        pl.when(step >= 3)(lambda: fetch(0, front_pairs + 2 - step))
+        remaining = jnp.logical_and(step >= 2, step < left + 2)
+        pl.when(remaining)(lambda: fetch(1, left + 1 - step))
+        for stage in range(5):
+            pl.when(step == after + stage)(lambda stage=stage: embed_stage(1, stage))
+        pl.when(step == after)(lambda: start_swaps(1))
+        pl.when(step == after + 2)(lambda: finish_inputs(1))
+        retreat(0, length - 2 - 2 * step)
+        pl.when(step >= 3)(lambda: accumulate(0, front_pairs + 2 - step))
+        pl.when(remaining)(lambda: accumulate(1, left + 1 - step))
+        out_steps(0, step - 1)
+        out_steps(1, step - 1)
+        return carry
+
+    final = half_len - 1
+    assert begin == 3 and after + 5 <= final
+    lax.fori_loop(1, final, turn, 0)
+    retreat(0, 1)
+    fetch(0, 3)
+    last(0)
+    fetch(0, 2)
+    accumulate(0, 3)
+    accumulate(0, 2)
+    fetch(0, 1)
+    for m in range(2):
+        for j in range(groups - 1):
+            out_share(m, j).wait()
+        r.grad_out[:, m, :] = r.out_total[m, :vocab, :units]
+        r.grad_bout[m : m + 1, :] = r.out_total[m, :, units:].T[:1, :vocab]
+    finish_swaps(1)
+    accumulate(0, 1)
+    fetch(0, 0)
+    accumulate(0, 0)
+    embed_stage(0, 0)
+    start_swaps(0)
+    embed_stage(0, 1)
     for m in range(2):
         for j in range(groups - 1):
             part = wides[m].at[:, 0]
             to_group(part, part, r.wide_send.at[m, j], r.wide_recv.at[m, 0], others[j]).wait_send()
-    for k in range(len(peers)):
-        embed_gather(k).wait()
-    whole_half = r.embed_full.at[:, span(core, half)]
-    pair_copy = to_group(whole_half, whole_half, r.embed_send.at[1], r.embed_recv.at[1], sibling)
-    pair_copy.start()
-    pair_copy.wait()
-    for m in range(2):
-        r.grad_embed[:, m, :] = r.embed_full[m, :vocab, :embed]
+    embed_stage(0, 2)
+    finish_inputs(0)
+    finish_swaps(0)
+    embed_stage(0, 3)
+    embed_stage(0, 4)
 
 
 def run_step(count, groups, factor, char_ids, prefix, embedding, w_in, w_rec, gate_bias, w_out, b_out):
@@ -1056,7 +1121,7 @@
         embed_part=((2, padded, depth), F32),
         embed_half=((2, reduced, depth), F32),
         embed_full=((2, padded, depth), F32),
-        embed_inbox=((links, 2, reduced // count, depth), F32),
+        embed_inbox=((2, links, reduced // count, depth), F32),
         wide_slot=((2, 2, 2, groups, rows, 2 * shard_units), B16),
         past_slot=((2, 2, 2, groups, rows, wide), B16),
     )
@@ -1088,12 +1153,12 @@
         swap_send=(2, 2, 2),
         swap_recv=(2, 2, 2),
         keep_sem=(2, 2),
-        embed_send=(2,),
-        embed_recv=(2,),
-        reduce_send=(links,),
-        reduce_recv=(links,),
-        gather_send=(links,),
-        gather_recv=(links,),
+        embed_send=(2, 2),
+        embed_recv=(2, 2),
+        reduce_send=(2, links),
+        reduce_recv=(2, links),
+        gather_send=(2, links),
+        gather_recv=(2, links),
     )
     scratch = {key: pltpu.VMEM(shape, kind) for key, (shape, kind) in arrays.items()}
     scratch |= {key: dma(shape) for key, shape in semaphores.items()}

time: 485 us -> 479 us (0.988)
  Pallas kernels: 473 us -> 467 us
    pallas_call x1, Pallas kernels: 473 us -> 467 us  [call(): pl.pallas_call(kernel, out_shape=tuple((jax.ShapeDtypeStruct(shape, kind)...]
where the time goes in v5:
time: 479 us
  Pallas kernels  467 us (97%)
  local copies, waits for them, and re-layouts  11.5 us (2%)
    pallas_call x1, Pallas kernels, call(): pl.pallas_call(kernel, out_shape=tuple((jax.ShapeDtypeStruct(shape, kind)...  467 us
    unnamed x12, local copies, waits for them, and re-layouts  11.5 us

profile of v5, /device:TPU:0, one launch (start us, length us, event | category | flops | bytes accessed | tf_op | source)
XLA Modules:
  0.0 479.0 jit_solution(10841075415339463825)
XLA Ops:
  0.6 466.9 %lstm_step.1 = (f32[275,2,100]{2,1,0:T(2,128)}, f32[2,100,4,512]{3,2,1,0:T(4,128)}, f32[2,4,256,512]{3,2,1,0:T(8,128)}, f32[2,4,512]{2,1,0:T(4,128)}, f32[275,2,...) custom-call(s32[4,48]{1,0:T(4,128)} %refs_0_.1, ...), custom_call_target="tpu_custom_call" | custom-call | flops 99999997952 | bytes 52428800 | tf_op jit(solution)/shard_map/lstm_step/pallas_call | solution.py:97
  467.5 1.7 copy.20
  469.2 2.9 copy.21
  472.1 0.0 copy-start.1
  472.1 0.0 copy-start
  472.1 0.0 copy-start.2
  472.1 4.7 copy.22
  476.8 0.0 copy-done.1
  476.8 0.6 copy.23
  477.4 0.0 copy-done
  477.4 1.0 copy.24
  478.4 0.0 copy-done.2
  478.4 0.6 copy.25
Async XLA Ops:
  472.1 4.7 copy-start.1
  472.1 5.3 %copy-start = (f32[275,2,512]{2,1,0:T(2,128)S(1)}, f32[275,2,512]{2,1,0:T(2,128)}, u32[]{:S(2)}) copy-start(f32[275,2,512]{2,1,0:T(2,128)} %get-tuple-element.16) | copy-start | bytes 3379204
  472.1 6.3 %copy-start.2 = (f32[2,275]{1,0:T(2,128)S(1)}, f32[2,275]{1,0:T(2,128)}, u32[]{:S(2)}) copy-start(f32[2,275]{1,0:T(2,128)} %get-tuple-element.29) | copy-start | bytes 6604

commit v6 on v5

--- a/solution.py
+++ b/solution.py
@@ -88,20 +88,27 @@
     return first, second, (rest - second.astype(F32)).astype(B16)
 
 
-def call(body, name, ins, outs, scratch, collective_id, cost):
+def call(body, name, ins, outs, scratch, collective_id, cost, resident=False):
     names = [*ins, *outs, *scratch]
+
+    def result(shape, kind, spec):
+        if resident and spec is VMEM:
+            return pltpu.VMEM(shape, kind)
+        return jax.ShapeDtypeStruct(shape, kind)
 
     def kernel(*refs):
         body(types.SimpleNamespace(**dict(zip(names, refs))))
 
     results = pl.pallas_call(
         kernel,
-        out_shape=tuple(jax.ShapeDtypeStruct(shape, kind) for shape, kind, _ in outs.values()),
+        out_shape=tuple(result(*out) for out in outs.values()),
         in_specs=[spec for _, spec in ins.values()],
         out_specs=tuple(spec for _, _, spec in outs.values()),
         scratch_shapes=list(scratch.values()),
         compiler_params=pltpu.CompilerParams(
-            collective_id=collective_id, has_side_effects=True, vmem_limit_bytes=62 * MIB
+            collective_id=collective_id,
+            has_side_effects=True,
+            vmem_limit_bytes=(59 if resident else 62) * MIB,
         ),
         cost_estimate=pl.CostEstimate(flops=cost, bytes_accessed=50 * MIB, transcendentals=0),
         name=name,
@@ -1163,7 +1170,7 @@
     scratch = {key: pltpu.VMEM(shape, kind) for key, (shape, kind) in arrays.items()}
     scratch |= {key: dma(shape) for key, shape in semaphores.items()}
     body = functools.partial(step_body, count, groups, factor)
-    return call(body, "lstm_step", ins, outs, scratch, 2, 10**11)
+    return call(body, "lstm_step", ins, outs, scratch, 2, 10**11, resident=True)
 
 
 def shifted(values):

time: 479 us -> 472 us (0.985)
  local copies, waits for them, and re-layouts: 11.5 us -> 6.07 us
    unnamed x12 -> x8, local copies, waits for them, and re-layouts: 11.5 us -> 6.07 us
where the time goes in v6:
time: 472 us; the launch traced here: 471 us
  Pallas kernels  465 us (99%)
  local copies, waits for them, and re-layouts  6.07 us (1%)
    pallas_call x1, Pallas kernels, call(): pl.pallas_call(kernel, out_shape=tuple((result(*out) for out in outs.valu...  465 us

profile of v6, /device:TPU:0, one launch (start us, length us, event | category | flops | bytes accessed | tf_op | source)
XLA Modules:
  0.0 471.2 jit_solution(10089933801659403481)
XLA Ops:
  0.6 464.5 %lstm_step.1 = (f32[275,2,100]{2,1,0:T(2,128)S(1)}, f32[2,100,4,512]{3,2,1,0:T(4,128)S(1)}, f32[2,4,256,512]{3,2,1,0:T(8,128)}, f32[2,4,512]{2,1,0:T(4,128)S(1)}...) custom-call(s32[4,48]{1,0:T(4,128)} %refs_0_.1, ...), custom_call_target="tpu_custom_call" | custom-call | flops 99999997952 | bytes 52428800 | tf_op jit(solution)/shard_map/lstm_step/pallas_call | solution.py:102
  465.1 0.0 copy-start
  465.2 0.7 copy.20
  465.9 1.2 copy.21
  467.0 0.6 copy.24
  467.6 0.6 copy.22
  468.2 1.0 copy.23
  469.2 0.0 copy-done
  469.2 2.0 copy.25
Async XLA Ops:
  465.1 4.1 copy-start

commit v7 on v6

--- a/solution.py
+++ b/solution.py
@@ -725,8 +725,9 @@
         for g in range(2):
             term = dot_last(dz[:, g * units : (g + 1) * units], r.inputs[m, 2 * core + g])
             grad_x = term if grad_x is None else grad_x + term
-        for part in split_three(grad_x):
-            r.embed_part[m] += dot_first(spots, part)
+        width = grad_x.shape[1]
+        three = dot_first(spots, jnp.concatenate(split_three(grad_x), axis=1))
+        r.embed_part[m] += three[:, :width] + three[:, width : 2 * width] + three[:, 2 * width :]
 
     def give(m, t, k, peer):
         slot = lax.rem(t, 2)

time: 472 us -> 471 us (level)
  no operation moved by 1% of the time
where the time goes in v7:
time: 471 us
  Pallas kernels  464 us (99%)
  local copies, waits for them, and re-layouts  6.07 us (1%)
    pallas_call x1, Pallas kernels, call(): pl.pallas_call(kernel, out_shape=tuple((result(*out) for out in outs.valu...  464 us

profile of v7, /device:TPU:0, one launch (start us, length us, event | category | flops | bytes accessed | tf_op | source)
XLA Modules:
  0.0 470.7 jit_solution(3509112259881994015)
XLA Ops:
  0.6 464.0 %lstm_step.1 = (f32[275,2,100]{2,1,0:T(2,128)S(1)}, f32[2,100,4,512]{3,2,1,0:T(4,128)S(1)}, f32[2,4,256,512]{3,2,1,0:T(8,128)}, f32[2,4,512]{2,1,0:T(4,128)S(1)}...) custom-call(s32[4,48]{1,0:T(4,128)} %refs_0_.1, ...), custom_call_target="tpu_custom_call" | custom-call | flops 99999997952 | bytes 52428800 | tf_op jit(solution)/shard_map/lstm_step/pallas_call | solution.py:102
  464.6 0.0 copy-start
  464.6 0.7 copy.20
  465.3 1.2 copy.21
  466.5 0.6 copy.24
  467.1 0.6 copy.22
  467.7 1.0 copy.23
  468.7 0.0 copy-done
  468.7 2.0 copy.25
Async XLA Ops:
  464.6 4.1 copy-start
